TPU v7x, 32 devices: a whole 2x2x4 slice. The times are simulated.
32 devices in a mesh: seq: 8 (over z, y), tok: 4 (over x, core).
Axes of the slice: x: 2, y: 2, z: 4, core: 2. Of those that a mesh axis runs over, the one named last changes fastest.
Arguments:
- tokens: bfloat16 [8, 1024, 1024], P('seq', 'tok'), may hold values from -6 to 6
- out_grad: bfloat16 [8, 1024, 1024], P('seq', 'tok'), may hold values from -6 to 6
- segments: int32 [8, 1024], P('seq'), may hold values from 0 to 2, never falling along the last dimension, each value on 1 to 512 neighbouring positions
- adapter_index: int32 [8], P('seq'), may hold values from 0 to 7
- qkv_weight: bfloat16 [1024, 3072], P('tok', 'seq'), may hold values from -0.1875 to 0.1875
- out_weight: bfloat16 [1024, 1024], P('tok', 'seq'), may hold values from -0.75 to 0.75
- in_weight: bfloat16 [1024, 5248], P('tok', 'seq'), may hold values from -0.1875 to 0.1875
- out2_weight: bfloat16 [2624, 1024], P('tok', 'seq'), may hold values from -0.15625 to 0.15625
- attn_gain: bfloat16 [1024], P('tok'), may hold values from 0.099609375 to 1.8984375
- mlp_gain: bfloat16 [1024], P('tok'), may hold values from 0.099609375 to 1.8984375
- qkv_down: bfloat16 [8, 16, 1024], replicated, may hold values from -0.1875 to 0.1875
- qkv_up: bfloat16 [8, 16, 3072], replicated, may hold values from -0.5 to 0.5
- out_down: bfloat16 [8, 16, 1024], replicated, may hold values from -0.1875 to 0.1875
- out_up: bfloat16 [8, 16, 1024], replicated, may hold values from -1.5 to 1.5
- in_down: bfloat16 [8, 16, 1024], replicated, may hold values from -0.1875 to 0.1875
- in_up: bfloat16 [8, 16, 5248], replicated, may hold values from -0.5 to 0.5
- out2_down: bfloat16 [8, 16, 2624], replicated, may hold values from -0.125 to 0.125
- out2_up: bfloat16 [8, 16, 1024], replicated, may hold values from -0.5 to 0.5
Outputs:
- layer_out: bfloat16 [8, 1024, 1024], P('seq', 'tok')
- input_grad: bfloat16 [8, 1024, 1024], P('seq', 'tok')
- qkv_down_grad: float32 [8, 16, 1024], replicated
- qkv_up_grad: float32 [8, 16, 3072], replicated
- out_down_grad: float32 [8, 16, 1024], replicated
- out_up_grad: float32 [8, 16, 1024], replicated
- in_down_grad: float32 [8, 16, 1024], replicated
- in_up_grad: float32 [8, 16, 5248], replicated
- out2_down_grad: float32 [8, 16, 2624], replicated
- out2_up_grad: float32 [8, 16, 1024], replicated
Inputs may be any that keep to these rules, and one draw needn't show every extreme that they name: `segments`: within a sequence the document numbers never fall; each document has 1 to 512 tokens, one of each sequence exactly 512.
All inputs are finite; a program needn't handle non-finite values.
Results may differ from a plain program's by a relative error of at most 0.018.
Values may be sent and summed in bfloat16 or wider, within the bound.
No kernel may reach another device: no remote copies, remote signals or barrier semaphores. Data moves between devices by JAX's collectives and lax.ppermute only.
A program may use at most 128 MiB of HBM per device.

v0:
```python
import jax
import jax.numpy as jnp
from jax import lax
from jax.sharding import PartitionSpec as P

HEADS = 16
HEAD_DIM = 64
FF = 2624
ADAPTERS = 8


EPS = 1e-05
THETA = 160000.0
HIGH = lax.Precision.HIGHEST


def layer_norm(values, gain_vec):
    middle = jnp.mean(values, axis=-1, keepdims=True)
    centered = values - middle
    spread = jnp.mean(centered * centered, axis=-1, keepdims=True)
    return centered * lax.rsqrt(spread + EPS) * gain_vec


def rotary_table(positions, head_width):
    exponent = jnp.arange(0, head_width, 2).astype(jnp.float32) / head_width
    inverse = 1.0 / THETA**exponent
    phases = positions.astype(jnp.float32)[:, None] * inverse[None, :]
    cosine = jnp.concatenate([jnp.cos(phases), jnp.cos(phases)], -1)
    sine_part = jnp.concatenate([jnp.sin(phases), jnp.sin(phases)], -1)
    return (cosine, sine_part)


def rotary(values, cosine, sine_part):
    half_width = values.shape[-1] // 2
    turned = jnp.concatenate([-values[..., half_width:], values[..., :half_width]], -1)
    return values * cosine[None, :, None, :] + turned * sine_part[None, :, None, :]


def glu_act(inputs, gate_vals):
    return jax.nn.gelu(inputs, approximate=False) * gate_vals


def select(table_rows, onehot_low):
    return jnp.einsum(
        "sa,ayz->syz", onehot_low, table_rows, preferred_element_type=jnp.float32
    ).astype(jnp.bfloat16)


def spread_back(term_rows, onehot):
    return jnp.einsum(
        "sa,syz->ayz", onehot, term_rows, precision=HIGH, preferred_element_type=jnp.float32
    )


def project(inputs, weight, down_rows, up_rows):
    seq_count, row_count, width_in = inputs.shape
    main_part = jnp.dot(
        inputs.reshape(seq_count * row_count, width_in), weight, preferred_element_type=jnp.float32
    )
    narrow = jnp.einsum(
        "std,srd->str", inputs, down_rows, preferred_element_type=jnp.float32
    ).astype(jnp.bfloat16)
    extra_part = jnp.einsum("str,sre->ste", narrow, up_rows, preferred_element_type=jnp.float32)
    return (main_part.reshape(seq_count, row_count, -1) + extra_part, narrow)


def project_back(grad_out, inputs, narrow, weight, down_rows, up_rows):
    seq_count, row_count, width_out = grad_out.shape
    main_part = lax.dot_general(
        grad_out.reshape(seq_count * row_count, width_out),
        weight,
        (((1,), (1,)), ((), ())),
        preferred_element_type=jnp.float32,
    )
    inner_grad = jnp.einsum(
        "ste,sre->str", grad_out, up_rows, preferred_element_type=jnp.float32
    ).astype(jnp.bfloat16)
    back_sum = main_part.reshape(seq_count, row_count, -1) + jnp.einsum(
        "str,srd->std", inner_grad, down_rows, preferred_element_type=jnp.float32
    )
    grad_up = jnp.einsum("str,ste->sre", narrow, grad_out, preferred_element_type=jnp.float32)
    grad_down = jnp.einsum("str,std->srd", inner_grad, inputs, preferred_element_type=jnp.float32)
    return (back_sum, grad_down, grad_up)


def masked_scores(query_part, key_part, doc_mask):
    scores = (
        jnp.einsum("sqhd,skhd->shqk", query_part, key_part, preferred_element_type=jnp.float32)
        * 0.125
    )
    return jnp.where(doc_mask[:, None, :, :], scores, -1e30)


def heads_slice(source, group_index, group_width, head_width):
    part_cols = lax.dynamic_slice_in_dim(source, group_index * group_width, group_width, 2)
    return part_cols.reshape(
        part_cols.shape[0], part_cols.shape[1], group_width // head_width, head_width
    )


def join_groups(parts):
    moved = jnp.moveaxis(parts, 0, 2)
    return moved.reshape(moved.shape[0], moved.shape[1], -1)


def body(
    tokens,
    out_grad,
    segments,
    adapter_index,
    qkv_weight,
    out_weight,
    in_weight,
    out2_weight,
    attn_gain,
    mlp_gain,
    qkv_down,
    qkv_up,
    out_down,
    out_up,
    in_down,
    in_up,
    out2_down,
    out2_up,
):
    seq_count, tok_rows, model_width = tokens.shape
    head_width = HEAD_DIM
    group_width = 2 * head_width
    groups = jnp.arange(HEADS // 2)
    seq_length = segments.shape[1]
    tok_start = lax.axis_index("tok") * tok_rows
    positions = tok_start + jnp.arange(tok_rows)
    cosine, sine_part = rotary_table(positions, head_width)
    own_segments = lax.dynamic_slice_in_dim(segments, tok_start, tok_rows, 1)
    doc_mask = own_segments[:, :, None] == segments[:, None, :]
    pick_bits = adapter_index[:, None] == jnp.arange(ADAPTERS)[None, :]
    onehot = pick_bits.astype(jnp.float32)
    onehot_low = pick_bits.astype(jnp.bfloat16)
    picked = [
        select(table_rows, onehot_low)
        for table_rows in (qkv_down, qkv_up, out_down, out_up, in_down, in_up, out2_down, out2_up)
    ]
    tok_parts = (
        lax.all_gather(qkv_weight, "tok", axis=0, tiled=True),
        lax.all_gather(out_weight, "tok", axis=0, tiled=True),
        lax.all_gather(in_weight, "tok", axis=0, tiled=True),
        lax.all_gather(out2_weight, "tok", axis=0, tiled=True),
        lax.all_gather(attn_gain, "tok", axis=0, tiled=True),
        lax.all_gather(mlp_gain, "tok", axis=0, tiled=True),
    )
    w_qkv, w_out, w_in, w_out2 = (
        lax.all_gather(tok_parts[0], "seq", axis=1, tiled=True),
        lax.all_gather(tok_parts[1], "seq", axis=1, tiled=True),
        lax.all_gather(tok_parts[2], "seq", axis=1, tiled=True),
        lax.all_gather(tok_parts[3], "seq", axis=1, tiled=True),
    )
    gain_one = tok_parts[4].astype(jnp.float32)
    gain_two = tok_parts[5].astype(jnp.float32)
    inputs = tokens.astype(jnp.float32)
    norm_one = layer_norm(inputs, gain_one).astype(jnp.bfloat16)
    qkv, narrow_qkv = project(norm_one, w_qkv, picked[0], picked[1])
    head_shape = (seq_count, tok_rows, HEADS, head_width)
    query_pre = qkv[..., :model_width].reshape(head_shape)
    query_low = (
        rotary(query_pre, cosine, sine_part)
        .reshape(seq_count, tok_rows, model_width)
        .astype(jnp.bfloat16)
    )
    key_low = (
        rotary(qkv[..., model_width : 2 * model_width].reshape(head_shape), cosine, sine_part)
        .reshape(seq_count, tok_rows, model_width)
        .astype(jnp.bfloat16)
    )
    value_low = qkv[..., 2 * model_width :].astype(jnp.bfloat16)
    keys_all, values_all = (
        lax.all_gather(key_low, "tok", axis=1, tiled=True),
        lax.all_gather(value_low, "tok", axis=1, tiled=True),
    )

    def forward_group(group_index):
        query_part = heads_slice(query_low, group_index, group_width, head_width)
        key_part = heads_slice(keys_all, group_index, group_width, head_width)
        value_part = heads_slice(values_all, group_index, group_width, head_width)
        scores = masked_scores(query_part, key_part, doc_mask)
        row_max = jnp.max(scores, axis=-1, keepdims=True)
        row_total = jnp.sum(jnp.exp(scores - row_max), axis=-1, keepdims=True)
        log_total = row_max + jnp.log(row_total)
        attn_prob = jnp.exp(scores - log_total).astype(jnp.bfloat16)
        mixed = jnp.einsum(
            "shqk,skhd->sqhd", attn_prob, value_part, preferred_element_type=jnp.float32
        )
        return (mixed.reshape(seq_count, tok_rows, group_width), log_total[..., 0])

    mixed_parts, log_totals = lax.map(forward_group, groups)
    attn_low = join_groups(mixed_parts).astype(jnp.bfloat16)
    attn_branch, narrow_out = project(attn_low, w_out, picked[2], picked[3])
    middle = inputs + attn_branch
    norm_two = layer_norm(middle, gain_two).astype(jnp.bfloat16)
    gate_up, narrow_in = project(norm_two, w_in, picked[4], picked[5])
    act_low = glu_act(gate_up[..., :FF], gate_up[..., FF:]).astype(jnp.bfloat16)
    mlp_branch, narrow_out2 = project(act_low, w_out2, picked[6], picked[7])
    layer_out = (middle + mlp_branch).astype(jnp.bfloat16)
    back_parts = (
        lax.all_gather(qkv_weight, "tok", axis=0, tiled=True),
        lax.all_gather(out_weight, "tok", axis=0, tiled=True),
        lax.all_gather(in_weight, "tok", axis=0, tiled=True),
        lax.all_gather(out2_weight, "tok", axis=0, tiled=True),
    )
    w_qkv, w_out, w_in, w_out2 = (
        lax.all_gather(back_parts[0], "seq", axis=1, tiled=True),
        lax.all_gather(back_parts[1], "seq", axis=1, tiled=True),
        lax.all_gather(back_parts[2], "seq", axis=1, tiled=True),
        lax.all_gather(back_parts[3], "seq", axis=1, tiled=True),
    )
    grad_y = out_grad.astype(jnp.float32)
    back_act, down_o2, up_o2 = project_back(
        out_grad, act_low, narrow_out2, w_out2, picked[6], picked[7]
    )
    _, glu_back = jax.vjp(glu_act, gate_up[..., :FF], gate_up[..., FF:])
    grad_in, grad_gate = glu_back(back_act)
    grad_z = jnp.concatenate([grad_in, grad_gate], axis=-1).astype(jnp.bfloat16)
    back_norm_two, down_in, up_in = project_back(
        grad_z, norm_two, narrow_in, w_in, picked[4], picked[5]
    )
    _, norm_two_back = jax.vjp(lambda field: layer_norm(field, gain_two), middle)
    grad_mid = grad_y + norm_two_back(back_norm_two)[0]
    grad_a = grad_mid.astype(jnp.bfloat16)
    back_attn, down_out, up_out = project_back(
        grad_a, attn_low, narrow_out, w_out, picked[2], picked[3]
    )
    grad_attn = back_attn.astype(jnp.bfloat16)

    def query_grads(group_index):
        query_part = heads_slice(query_low, group_index, group_width, head_width)
        key_part = heads_slice(keys_all, group_index, group_width, head_width)
        value_part = heads_slice(values_all, group_index, group_width, head_width)
        grad_part = heads_slice(grad_attn, group_index, group_width, head_width)
        scores = masked_scores(query_part, key_part, doc_mask)
        attn_prob = jnp.exp(scores - log_totals[group_index][..., None])
        grad_prob = jnp.einsum(
            "sqhd,skhd->shqk", grad_part, value_part, preferred_element_type=jnp.float32
        )
        row_dot = jnp.sum(attn_prob * grad_prob, axis=-1)
        grad_scores = (attn_prob * (grad_prob - row_dot[..., None]) * 0.125).astype(jnp.bfloat16)
        grad_query = jnp.einsum(
            "shqk,skhd->sqhd", grad_scores, key_part, preferred_element_type=jnp.float32
        )
        return (
            query_part,
            grad_part,
            attn_prob,
            grad_scores,
            grad_query.reshape(seq_count, tok_rows, group_width),
            row_dot,
        )

    def summed_group(group_index):
        query_part, grad_part, attn_prob, grad_scores, grad_query, row_dot = query_grads(
            group_index
        )
        grad_key = jnp.einsum(
            "shqk,sqhd->skhd", grad_scores, query_part, preferred_element_type=jnp.float32
        )
        grad_value = jnp.einsum(
            "shqk,sqhd->skhd",
            attn_prob.astype(jnp.bfloat16),
            grad_part,
            preferred_element_type=jnp.float32,
        )
        grad_key, grad_value = (
            lax.psum_scatter(
                grad_key.reshape(seq_count, seq_length, group_width).astype(jnp.bfloat16),
                "tok",
                scatter_dimension=1,
                tiled=True,
            ).astype(jnp.float32),
            lax.psum_scatter(
                grad_value.reshape(seq_count, seq_length, group_width).astype(jnp.bfloat16),
                "tok",
                scatter_dimension=1,
                tiled=True,
            ).astype(jnp.float32),
        )
        return (grad_query, grad_key, grad_value)

    query_parts, key_parts, value_parts = lax.map(summed_group, groups)
    grad_query = join_groups(query_parts)
    grad_key = join_groups(key_parts)
    grad_value = join_groups(value_parts)
    _, rotate_back = jax.vjp(lambda field: rotary(field, cosine, sine_part), query_pre)
    grad_query_pre = rotate_back(grad_query.reshape(head_shape))[0].reshape(
        seq_count, tok_rows, model_width
    )
    grad_key_pre = rotate_back(grad_key.reshape(head_shape))[0].reshape(
        seq_count, tok_rows, model_width
    )
    grad_qkv = jnp.concatenate([grad_query_pre, grad_key_pre, grad_value], axis=-1).astype(
        jnp.bfloat16
    )
    back_norm_one, down_qkv, up_qkv = project_back(
        grad_qkv, norm_one, narrow_qkv, w_qkv, picked[0], picked[1]
    )
    _, norm_one_back = jax.vjp(lambda field: layer_norm(field, gain_one), inputs)
    input_grad = (grad_mid + norm_one_back(back_norm_one)[0]).astype(jnp.bfloat16)
    terms = (down_qkv, up_qkv, down_out, up_out, down_in, up_in, down_o2, up_o2)
    summed = lax.psum(
        (
            spread_back(terms[0], onehot),
            spread_back(terms[1], onehot),
            spread_back(terms[2], onehot),
            spread_back(terms[3], onehot),
            spread_back(terms[4], onehot),
            spread_back(terms[5], onehot),
            spread_back(terms[6], onehot),
            spread_back(terms[7], onehot),
        ),
        ("seq", "tok"),
    )
    return (
        layer_out,
        input_grad,
        summed[0],
        summed[1],
        summed[2],
        summed[3],
        summed[4],
        summed[5],
        summed[6],
        summed[7],
    )


def solution(mesh):
    return jax.shard_map(
        body,
        mesh=mesh,
        in_specs=(
            P("seq", "tok", None),
            P("seq", "tok", None),
            P("seq", None),
            P("seq"),
            P("tok", "seq"),
            P("tok", "seq"),
            P("tok", "seq"),
            P("tok", "seq"),
            P("tok"),
            P("tok"),
            P(),
            P(),
            P(),
            P(),
            P(),
            P(),
            P(),
            P(),
        ),
        out_specs=(
            P("seq", "tok", None),
            P("seq", "tok", None),
            P(),
            P(),
            P(),
            P(),
            P(),
            P(),
            P(),
            P(),
        ),
        check_vma=False,
    )
```

profile of v0, /device:TPU:0, one launch (start us, length us, event | category | flops | bytes accessed | tf_op | source)
XLA Modules:
  0.0 1193.6 jit_solution(8519961414103918297)
XLA Ops:
  7.3 11.8 all_gather.45
  19.9 8.8 all_gather.54
  28.7 5.2 all-gather
  44.1 75.4 %all-gather.10.cloned.1.call-done = bf16[1024,3072]{1,0:T(8,128)(2,1)} async-done(((bf16[1024,384]{1,0:T(8,128)(2,1)}), bf16[1024,3072]{1,0:T(8,128)(2,1)}) %all-gather.10.cloned.1.call-update) | async-done | bytes 6291472 | tf_op jit(solution)/shard_map/all_gather | solution.py:152
  149.3 6.4 all_gather.49
  156.6 5.2 all-gather.1
  169.3 59.4 %all-gather.22.cloned.1.call-done = bf16[2624,1024]{1,0:T(8,128)(2,1)} async-done(((bf16[2624,128]{1,0:T(8,128)(2,1)}), bf16[2624,1024]{1,0:T(8,128)(2,1)}) %all-gather.22.cloned.1.call-update) | async-done | bytes 5373968 | tf_op jit(solution)/shard_map/all_gather | solution.py:155
  236.1 15.5 %all-gather.14.cloned.1.call-done = bf16[1,1024,1024]{2,1,0:T(8,128)(2,1)} async-done(((bf16[1,256,1024]{2,1,0:T(8,128)(2,1)}), bf16[1,1024,1024]{2,1,0:T(8,128)(2,1)}) %all-gather.14.cloned.1.call-update) | async-done | bytes 2097168 | tf_op jit(solution)/shard_map/all_gather | solution.py:176
  255.5 20.6 %all-gather.12.cloned.1.call-done = bf16[1,1024,1024]{2,1,0:T(8,128)(2,1)} async-done(((bf16[1,256,1024]{2,1,0:T(8,128)(2,1)}), bf16[1,1024,1024]{2,1,0:T(8,128)(2,1)}) %all-gather.12.cloned.1.call-update) | async-done | bytes 2097168 | tf_op jit(solution)/shard_map/all_gather | solution.py:177
  280.1 45.8 %while.30 = (s32[]{:T(128)}, bf16[8,1,256,128]{2,3,1,0:T(8,128)(2,1)S(1)}, f32[8,1,2,256]{3,2,1,0:T(2,128)}, s32[8]{0:T(128)S(1)}, bf16[1,1024,1024]{1,2,0:T(8,1...) while((s32[]{:T(128)}, ...), condition=%wide.region_5.6_spmd.clone.clone, body=%wide.region_2.5_spmd.clone.sunk.clone | while | flops 138149376 | bytes 8804011 | solution.py:194
  332.7 151.0 %all-gather.20.cloned.1.call-done = bf16[1024,5248]{0,1:T(8,128)(2,1)} async-done(((bf16[1024,656]{0,1:T(8,128)(2,1)}), bf16[1024,5248]{0,1:T(8,128)(2,1)}) %all-gather.20.cloned.1.call-update) | async-done | bytes 10747920 | tf_op jit(solution)/shard_map/all_gather | solution.py:154
  483.7 6.0 fusion.119
  491.5 6.7 fusion.48
  511.9 468.5 %while.31 = (s32[]{:T(128)}, f32[8,1,256,128]{2,3,1,0:T(8,128)}, f32[8,1,256,128]{2,3,1,0:T(8,128)}, bf16[8,1,256,128]{2,3,1,0:T(8,128)(2,1)}, s32[8]{0:T(128)S(...) while((s32[]{:T(128)}, f32[8,1,256,128]{2,3,1,0:T(8,128)}, ...), condition=%wide.region_14.15_spmd.clone.clone, body=%wide.region_10.14_spmd.clone.sunk.clone | while | flops 343477248 | bytes 23342488 | solution.py:286
  534.3 10.5 reduce-scatter.3.cloned.1.call-done
  546.3 21.2 %reduce-scatter.5.cloned.1.call-done = bf16[1,256,128]{1,2,0:T(8,128)(2,1)} async-done(((bf16[1,1024,128]{1,2,0:T(8,128)(2,1)}), bf16[1,256,128]{1,2,0:T(8,128)(2,1)}) %reduce-scatter.5.cloned.1.call-update) | async-done | bytes 65552 | tf_op jit(solution)/shard_map/while/body/eval_jaxpr/reduce_scatter | solution.py:277
  591.2 12.4 %reduce-scatter.3.cloned.1.call-done = bf16[1,256,128]{1,2,0:T(8,128)(2,1)} async-done(((bf16[1,1024,128]{1,2,0:T(8,128)(2,1)}), bf16[1,256,128]{1,2,0:T(8,128)(2,1)}) %reduce-scatter.3.cloned.1.call-update) | async-done | bytes 65552 | tf_op jit(solution)/shard_map/while/body/eval_jaxpr/reduce_scatter | solution.py:271
  605.1 21.2 %reduce-scatter.5.cloned.1.call-done = bf16[1,256,128]{1,2,0:T(8,128)(2,1)} async-done(((bf16[1,1024,128]{1,2,0:T(8,128)(2,1)}), bf16[1,256,128]{1,2,0:T(8,128)(2,1)}) %reduce-scatter.5.cloned.1.call-update) | async-done | bytes 65552 | tf_op jit(solution)/shard_map/while/body/eval_jaxpr/reduce_scatter | solution.py:277
  650.1 12.4 %reduce-scatter.3.cloned.1.call-done = bf16[1,256,128]{1,2,0:T(8,128)(2,1)} async-done(((bf16[1,1024,128]{1,2,0:T(8,128)(2,1)}), bf16[1,256,128]{1,2,0:T(8,128)(2,1)}) %reduce-scatter.3.cloned.1.call-update) | async-done | bytes 65552 | tf_op jit(solution)/shard_map/while/body/eval_jaxpr/reduce_scatter | solution.py:271
  664.0 21.2 %reduce-scatter.5.cloned.1.call-done = bf16[1,256,128]{1,2,0:T(8,128)(2,1)} async-done(((bf16[1,1024,128]{1,2,0:T(8,128)(2,1)}), bf16[1,256,128]{1,2,0:T(8,128)(2,1)}) %reduce-scatter.5.cloned.1.call-update) | async-done | bytes 65552 | tf_op jit(solution)/shard_map/while/body/eval_jaxpr/reduce_scatter | solution.py:277
  708.9 12.4 %reduce-scatter.3.cloned.1.call-done = bf16[1,256,128]{1,2,0:T(8,128)(2,1)} async-done(((bf16[1,1024,128]{1,2,0:T(8,128)(2,1)}), bf16[1,256,128]{1,2,0:T(8,128)(2,1)}) %reduce-scatter.3.cloned.1.call-update) | async-done | bytes 65552 | tf_op jit(solution)/shard_map/while/body/eval_jaxpr/reduce_scatter | solution.py:271
  722.8 21.0 %reduce-scatter.5.cloned.1.call-done = bf16[1,256,128]{1,2,0:T(8,128)(2,1)} async-done(((bf16[1,1024,128]{1,2,0:T(8,128)(2,1)}), bf16[1,256,128]{1,2,0:T(8,128)(2,1)}) %reduce-scatter.5.cloned.1.call-update) | async-done | bytes 65552 | tf_op jit(solution)/shard_map/while/body/eval_jaxpr/reduce_scatter | solution.py:277
  767.6 12.4 %reduce-scatter.3.cloned.1.call-done = bf16[1,256,128]{1,2,0:T(8,128)(2,1)} async-done(((bf16[1,1024,128]{1,2,0:T(8,128)(2,1)}), bf16[1,256,128]{1,2,0:T(8,128)(2,1)}) %reduce-scatter.3.cloned.1.call-update) | async-done | bytes 65552 | tf_op jit(solution)/shard_map/while/body/eval_jaxpr/reduce_scatter | solution.py:271
  781.5 21.0 %reduce-scatter.5.cloned.1.call-done = bf16[1,256,128]{1,2,0:T(8,128)(2,1)} async-done(((bf16[1,1024,128]{1,2,0:T(8,128)(2,1)}), bf16[1,256,128]{1,2,0:T(8,128)(2,1)}) %reduce-scatter.5.cloned.1.call-update) | async-done | bytes 65552 | tf_op jit(solution)/shard_map/while/body/eval_jaxpr/reduce_scatter | solution.py:277
  826.3 12.4 %reduce-scatter.3.cloned.1.call-done = bf16[1,256,128]{1,2,0:T(8,128)(2,1)} async-done(((bf16[1,1024,128]{1,2,0:T(8,128)(2,1)}), bf16[1,256,128]{1,2,0:T(8,128)(2,1)}) %reduce-scatter.3.cloned.1.call-update) | async-done | bytes 65552 | tf_op jit(solution)/shard_map/while/body/eval_jaxpr/reduce_scatter | solution.py:271
  840.2 21.2 %reduce-scatter.5.cloned.1.call-done = bf16[1,256,128]{1,2,0:T(8,128)(2,1)} async-done(((bf16[1,1024,128]{1,2,0:T(8,128)(2,1)}), bf16[1,256,128]{1,2,0:T(8,128)(2,1)}) %reduce-scatter.5.cloned.1.call-update) | async-done | bytes 65552 | tf_op jit(solution)/shard_map/while/body/eval_jaxpr/reduce_scatter | solution.py:277
  885.0 12.4 %reduce-scatter.3.cloned.1.call-done = bf16[1,256,128]{1,2,0:T(8,128)(2,1)} async-done(((bf16[1,1024,128]{1,2,0:T(8,128)(2,1)}), bf16[1,256,128]{1,2,0:T(8,128)(2,1)}) %reduce-scatter.3.cloned.1.call-update) | async-done | bytes 65552 | tf_op jit(solution)/shard_map/while/body/eval_jaxpr/reduce_scatter | solution.py:271
  899.0 21.2 %reduce-scatter.5.cloned.1.call-done = bf16[1,256,128]{1,2,0:T(8,128)(2,1)} async-done(((bf16[1,1024,128]{1,2,0:T(8,128)(2,1)}), bf16[1,256,128]{1,2,0:T(8,128)(2,1)}) %reduce-scatter.5.cloned.1.call-update) | async-done | bytes 65552 | tf_op jit(solution)/shard_map/while/body/eval_jaxpr/reduce_scatter | solution.py:277
  943.9 12.4 %reduce-scatter.3.cloned.1.call-done = bf16[1,256,128]{1,2,0:T(8,128)(2,1)} async-done(((bf16[1,1024,128]{1,2,0:T(8,128)(2,1)}), bf16[1,256,128]{1,2,0:T(8,128)(2,1)}) %reduce-scatter.3.cloned.1.call-update) | async-done | bytes 65552 | tf_op jit(solution)/shard_map/while/body/eval_jaxpr/reduce_scatter | solution.py:271
  957.8 21.2 %reduce-scatter.5.cloned.1.call-done = bf16[1,256,128]{1,2,0:T(8,128)(2,1)} async-done(((bf16[1,1024,128]{1,2,0:T(8,128)(2,1)}), bf16[1,256,128]{1,2,0:T(8,128)(2,1)}) %reduce-scatter.5.cloned.1.call-update) | async-done | bytes 65552 | tf_op jit(solution)/shard_map/while/body/eval_jaxpr/reduce_scatter | solution.py:277
  994.2 5.0 fusion.107
  1007.7 166.8 %all-reduce.7.cloned.1.call-done = (f32[8,16,1024]{2,1,0:T(8,128)}, f32[8,16,3072]{2,1,0:T(8,128)}, f32[8,16,1024]{2,1,0:T(8,128)}, f32[8,16,1024]{2,1,0:T(8,128...) async-done(((f32[8,16,1024]{2,1,0:T(8,128)}, f32[8,16,3072]{2,1,0:T(8,128)}, f32[8,16,1024]{2,1,0:T(8,128)}, ...) | async-done | bytes 8224784 | tf_op jit(solution)/shard_map/psum | solution.py:306
  (509 shorter events, 340.1 us)
Async XLA Ops:
  7.2 161.6 %copy-start = (bf16[8,16,5248]{2,1,0:T(8,128)(2,1)S(1)}, bf16[8,16,5248]{2,1,0:T(8,128)(2,1)}, u32[]{:S(2)}) copy-start(bf16[8,16,5248]{2,1,0:T(8,128)(2,1)} %param.37) | copy-start | bytes 4030468
  7.2 21.5 %copy-start.54 = (bf16[256]{0:T(256)(128)(2,1)S(1)}, bf16[256]{0:T(256)(128)(2,1)}, u32[]{:S(2)}) copy-start(bf16[256]{0:T(256)(128)(2,1)} %param.30) | copy-start | bytes 1540
  7.2 112.3 %all-gather.10.cloned.1.call-start = ((), (), s32[]{:S(2)}) async-start(), calls=%async_computation.2 | async-start | bytes 7077888 | tf_op jit(solution)/shard_map/all_gather | solution.py:152
  19.1 136.7 %all-gather.18.cloned.1.call-start = ((), (), s32[]{:S(2)}) async-start(), calls=%async_computation.6 | async-start | bytes 1679360 | tf_op jit(solution)/shard_map/all_gather | solution.py:146
  19.8 208.9 %all-gather.22.cloned.1.call-start = ((), (), s32[]{:S(2)}) async-start(), calls=%async_computation.8 | async-start | bytes 6045696 | tf_op jit(solution)/shard_map/all_gather | solution.py:155
  28.6 222.9 %all-gather.14.cloned.1.call-start = ((), (), s32[]{:S(2)}) async-start(), calls=%async_computation.4 | async-start | bytes 2621440 | tf_op jit(solution)/shard_map/all_gather | solution.py:176
  42.5 81.6 %copy-start.18 = (bf16[256,1024]{1,0:T(8,128)(2,1)}, bf16[256,1024]{1,0:T(8,128)(2,1)S(1)}, u32[]{:S(2)}) copy-start(bf16[256,1024]{1,0:T(8,128)(2,1)S(1)} %fusion.67) | copy-start | bytes 1572868
  146.9 14.9 %copy-start.50 = (bf16[8,16,1024]{2,1,0:T(8,128)(2,1)S(1)}, bf16[8,16,1024]{2,1,0:T(8,128)(2,1)}, u32[]{:S(2)}) copy-start(bf16[8,16,1024]{2,1,0:T(8,128)(2,1)} %param.34) | copy-start | bytes 786436
  146.9 129.2 %all-gather.12.cloned.1.call-start = ((), (), s32[]{:S(2)}) async-start(), calls=%async_computation.3 | async-start | bytes 2621440 | tf_op jit(solution)/shard_map/all_gather | solution.py:177
  149.3 17.8 %copy-start.13 = (bf16[1,256,1024]{2,1,0:T(8,128)(2,1)S(1)}, bf16[1,256,1024]{2,1,0:T(8,128)(2,1)}, u32[]{:S(2)}) copy-start(bf16[1,256,1024]{2,1,0:T(8,128)(2,1)} %param.23) | copy-start | bytes 1572868
  149.3 179.9 %all-gather.16.cloned.1.call-start = ((), (), s32[]{:S(2)}) async-start(), calls=%async_computation.5 | async-start | bytes 2359296 | tf_op jit(solution)/shard_map/all_gather | solution.py:153
  155.7 327.9 %all-gather.20.cloned.1.call-start = ((), (), s32[]{:S(2)}) async-start(), calls=%async_computation.7 | async-start | bytes 12091392 | tf_op jit(solution)/shard_map/all_gather | solution.py:154
  168.8 64.2 %copy-start.27 = (bf16[1,16,2624]{2,0,1:T(2,128)(2,1)}, bf16[1,16,2624]{2,0,1:T(2,128)(2,1)S(1)}, u32[]{:S(2)}) copy-start(bf16[1,16,2624]{2,0,1:T(2,128)(2,1)S(1)} %fusion.62) | copy-start | bytes 251908
  255.5 24.6 %copy-start.12 = (bf16[8,1,256,128]{2,3,1,0:T(8,128)(2,1)S(1)}, bf16[8,1,256,128]{2,3,1,0:T(8,128)(2,1)}, u32[]{:S(2)}) copy-start(bf16[8,1,256,128]{2,3,1,0:T(8,128)(2,1)} %copy-done.10) | copy-start | bytes 1572868
  280.1 45.8 %copy-start.48 = (bf16[1,16,1024]{2,0,1:T(2,128)(2,1)S(1)}, bf16[1,16,1024]{2,0,1:T(2,128)(2,1)}, u32[]{:S(2)}) copy-start(bf16[1,16,1024]{2,0,1:T(2,128)(2,1)} %fusion.79) | copy-start | bytes 98308
  511.9 32.8 %reduce-scatter.3.cloned.1.call-start = ((), (), s32[]{:S(2)}) async-start(), calls=%async_computation.10 | async-start | bytes 327680 | tf_op jit(solution)/shard_map/while/body/eval_jaxpr/reduce_scatter | solution.py:271
  526.4 41.1 %reduce-scatter.5.cloned.1.call-start = ((), (), s32[]{:S(2)}) async-start(), calls=%async_computation.11 | async-start | bytes 327680 | tf_op jit(solution)/shard_map/while/body/eval_jaxpr/reduce_scatter | solution.py:277
  569.0 34.7 %reduce-scatter.3.cloned.1.call-start = ((), (), s32[]{:S(2)}) async-start(), calls=%async_computation.10 | async-start | bytes 327680 | tf_op jit(solution)/shard_map/while/body/eval_jaxpr/reduce_scatter | solution.py:271
  583.5 42.9 %reduce-scatter.5.cloned.1.call-start = ((), (), s32[]{:S(2)}) async-start(), calls=%async_computation.11 | async-start | bytes 327680 | tf_op jit(solution)/shard_map/while/body/eval_jaxpr/reduce_scatter | solution.py:277
  627.8 34.7 %reduce-scatter.3.cloned.1.call-start = ((), (), s32[]{:S(2)}) async-start(), calls=%async_computation.10 | async-start | bytes 327680 | tf_op jit(solution)/shard_map/while/body/eval_jaxpr/reduce_scatter | solution.py:271
  642.3 42.9 %reduce-scatter.5.cloned.1.call-start = ((), (), s32[]{:S(2)}) async-start(), calls=%async_computation.11 | async-start | bytes 327680 | tf_op jit(solution)/shard_map/while/body/eval_jaxpr/reduce_scatter | solution.py:277
  686.6 34.7 %reduce-scatter.3.cloned.1.call-start = ((), (), s32[]{:S(2)}) async-start(), calls=%async_computation.10 | async-start | bytes 327680 | tf_op jit(solution)/shard_map/while/body/eval_jaxpr/reduce_scatter | solution.py:271
  701.1 42.7 %reduce-scatter.5.cloned.1.call-start = ((), (), s32[]{:S(2)}) async-start(), calls=%async_computation.11 | async-start | bytes 327680 | tf_op jit(solution)/shard_map/while/body/eval_jaxpr/reduce_scatter | solution.py:277
  745.3 34.7 %reduce-scatter.3.cloned.1.call-start = ((), (), s32[]{:S(2)}) async-start(), calls=%async_computation.10 | async-start | bytes 327680 | tf_op jit(solution)/shard_map/while/body/eval_jaxpr/reduce_scatter | solution.py:271
  759.8 42.7 %reduce-scatter.5.cloned.1.call-start = ((), (), s32[]{:S(2)}) async-start(), calls=%async_computation.11 | async-start | bytes 327680 | tf_op jit(solution)/shard_map/while/body/eval_jaxpr/reduce_scatter | solution.py:277
  804.0 34.7 %reduce-scatter.3.cloned.1.call-start = ((), (), s32[]{:S(2)}) async-start(), calls=%async_computation.10 | async-start | bytes 327680 | tf_op jit(solution)/shard_map/while/body/eval_jaxpr/reduce_scatter | solution.py:271
  818.5 42.9 %reduce-scatter.5.cloned.1.call-start = ((), (), s32[]{:S(2)}) async-start(), calls=%async_computation.11 | async-start | bytes 327680 | tf_op jit(solution)/shard_map/while/body/eval_jaxpr/reduce_scatter | solution.py:277
  862.8 34.6 %reduce-scatter.3.cloned.1.call-start = ((), (), s32[]{:S(2)}) async-start(), calls=%async_computation.10 | async-start | bytes 327680 | tf_op jit(solution)/shard_map/while/body/eval_jaxpr/reduce_scatter | solution.py:271
  877.3 42.9 %reduce-scatter.5.cloned.1.call-start = ((), (), s32[]{:S(2)}) async-start(), calls=%async_computation.11 | async-start | bytes 327680 | tf_op jit(solution)/shard_map/while/body/eval_jaxpr/reduce_scatter | solution.py:277
  921.6 34.7 %reduce-scatter.3.cloned.1.call-start = ((), (), s32[]{:S(2)}) async-start(), calls=%async_computation.10 | async-start | bytes 327680 | tf_op jit(solution)/shard_map/while/body/eval_jaxpr/reduce_scatter | solution.py:271
  936.1 42.9 %reduce-scatter.5.cloned.1.call-start = ((), (), s32[]{:S(2)}) async-start(), calls=%async_computation.11 | async-start | bytes 327680 | tf_op jit(solution)/shard_map/while/body/eval_jaxpr/reduce_scatter | solution.py:277
  980.5 194.1 %all-reduce.7.cloned.1.call-start = ((), (), s32[]{:S(2)}) async-start(), calls=%async_computation.9 | async-start | bytes 16515072 | tf_op jit(solution)/shard_map/psum | solution.py:306
  (72 other events, 243.3 us)
Sparse Core Ops, SparseCore 0:
  19.2 100.2 all-gather.9
  121.1 16.6 all-gather.17
  139.8 88.8 all-gather.21
  230.7 20.7 all-gather.13
  253.5 22.5 all-gather.11
  278.0 51.1 all-gather.15
  331.4 152.2 all-gather.19
  526.6 18.1 reduce-scatter.2
  547.4 20.0 reduce-scatter.4
  583.6 19.9 reduce-scatter.2
  606.2 20.0 reduce-scatter.4
  642.4 19.9 reduce-scatter.2
  665.0 20.0 reduce-scatter.4
  701.2 20.0 reduce-scatter.2
  723.8 20.0 reduce-scatter.4
  759.9 20.0 reduce-scatter.2
  782.4 20.0 reduce-scatter.4
  818.6 20.0 reduce-scatter.2
  841.3 20.0 reduce-scatter.4
  877.4 20.0 reduce-scatter.2
  900.1 20.0 reduce-scatter.4
  936.2 20.0 reduce-scatter.2
  958.9 20.0 reduce-scatter.4
  994.3 180.2 all-reduce.6
where the time goes:
time: 1200 us; the launch traced here: 1190 us
  waiting for transfers between devices  760 us (63%)
  matrix products  161 us (13%)
  local copies, waits for them, and re-layouts  125 us (10%)
  other arithmetic  65.7 us (5%)
  blocking collectives  37.4 us (3%)
  loops' own time  27.1 us (2%)
  between operations  16 us (1%)
    reduce_scatter x8, waiting for transfers between devices, summed_group(): lax.psum_scatter(grad_value.reshape(seq_count, seq_length, group_width).a...  169 us
    psum x1, waiting for transfers between devices, body(): lax.psum((spread_back(terms[0], onehot), spread_back(terms[1], onehot), s...  167 us
    all_gather x1, waiting for transfers between devices, body(): lax.all_gather(tok_parts[2], 'seq', axis=1, tiled=True)  151 us
    reduce_scatter x8, waiting for transfers between devices, summed_group(): lax.psum_scatter(grad_key.reshape(seq_count, seq_length, group_width).ast...  97.4 us
    all_gather x1, waiting for transfers between devices, body(): lax.all_gather(tok_parts[0], 'seq', axis=1, tiled=True)  75.4 us
    all_gather x1, waiting for transfers between devices, body(): lax.all_gather(tok_parts[3], 'seq', axis=1, tiled=True)  59.4 us
    dynamic_slice x48, local copies, waits for them, and re-layouts, heads_slice(): lax.dynamic_slice_in_dim(source, group_index * group_width, group_width, 2)  48.9 us
    dot_general x8, matrix products, summed_group(): jnp.einsum('shqk,sqhd->skhd', grad_scores, query_part, preferred_element_...  28.5 us
  transfers between devices with their start and end apart: 24, of which 23 were waited for; matrix products, arithmetic and copies ran while one was open for 16% of the time, Pallas kernels for 0%

commit v1 on v0

v1 whole, which is shorter than its diff:
```python
import functools

import jax
import jax.numpy as jnp
from jax import lax
from jax.experimental import pallas as pl
from jax.experimental.pallas import tpu as pltpu
from jax.sharding import PartitionSpec as P

HEADS = 16
HEAD_DIM = 64
EPS = 1e-05
THETA = 160000.0
F32 = jnp.float32
BF16 = jnp.bfloat16
MIB = 1024 * 1024


def nn(a, b):
    return lax.dot_general(a, b, (((1,), (0,)), ((), ())), preferred_element_type=F32)


def nt(a, b):
    return lax.dot_general(a, b, (((1,), (1,)), ((), ())), preferred_element_type=F32)


def tn(a, b):
    return lax.dot_general(a, b, (((0,), (0,)), ((), ())), preferred_element_type=F32)


def call(kernel, out_shape, args, scratch=(), smem=(), micros=1, name=None):
    out_shape = list(out_shape)
    size = lambda a: a.size * a.dtype.itemsize
    moved = sum(size(a) for a in args) + sum(size(o) for o in out_shape)
    flops = max(micros, 1) * 10**9
    specs = [
        pl.BlockSpec(memory_space=pltpu.SMEM if n in smem else pltpu.VMEM)
        for n in range(len(args))
    ]
    return pl.pallas_call(
        kernel,
        out_shape=out_shape,
        in_specs=specs,
        out_specs=[pl.BlockSpec(memory_space=pltpu.VMEM) for _ in out_shape],
        scratch_shapes=list(scratch),
        compiler_params=pltpu.CompilerParams(vmem_limit_bytes=60 * MIB),
        cost_estimate=pl.CostEstimate(
            flops=int(flops), bytes_accessed=int(moved), transcendentals=0
        ),
        name=name,
    )(*args)


def shape(dims, dtype):
    return jax.ShapeDtypeStruct(tuple(dims), dtype)


def to_slot(refs, index, value):
    for n, ref in enumerate(refs):

        @pl.when(index == n)
        def _(ref=ref):
            ref[...] = value


def normalized(rows):
    mean = jnp.mean(rows, axis=-1, keepdims=True)
    centered = rows - mean
    scale = lax.rsqrt(jnp.mean(centered * centered, axis=-1, keepdims=True) + EPS)
    return centered * scale, scale


def norm_back(rows, gain, grad):
    unit, scale = normalized(rows)
    weighted = grad * gain
    first = jnp.mean(weighted, axis=-1, keepdims=True)
    second = jnp.mean(weighted * unit, axis=-1, keepdims=True)
    return (weighted - first - unit * second) * scale


def swapped(rows):
    width = rows.shape[1]
    if width % 128:
        half = HEAD_DIM // 2
        parts = []
        for start in range(0, width, HEAD_DIM):
            parts += [rows[:, start + half : start + HEAD_DIM], rows[:, start : start + half]]
        return jnp.concatenate(parts, axis=1)
    lane = lax.broadcasted_iota(jnp.int32, rows.shape, 1)
    ahead = pltpu.roll(rows, width - HEAD_DIM // 2, 1)
    behind = pltpu.roll(rows, HEAD_DIM // 2, 1)
    return jnp.where(lane % HEAD_DIM < HEAD_DIM // 2, ahead, behind)


def widened(table, width):
    if width <= table.shape[1]:
        return table[:, :width]
    return jnp.concatenate([table] * (width // table.shape[1]), axis=1)


def head_part(rows, head):
    lane = lax.broadcasted_iota(jnp.int32, rows.shape, 1)
    return jnp.where(lane // HEAD_DIM == head, rows, jnp.zeros_like(rows))


def norm_kernel(tokens, norm_out, gain_out):
    count, rows, width = tokens.shape
    rows = rows - 16
    part = width // count
    for n in range(count):
        gain_out[:, n * part : (n + 1) * part] = tokens[n, rows:, :part].astype(F32)[:2]

    def step(n, _):
        unit, _ = normalized(tokens[n, :rows].astype(F32))
        at = pl.ds(pl.multiple_of(n * rows, rows), rows)
        norm_out[at, :] = (unit * gain_out[0:1, :]).astype(BF16)
        return 0

    lax.fori_loop(0, count, step, 0)


def qkv_kernel(pieces, block, place, norm, down, ups, cosine, sine, *refs):
    weights, (query, key, value, whole) = refs[:pieces], refs[pieces : pieces + 4]
    width = query.shape[1]
    if pieces == 1:
        whole[...] = weights[0][...]
    else:
        out_weight = refs[pieces + 4]
        unit = width // 2
        first = 0
        for n in range(pieces):
            depth = weights[n].shape[0]
            spot = place[n]
            half, part = spot // 4, lax.rem(spot, 4)
            down_at = pl.ds(pl.multiple_of(part * width + first, depth), depth)
            double, single = place[pieces + half], place[pieces + 2]
            whole[double, down_at, :] = weights[n][:, :width]
            across = pl.ds(pl.multiple_of(half * unit, unit), unit)
            whole[single, down_at, across] = weights[n][:, width : width + unit]
            across = pl.ds(pl.multiple_of(spot * unit, unit), unit)
            out_weight[first : first + depth, across] = weights[n][:, width + unit :]
            first = (first + depth) % width
    for kind in range(3):
        whole[kind] = (whole[kind].astype(F32) + tn(down[...], ups[kind])).astype(BF16)

    def step(n, _):
        at = pl.ds(pl.multiple_of(n * block, block), block)
        rows = norm[at, :]
        cos, sin = widened(cosine[at, :], width), widened(sine[at, :], width)
        for kind, out in enumerate((query, key, value)):
            part = nn(rows, whole[kind])
            if kind < 2:
                part = part * cos + swapped(part) * sin
            if kind == 0:
                part = part.astype(BF16).astype(F32) * 0.125
            out[at, :] = part.astype(BF16)
        return 0

    lax.fori_loop(0, norm.shape[0] // block, step, 0)


def chunked(ref, base, value):
    count = -(-value.shape[1] // 128)
    for n in range(count):
        part = value[:, n * 128 : (n + 1) * 128].astype(ref.dtype)
        if part.shape[1] < 128:
            ref[base + n] = jnp.zeros(ref.shape[1:], ref.dtype)
            ref[base + n, :, : part.shape[1]] = part
        else:
            ref[base + n] = part
    return base + count


def attend_kernel(count, order, query, key, value, seg_col, seg_row, *refs):
    outs, (log_total, value_t, bias) = refs[:count], refs[count:]
    block = outs[0].shape[0]
    width = query.shape[1]
    value_t[...] = value[...].T

    def step(n, _):
        at = pl.ds(pl.multiple_of(order[n] * block, block), block)
        rows = query[at, :]
        bias[...] = jnp.where(seg_col[...] == seg_row[:, at], 0.0, -1e30)
        parts = []
        for head in range(width // HEAD_DIM):
            scores = nt(key[...], head_part(rows, head)) + bias[...]
            top = jnp.max(scores, axis=0, keepdims=True)
            raised = jnp.exp(scores - top)
            total = jnp.sum(raised, axis=0, keepdims=True)
            log_total[head : head + 1, at] = top + jnp.log(total)
            prob = (raised * (1.0 / total)).astype(BF16)
            parts.append(nn(value_t[head * HEAD_DIM : (head + 1) * HEAD_DIM, :], prob))
        mixed = jnp.concatenate(parts, axis=0).T
        to_slot(outs, n, mixed.astype(BF16))
        return 0

    lax.fori_loop(0, count, step, 0)


def out_kernel(count, order, inputs, gain, down, up, *refs):
    attn, weights = refs[:count], refs[count : 2 * count]
    middle, norm, narrow = refs[2 * count :]
    width = attn[0].shape[1]
    total = inputs[...].astype(F32)
    thin = jnp.zeros(narrow.shape, F32)
    for n in range(count):
        total = total + nn(attn[n][...], weights[n][...])
        thin = thin + nt(attn[n][...], down[order[n]])
    thin = thin.astype(BF16)
    total = total + nn(thin, up[...])
    middle[...] = total
    narrow[...] = thin
    norm[...] = (normalized(total)[0] * gain[1:2, :]).astype(BF16)


def mlp_pre_kernel(packed, order, place, down_in, up_in, down_out, up_out, grads, *refs):
    pieces = 9 if packed else 2
    weights, (w_in, w_out, grad_act) = refs[:pieces], refs[pieces:]
    hidden, width = w_out.shape
    if packed:
        depth, thin = width // 4, width // 8
        first = 0
        for n in range(pieces):
            rows = slice(first, first + weights[n].shape[0])
            spot = place[n]
            across = pl.ds(pl.multiple_of(lax.rem(spot, 4) * depth, depth), depth)
            w_in[spot // 4, rows, across] = weights[n][:, :depth]
            across = pl.ds(pl.multiple_of(spot * thin, thin), thin)
            w_out[rows, across] = weights[n][:, depth:]
            first = rows.stop % hidden
    else:
        w_in[...] = weights[0][...]
        w_out[...] = weights[1][...]
    for n in range(2):
        w_in[n] = (w_in[n].astype(F32) + tn(up_in[n], down_in[...])).astype(BF16)
    w_out[...] = (w_out[...].astype(F32) + tn(down_out[...], up_out[...])).astype(BF16)

    for n in range(grads.shape[0]):
        grad_act[n] = nt(grads[order[n]], w_out[...])


def mlp_kernel(count, first, w_in, grad_act, *refs):
    norms, backs, (act_out, grad_out) = refs[:count], refs[count : 2 * count], refs[2 * count :]
    rows = norms[0].shape[0]
    for n in range(count):
        norm = norms[n][...]
        inputs, gate = nt(norm, w_in[0]), nt(norm, w_in[1])
        phi = 0.5 + 0.5 * lax.erf(inputs * (0.5**0.5))
        gelu = inputs * phi
        act_out[n] = (gelu * gate).astype(BF16)
        back_act = grad_act[first + n]
        slope = phi + inputs * (jnp.exp(-0.5 * inputs * inputs) * 0.3989422804014327)
        grad_inputs = (back_act * gate * slope).astype(BF16)
        grad_gate = (back_act * gelu).astype(BF16)
        grad_out[0, n] = grad_inputs
        grad_out[1, n] = grad_gate
        backs[n][...] = (nn(grad_inputs, w_in[0]) + nn(grad_gate, w_in[1])).astype(BF16)


def mlp_post_kernel(count, first, order, pick, down_in, up_in, down_out, up_out, w_out, *refs):
    acts, grads, out_grad, refs = refs[:2], refs[2:4], refs[4], refs[5:]
    norms, outs = refs[:count], refs[count : 2 * count]
    terms, norm_all, act_all, grad_all = refs[2 * count : 2 * count + 4]
    down_in_grad, up_in_grad, down_out_grad, up_out_grad = refs[2 * count + 4 :]
    for n in range(count):
        norm_all[n] = norms[n][...]
        act_all[n] = acts[n // 2][n % 2]
        for h in range(2):
            grad_all[h, n] = grads[n // 2][h, n % 2]
    for ref in (down_in_grad, up_in_grad, down_out_grad, up_out_grad):
        ref[...] = jnp.zeros_like(ref)

    def step(n, _):
        act, norm = act_all[n], norm_all[n]
        grad = out_grad[order[first + n]]
        to_slot(outs, n, nn(act, w_out[...]).astype(BF16))
        narrow = nt(norm, down_in[...]).astype(BF16)
        narrow_two = nt(act, down_out[...]).astype(BF16)
        inner = nt(grad, up_out[...]).astype(BF16)
        inner_in = (nt(grad_all[0, n], up_in[0]) + nt(grad_all[1, n], up_in[1])).astype(BF16)
        down_in_grad[...] += tn(inner_in, norm)
        up_in_grad[0] += tn(narrow, grad_all[0, n])
        up_in_grad[1] += tn(narrow, grad_all[1, n])
        down_out_grad[...] += tn(inner, act)
        up_out_grad[...] += tn(narrow_two, grad)
        return 0

    lax.fori_loop(0, count, step, 0)
    at = chunked(terms, 0, up_in_grad[0])
    at = chunked(terms, at, up_in_grad[1])
    at = chunked(terms, at, down_out_grad[...])
    terms[at] = jnp.full(terms.shape[1:], pick[0].astype(F32)).astype(terms.dtype)
    at = chunked(terms, at + 1, down_in_grad[...])
    chunked(terms, at, up_out_grad[...])


def out_back_kernel(count, parts, order, middle, out_grad, gain, down, up, narrow, *refs):
    back, refs = refs[:parts], refs[parts:]
    attn, weights = refs[:count], refs[count : 2 * count]
    grad_mid, refs = refs[2 * count], refs[2 * count + 1 :]
    slots, (terms, down_grad) = refs[:count], refs[count:]
    total = back[0][...].astype(F32)
    for ref in back[1:]:
        total = total + ref[...].astype(F32)
    grad = out_grad[...].astype(F32) + norm_back(middle[...], gain[1:2, :], total)
    grad_mid[...] = grad
    low = grad.astype(BF16)
    inner = nt(low, up[...]).astype(BF16)
    chunks = middle.shape[1] // 128
    chunked(terms, chunks, tn(narrow[...], low))
    for n in range(count):
        slots[n][...] = (nt(low, weights[n][...]) + nn(inner, down[order[n]])).astype(BF16)
        down_grad[order[n]] = tn(inner, attn[n][...])
    chunked(terms, 0, jnp.concatenate([down_grad[n] for n in range(count)], axis=1))


def attend_back_kernel(
    count, order, query, key, value, seg_col, seg_row, log_total, cosine, sine, weights, *refs
):
    grads, outs = refs[:count], refs[count : 2 * count]
    grad_qkv, key_t, bias, grad_all, grad_q, grad_k, grad_v = refs[2 * count :]
    block = outs[0].shape[0]
    width = query.shape[1]
    key_t[...] = key[...].T
    for n in range(count):
        grad_all[n * block : (n + 1) * block, :] = grads[n][...]
    for ref in (grad_k, grad_v):
        ref[...] = jnp.zeros_like(ref)

    def step(n, _):
        at = pl.ds(pl.multiple_of(order[n] * block, block), block)
        rows = query[at, :]
        grad = grad_all[pl.ds(pl.multiple_of(n * block, block), block), :]
        bias[...] = jnp.where(seg_col[...] == seg_row[:, at], 0.0, -1e30)
        parts = []
        for head in range(width // HEAD_DIM):
            own = head_part(rows, head)
            own_grad = head_part(grad, head)
            scores = nt(key[...], own) + bias[...]
            prob = jnp.exp(scores - log_total[head : head + 1, at])
            grad_prob = nt(value[...], own_grad)
            dots = jnp.sum(prob * grad_prob, axis=0, keepdims=True)
            grad_s = (prob * (grad_prob - dots)).astype(BF16)
            grad_k[...] += nn(grad_s, own)
            grad_v[...] += nn(prob.astype(BF16), own_grad)
            parts.append(nn(key_t[head * HEAD_DIM : (head + 1) * HEAD_DIM, :], grad_s))
        grad_q[at, :] = jnp.concatenate(parts, axis=0).T * 0.125
        return 0

    lax.fori_loop(0, count, step, 0)

    def finish(n, _):
        at = pl.ds(pl.multiple_of(order[n] * block, block), block)
        cos, sin = widened(cosine[at, :], width), widened(sine[at, :], width)
        low = []
        for ref in (grad_q, grad_k):
            part = ref[at, :]
            low.append((part * cos - swapped(part) * sin).astype(BF16))
        low.append(grad_v[at, :].astype(BF16))
        total = 0.0
        for kind in range(3):
            grad_qkv[kind, at, :] = low[kind]
            total = total + nt(low[kind], weights[kind])
        to_slot(outs, n, total.astype(BF16))
        return 0

    lax.fori_loop(0, count, finish, 0)


def qkv_terms_kernel(pick, norm, grad_qkv, down, ups, terms):
    narrow = nt(norm[...], down[...]).astype(BF16)
    inner = sum(nt(grad_qkv[kind], ups[kind]) for kind in range(3)).astype(BF16)
    at = 0
    for kind in range(3):
        at = chunked(terms, at, tn(narrow, grad_qkv[kind]))
    terms[at] = jnp.full(terms.shape[1:], pick[0].astype(F32)).astype(terms.dtype)
    chunked(terms, at + 1, tn(inner, norm[...]))


def last_kernel(parts, inputs, grad_mid, gain, *refs):
    out = refs[parts]
    total = refs[0][...].astype(F32)
    for ref in refs[1:parts]:
        total = total + ref[...].astype(F32)
    back = norm_back(inputs[...].astype(F32), gain[0:1, :], total)
    out[...] = (grad_mid[...] + back).astype(BF16)


def pair_kernel(local, count, across, *refs):
    own, came, out = refs[:count], refs[count : 2 * count], refs[2 * count]
    out[pl.ds(across[0] * local, local)] = own[0][:local]
    out[pl.ds((1 - across[0]) * local, local)] = came[0][:local]
    at = 2 * local
    for n in range(count):
        first = local if n == 0 else 0
        size = own[n].shape[0] - first
        total = own[n][first:].astype(F32) + came[n][first:].astype(F32)
        out[at : at + size] = total.astype(BF16)
        at += size


def stack_kernel(pieces, place, *refs):
    out = refs[pieces]
    first = 0
    for n in range(pieces):
        size = refs[n].shape[0]
        out[place[n], first : first + size] = refs[n][...]
        first = (first + size) % out.shape[1]


def spread_kernel(widths, local, core, mine, other, *refs):
    outs, both = refs[: len(widths)], refs[len(widths)]
    both[core[0]] = mine[...]
    both[1 - core[0]] = other[...]
    for out in outs:
        out[...] = jnp.zeros_like(out)

    def step(n, _):
        pick = jnp.max(both[0, n, local - 1].astype(F32)).astype(jnp.int32)
        at, rest = 0, 2 * local
        for out, width in zip(outs, widths):
            if not width:
                for first in range(0, out.shape[2], 128):
                    term = both[0, n, rest].astype(F32) + both[1, n, rest].astype(F32)
                    out[pick, :, first : first + 128] += term
                    rest += 1
                continue
            blocks = -(-width // 128)
            for group in range(out.shape[2] // (4 * width)):
                for tok in range(4):
                    first = (group * 4 + tok) * width
                    base = (tok // 2) * local + at
                    parts = [both[tok % 2, n, base + m] for m in range(blocks)]
                    term = jnp.concatenate(parts, axis=1)[:, :width].astype(F32)
                    out[pick, :, first : first + width] += term
                at += blocks
        return 0

    lax.fori_loop(0, mine.shape[0], step, 0)


class Exchange:
    def __init__(self, size):
        self.size = size
        self.direct = size == 4
        own = lax.axis_index("tok")
        steps = jnp.arange(size, dtype=jnp.int32)
        self.order = jnp.bitwise_xor(own, steps) if self.direct else steps

    def swap(self, block, bits):
        pairs = [(n, n ^ bits) for n in range(self.size)]
        return lax.ppermute(block, "tok", pairs)

    def gather(self, block):
        if not self.direct:
            whole = lax.all_gather(block, "tok", axis=0)
            return [whole[n] for n in range(self.size)]
        across = self.swap(block, 2)
        return [block, self.swap(block, 1), across, self.swap(across, 1)]

    def hop(self, block):
        if not self.direct:
            return self.gather(block)
        return [block, self.swap(block, 1), self.swap(block, 2)]

    def land(self, parts):
        if not self.direct:
            return parts
        return parts + [self.swap(parts[2], 1)]

    def turn(self, slots):
        if not self.direct:
            whole = lax.all_to_all(jnp.stack(slots), "tok", 0, 0)
            return [whole[n] for n in range(self.size)]
        return [slots[0]] + [self.swap(slots[n], n) for n in range(1, self.size)]

    def reduce(self, slots):
        if not self.direct:
            return [lax.psum_scatter(jnp.stack(slots), "tok", scatter_dimension=0)]
        near, both = self.halve(slots)
        return [slots[0], near, self.swap(both, 2)]

    def halve(self, slots):
        near, far = self.swap(slots[1], 1), self.swap(slots[3], 1)
        return near, (slots[2].astype(F32) + far.astype(F32)).astype(slots[2].dtype)

    def slots_of(self, whole):
        return [lax.dynamic_index_in_dim(whole, self.order[n], 0, False) for n in range(self.size)]


RING = (0, 2, 4, 6, 7, 5, 3, 1)


def meet(*arrays):
    return lax.optimization_barrier(arrays)


class Ring:
    def __init__(self, block):
        self.blocks, self.shifts = [block], [0]
        self.right = self.left = block
        rows = block.shape[0]
        self.half = rows // 32 * 16 if block.ndim == 2 else rows // 2
        self.ahead = [(RING[n], RING[(n + 1) % len(RING)]) for n in range(len(RING))]
        self.behind = [(b, a) for a, b in self.ahead]

    def step(self):
        step = len(self.blocks) // 2 + 1
        if step == len(RING) // 2:
            self.right, self.left = self.right[: self.half], self.left[self.half :]
        self.right = lax.ppermute(self.right, "seq", self.ahead)
        self.left = lax.ppermute(self.left, "seq", self.behind)
        self.blocks += [self.right, self.left]
        self.shifts += [-step, step]

    def meet(self, *arrays):
        self.right, self.left, *arrays = meet(self.right, self.left, *arrays)
        if len(self.blocks) > 1:
            self.blocks[-2:] = [self.right, self.left]
        return arrays

    def came(self):
        own, size = lax.axis_index("seq"), len(RING)
        place = jnp.where(own % 2 == 0, own // 2, size - 1 - own // 2)
        came = jnp.remainder(place + jnp.array(self.shifts, jnp.int32), size)
        came = jnp.where(came < size // 2, 2 * came, 2 * (size - 1 - came) + 1)
        return came.astype(jnp.int32)


def owner_of_columns(seq, tok):
    double, single, seen = [], [], [0] * tok
    kinds = [[0, 0, 0] for _ in range(tok)]
    for s in range(seq):
        first = 3 * s + s % 2
        owner = first % seq // 2
        double.append((owner, seen[owner]))
        kinds[owner][seen[owner]] = first // seq
        seen[owner] += 1
        last = 3 * s + 2 * (1 - s % 2)
        single.append((last % seq // 2, last % 2))
        kinds[last % seq // 2][2] = last // seq
    return double, single, kinds


def body(
    tokens,
    out_grad,
    segments,
    adapter_index,
    qkv_weight,
    out_weight,
    in_weight,
    out2_weight,
    attn_gain,
    mlp_gain,
    qkv_down,
    qkv_up,
    out_down,
    out_up,
    in_down,
    in_up,
    out2_down,
    out2_up,
):
    seq, tok = lax.axis_size("seq"), lax.axis_size("tok")
    own_seq, own_tok = lax.axis_index("seq"), lax.axis_index("tok")
    move = Exchange(tok)
    fast = tok == 4 and seq == 8
    order = move.order
    adapters, rank, width = qkv_down.shape
    length = segments.shape[1]
    rows = tokens.shape[1]
    heads = HEADS // tok
    lanes = heads * HEAD_DIM
    hidden = out2_weight.shape[0]
    hidden_all = hidden * tok
    inputs, out_grad = tokens[0], out_grad[0]
    pick = adapter_index[0]

    def chosen(table, start=0, size=None):
        size = table.shape[2] if size is None else size
        return lax.dynamic_slice(table, (pick, 0, start), (1, rank, size))[0]

    gain_rows = jnp.pad(jnp.stack([attn_gain, mlp_gain]), ((0, 14), (0, width - width // tok)))
    token_all = lax.all_gather(jnp.concatenate([inputs, gain_rows], axis=0), "tok", axis=0)
    norm_one, gain = call(
        norm_kernel,
        [shape((length, width), BF16), shape((2, width), F32)],
        [token_all],
        name="norm_one",
    )
    token_all, out_grad_in = meet(token_all, out_grad)
    grad_all = lax.all_gather(out_grad_in, "tok", axis=0)
    if fast:
        unit = width // seq
        double, single, kinds = owner_of_columns(seq, tok)
        odd = (own_seq % 2) * unit
        parts = []
        for owners, start, size in ((double, odd, 2 * unit), (single, 2 * (unit - odd), unit)):
            pairs = [
                (s * tok + t, (owners[s][1] * tok + t) * tok + owners[s][0])
                for s in range(seq)
                for t in range(tok)
            ]
            piece = lax.dynamic_slice_in_dim(qkv_weight, start, size, 1)
            parts.append(lax.ppermute(piece, ("seq", "tok"), pairs))
        ring = Ring(jnp.concatenate(parts + [out_weight], axis=1))
        ring.step()
        ring.step()
        (in_piece,) = ring.meet(in_weight.T)
        pairs = [
            (s * tok + t, ((s // tok) * tok + t) * tok + s % tok)
            for s in range(seq)
            for t in range(tok)
        ]
        in_piece = lax.ppermute(in_piece, ("seq", "tok"), pairs)
        ring.step()
        norm_one, gain = ring.meet(norm_one, gain)
        ring.step()
        mlp_piece = jnp.concatenate([in_piece, out2_weight], axis=1)
        (mlp_piece,) = ring.meet(mlp_piece)
        qkv_pieces = ring.blocks
        place = jnp.concatenate([ring.came(), jnp.array(kinds, jnp.int32)[own_tok]])
        mlp_ring = Ring(mlp_piece)
        mlp_ring.step()
    else:

        def columns(weight, count):
            block = lax.all_gather(weight, "seq", axis=1, tiled=True)
            split = block.reshape(block.shape[0], count, tok, -1).transpose(2, 1, 0, 3)
            turned = lax.all_to_all(split, "tok", 0, 0)
            return turned.transpose(1, 0, 2, 3).reshape(count, width, -1)

        qkv_pieces = [columns(qkv_weight, 3)]
        place = jnp.zeros((1,), jnp.int32)
        own_out = lax.all_gather(out_weight, "seq", axis=1, tiled=True)
        mlp_weights = [
            columns(in_weight, 2).transpose(0, 2, 1),
            lax.all_gather(out2_weight, "seq", axis=1, tiled=True),
        ]

    down_one = chosen(qkv_down)
    up_one = jnp.stack([chosen(qkv_up, n * width + own_tok * lanes, lanes) for n in range(3)])
    down_attn = chosen(out_down).reshape(rank, tok, lanes).transpose(1, 0, 2)
    up_attn = chosen(out_up)
    down_two = chosen(in_down)
    up_two = jnp.stack([chosen(in_up, n * hidden_all + own_tok * hidden, hidden) for n in range(2)])
    down_last = chosen(out2_down, own_tok * hidden, hidden)
    up_last = chosen(out2_up)
    exponent = jnp.arange(0, HEAD_DIM, 2).astype(F32) / HEAD_DIM
    inverse = 1.0 / THETA**exponent
    phases = jnp.arange(length).astype(F32)[:, None] * jnp.tile(inverse, 4)[None, :]
    sign = jnp.where(jnp.arange(2 * HEAD_DIM) % HEAD_DIM < HEAD_DIM // 2, -1.0, 1.0)
    cosine, sine = jnp.cos(phases), jnp.sin(phases) * sign[None, :]
    seg_col = segments.reshape(length, 1)

    query, key, value, w_qkv, *own_row = call(
        functools.partial(qkv_kernel, len(qkv_pieces), rows),
        [shape((length, lanes), BF16)] * 3
        + [shape((3, width, lanes), BF16)]
        + [shape((lanes, width), BF16)] * fast,
        [place, norm_one, down_one, up_one, cosine, sine] + qkv_pieces,
        smem=(0,),
        name="qkv",
    )
    if fast:
        query, key, value = mlp_ring.meet(query, key, value)
        mlp_ring.step()
    out_parts = move.hop(own_row[0] if fast else own_out)
    *attn_slots, log_total = call(
        functools.partial(attend_kernel, tok),
        [shape((rows, lanes), BF16)] * tok + [shape((heads, length), F32)],
        [order, query, key, value, seg_col, segments],
        smem=(0,),
        scratch=[pltpu.VMEM((lanes, length), BF16), pltpu.VMEM((length, rows), F32)],
        name="attend",
    )
    attn_slots, out_parts = meet(attn_slots, out_parts)
    if fast:
        attn_slots = mlp_ring.meet(*attn_slots)
        mlp_ring.step()
    attn = move.turn(attn_slots)
    out_weights = move.land(out_parts)
    if fast:
        attn = mlp_ring.meet(*attn)
        mlp_ring.step()
        mlp_weights, mlp_came = mlp_ring.blocks, mlp_ring.came()
    else:
        mlp_came = place
    middle, norm_two, narrow_attn = call(
        functools.partial(out_kernel, tok),
        [shape((rows, width), F32), shape((rows, width), BF16), shape((rows, rank), BF16)],
        [order, inputs, gain, down_attn, up_attn] + attn + out_weights,
        smem=(0,),
        name="out",
    )
    norm_slots = move.gather(norm_two)
    pieces = lambda columns: -(-columns // 128)
    early_local, late_local = 3 * pieces(hidden) + 1, 3 * pieces(lanes) + 1
    wide = pieces(width)
    w_in, w_out, grad_act = call(
        functools.partial(mlp_pre_kernel, fast),
        [
            shape((2, hidden, width), BF16),
            shape((hidden, width), BF16),
            shape((tok, rows, hidden), F32),
        ],
        [order, mlp_came, down_two, up_two, down_last, up_last, grad_all] + mlp_weights,
        smem=(0, 1),
        name="mlp_pre",
    )
    back_slots, acts, grads_z = [], [], []
    for first in range(0, tok, 2):
        *backs, act, grad_z = call(
            functools.partial(mlp_kernel, 2, first),
            [shape((rows, width), BF16)] * 2
            + [shape((2, rows, hidden), BF16), shape((2, 2, rows, hidden), BF16)],
            [w_in, grad_act] + norm_slots[first : first + 2],
            name="mlp",
        )
        back_slots += backs
        acts.append(act)
        grads_z.append(grad_z)
    pieces = lambda columns: -(-columns // 128)
    early_local, late_local = 3 * pieces(hidden) + 1, 3 * pieces(lanes) + 1
    wide = pieces(width)
    back_two = move.reduce(back_slots)
    grad_mid, *rest = call(
        functools.partial(out_back_kernel, tok, len(back_two)),
        [shape((rows, width), F32)]
        + [shape((rows, lanes), BF16)] * tok
        + [shape((2 * wide, rank, 128), BF16)],
        [order, middle, out_grad, gain, down_attn, up_attn, narrow_attn]
        + back_two
        + attn
        + out_weights,
        smem=(0,),
        scratch=[pltpu.VMEM((tok, rank, lanes), F32)],
        name="out_back",
    )
    attn_grads, out_terms = move.turn(rest[:tok]), rest[tok]
    out_slots, early = [], []
    for first in range(0, tok, 4):
        pair = slice(first // 2, first // 2 + 2)
        *outs, terms = call(
            functools.partial(mlp_post_kernel, 4, first),
            [shape((rows, width), BF16)] * 4
            + [shape((early_local + 2 * wide, rank, 128), BF16 if fast else F32)],
            [order, adapter_index, down_two, up_two, down_last, up_last, w_out]
            + acts[pair]
            + grads_z[pair]
            + [grad_all]
            + norm_slots[first : first + 4],
            smem=(0, 1),
            scratch=[
                pltpu.VMEM((4, rows, width), BF16),
                pltpu.VMEM((4, rows, hidden), BF16),
                pltpu.VMEM((2, 4, rows, hidden), BF16),
                pltpu.VMEM((rank, width), F32),
                pltpu.VMEM((2, rank, hidden), F32),
                pltpu.VMEM((rank, hidden), F32),
                pltpu.VMEM((rank, width), F32),
            ],
            name="mlp_post",
        )
        out_slots += outs
        early.append(terms)
    early = sum(early[1:], early[0])
    *one_slots, grad_qkv = call(
        functools.partial(attend_back_kernel, tok),
        [shape((rows, width), BF16)] * tok + [shape((3, length, lanes), BF16)],
        [order, query, key, value, seg_col, segments, log_total, cosine, sine, w_qkv] + attn_grads,
        smem=(0,),
        scratch=[
            pltpu.VMEM((lanes, length), BF16),
            pltpu.VMEM((length, rows), F32),
            pltpu.VMEM((length, lanes), BF16),
            pltpu.VMEM((length, lanes), F32),
            pltpu.VMEM((length, lanes), F32),
            pltpu.VMEM((length, lanes), F32),
        ],
        name="attend_back",
    )
    late = call(
        qkv_terms_kernel,
        [shape((late_local + wide, rank, 128), BF16)],
        [adapter_index, norm_one, grad_qkv, down_one, up_one],
        smem=(0,),
        name="qkv_terms",
    )[0]
    out_sums = move.reduce(out_slots)
    layer_out = (middle + sum(part.astype(F32) for part in out_sums)).astype(BF16)

    def last_of(back_one):
        return call(
            functools.partial(last_kernel, len(back_one)),
            [shape((rows, width), BF16)],
            [inputs, grad_mid, gain] + back_one,
            name="last",
        )[0]

    grads = lambda columns: shape((adapters, rank, columns), F32)
    if fast:
        across, core = (own_tok // 2).reshape(1), (own_tok % 2).reshape(1)

        def paired(local, terms, came):
            size = sum(term.shape[0] for term in terms) + local
            return call(
                functools.partial(pair_kernel, local, len(terms)),
                [shape((size, rank, 128), BF16)],
                [across] + terms + came,
                smem=(0,),
                name="pair",
            )[0]

        def spread(whole, local, widths, columns):
            return call(
                functools.partial(spread_kernel, widths, local),
                [grads(size) for size in columns],
                [core, whole, move.swap(whole, 1)],
                smem=(0,),
                scratch=[pltpu.VMEM((2,) + whole.shape, BF16)],
                name="spread",
            )

        terms = [early, out_terms]
        early = paired(early_local, terms, [move.swap(term, 2) for term in terms])
        early = lax.all_gather(early, "seq", axis=0)
        near, both = move.halve(one_slots)
        both, late_came = meet(both, move.swap(late, 2))
        back_one = [one_slots[0], near, move.swap(both, 2)]
        ring = Ring(paired(late_local, [late], [late_came]))
        ring.step()
        ring.step()
        early, back_one[2] = ring.meet(early, back_one[2])
        ring.step()
        (
            in_up_grad,
            out2_down_grad,
            in_down_grad,
            out2_up_grad,
            out_down_grad,
            out_up_grad,
        ) = spread(
            early,
            early_local,
            (hidden, hidden, 0, 0, 0, 0),
            (2 * hidden_all, hidden_all) + (width,) * 4,
        )
        (in_up_grad,) = ring.meet(in_up_grad)
        ring.step()
        (input_grad,) = ring.meet(last_of(back_one))
        late = call(
            functools.partial(stack_kernel, len(ring.blocks)),
            [shape((seq,) + ring.blocks[0].shape, BF16)],
            [ring.came()] + ring.blocks,
            smem=(0,),
            name="stack",
        )[0]
        qkv_up_grad, qkv_down_grad = spread(late, late_local, (lanes, 0), (3 * width, width))
    else:
        input_grad = last_of(move.reduce(one_slots))
        picked = (pick == jnp.arange(adapters)).astype(F32)[:, None, None]

        def term(blocks, columns):
            return blocks.astype(F32).transpose(1, 0, 2).reshape(rank, -1)[:, :columns]

        def placed(terms, first, groups, columns):
            total = jnp.zeros((rank, groups * tok * columns), F32)
            for group in range(groups):
                at = first + group * pieces(columns)
                part = term(terms[at : at + pieces(columns)], columns)
                start = (group * tok + own_tok) * columns
                total = lax.dynamic_update_slice(total, part, (0, start))
            return total

        whole = lambda terms, at: term(terms[at : at + wide], width)
        sums = (
            whole(late, late_local),
            placed(late, 0, 3, lanes),
            whole(out_terms, 0),
            whole(out_terms, wide),
            whole(early, early_local),
            placed(early, 0, 2, hidden),
            placed(early, 2 * pieces(hidden), 1, hidden),
            whole(early, early_local + wide),
        )
        summed = lax.psum(tuple(picked * part[None] for part in sums), ("seq", "tok"))
        qkv_down_grad, qkv_up_grad, out_down_grad, out_up_grad = summed[:4]
        in_down_grad, in_up_grad, out2_down_grad, out2_up_grad = summed[4:]
    return (
        layer_out[None],
        input_grad[None],
        qkv_down_grad,
        qkv_up_grad,
        out_down_grad,
        out_up_grad,
        in_down_grad,
        in_up_grad,
        out2_down_grad,
        out2_up_grad,
    )


def solution(mesh):
    grid = P("tok", "seq")
    split = P("seq", "tok", None)
    return jax.shard_map(
        body,
        mesh=mesh,
        in_specs=(split, split, P("seq", None), P("seq"), grid, grid, grid, grid, P("tok"), P("tok"))
        + (P(),) * 8,
        out_specs=(split, split) + (P(),) * 8,
        check_vma=False,
    )
```

time: 1200 us -> 292 us (0.24)
  waiting for transfers between devices: 760 us -> 76 us
  matrix products: 161 us -> 0 us
  Pallas kernels: 0 us -> 120 us
  local copies, waits for them, and re-layouts: 125 us -> 23.1 us
  other arithmetic: 65.7 us -> 10.2 us
  starting transfers between devices: 0.91 us -> 47 us
  blocking collectives: 37.4 us -> 0 us
  loops' own time: 27.1 us -> 0 us
    all_gather x7 -> x3, waiting for transfers between devices: 325 us -> 0.04 us  [the longest x1 0.02 us: body(): lax.all_gather(jnp.concatenate([inputs, gain_rows], axis=0), 'tok', axis=0)]
    reduce_scatter x16 -> x0, waiting for transfers between devices: 267 us -> none  [the longest x8 169 us: summed_group(): lax.psum_scatter(grad_value.reshape(seq_count, seq_length, group_width).a...]
    psum x1 -> x0, waiting for transfers between devices: 167 us -> none  [body(): lax.psum((spread_back(terms[0], onehot), spread_back(terms[1], onehot), s...]
    dot_general x96 -> x0, matrix products: 161 us -> none  [the longest x8 28.5 us: summed_group(): jnp.einsum('shqk,sqhd->skhd', grad_scores, query_part, preferred_element_...]
    pallas_call x0 -> x17, Pallas kernels: none -> 120 us  [call(): pl.pallas_call(kernel, out_shape=out_shape, in_specs=specs, out_specs=[pl...]
    ppermute x0 -> x53, waiting for transfers between devices: none -> 75.9 us  [the longest x26 35.6 us: swap(): return lax.ppermute(block, 'tok', pairs)]
    dynamic_slice x65 -> x5, local copies, waits for them, and re-layouts: 58.2 us -> 3.04 us  [the longest x3 3.01 us: chosen(): return lax.dynamic_slice(table, (pick, 0, start), (1, rank, size))[0]]
    ppermute x0 -> x53, starting transfers between devices: none -> 46.9 us  [the longest x12 26 us: step(): self.right = lax.ppermute(self.right, 'seq', self.ahead)]
  transfers between devices with their start and end apart: 24 -> 56, of which waited for: 23 -> 23; matrix products, arithmetic and copies ran while one was open for 16% -> 7% of each run, Pallas kernels for 0% -> 39%
where the time goes in v1:
time: 292 us; the launch traced here: 291 us
  Pallas kernels  120 us (41%)
  waiting for transfers between devices  76 us (26%)
  starting transfers between devices  47 us (16%)
  local copies, waits for them, and re-layouts  23.1 us (8%)
  between operations  15.1 us (5%)
  other arithmetic  10.2 us (3%)
    pallas_call x17, Pallas kernels, call(): pl.pallas_call(kernel, out_shape=out_shape, in_specs=specs, out_specs=[pl...  120 us
    ppermute x26, waiting for transfers between devices, swap(): return lax.ppermute(block, 'tok', pairs)  35.6 us
    ppermute x12, starting transfers between devices, step(): self.right = lax.ppermute(self.right, 'seq', self.ahead)  26 us
    ppermute x12, waiting for transfers between devices, step(): self.right = lax.ppermute(self.right, 'seq', self.ahead)  23.7 us
    ppermute x26, starting transfers between devices, swap(): return lax.ppermute(block, 'tok', pairs)  10.8 us
    unnamed x114, local copies, waits for them, and re-layouts  9.13 us
    ppermute x2, waiting for transfers between devices, body(): parts.append(lax.ppermute(piece, ('seq', 'tok'), pairs))  8.9 us
    ppermute x12, waiting for transfers between devices, step(): self.left = lax.ppermute(self.left, 'seq', self.behind)  7.8 us
  transfers between devices with their start and end apart: 56, of which 23 were waited for; matrix products, arithmetic and copies ran while one was open for 7% of the time, Pallas kernels for 39%

profile of v1, /device:TPU:0, one launch (start us, length us, event | category | flops | bytes accessed | tf_op | source)
XLA Modules:
  0.0 290.9 jit_solution(1540298478103692353)
XLA Ops:
  11.4 4.4 %collective-permute-start.1 = (bf16[256,128]{1,0:T(8,128)(2,1)S(1)}, bf16[256,128]{1,0:T(8,128)(2,1)S(1)}, u32[]{:S(2)}, u32[]{:S(2)}) collective-permute-start(bf16[256,128]{1,0:T(8,128)(2,1)S(1)} %constant_dynamic-slice_fusion.7), channel_id=1, source_target_pairs={{0,1},{1,5},{2,9},{3,13},{4,17},{5,21},{6,25},{7,29},{8,0},{9,4},{... | collective-permute-start | bytes 196616 | tf_op jit(solution)/shard_map/ppermute | solution.py:606
  15.8 8.9 %collective-permute-done.1 = bf16[256,128]{1,0:T(8,128)(2,1)S(1)} collective-permute-done((bf16[256,128]{1,0:T(8,128)(2,1)S(1)}, bf16[256,128]{1,0:T(8,128)(2,1)S(1)}, u32[]{:S(2)}, u32[]{:S(2)}) %collective-permute-start.1) | collective-permute-done | bytes 65568 | tf_op jit(solution)/shard_map/ppermute | solution.py:606
  28.3 3.4 %collective-permute-done.2.refs_1_ = bf16[256,512]{1,0:T(8,128)(2,1)S(1)} collective-permute-done((bf16[256,512]{1,0:T(8,128)(2,1)S(1)}, bf16[256,512]{1,0:T(8,128)(2,1)S(1)}, u32[]{:S(2)}, u32[]{:S(2)}) %collective-permute-start.2) | collective-permute-done | bytes 262176 | tf_op jit(solution)/shard_map/ppermute | solution.py:511
  33.7 4.3 %collective-permute-done.3.refs_3_ = bf16[256,512]{1,0:T(8,128)(2,1)S(1)} collective-permute-done((bf16[256,512]{1,0:T(8,128)(2,1)S(1)}, bf16[256,512]{1,0:T(8,128)(2,1)S(1)}, u32[]{:S(2)}, u32[]{:S(2)}) %collective-permute-start.3) | collective-permute-done | bytes 262176 | tf_op jit(solution)/shard_map/ppermute | solution.py:511
  42.8 4.5 %norm_one.1 = (bf16[1024,1024]{1,0:T(8,128)(2,1)}, f32[2,1024]{1,0:T(2,128)}) custom-call(bf16[4,272,1024]{2,1,0:T(8,128)(2,1)} %bitcast.43), custom_call_target="tpu_custom_call" | custom-call | flops 1000000000 | bytes 4333568 | tf_op jit(solution)/shard_map/norm_one/pallas_call | solution.py:40
  47.5 6.7 %collective-permute-start.8 = (bf16[128,512]{1,0:T(8,128)(2,1)S(1)}, bf16[128,512]{1,0:T(8,128)(2,1)S(1)}, u32[]{:S(2)}, u32[]{:S(2)}) collective-permute-start(bf16[128,512]{1,0:T(8,128)(2,1)S(1)} %slice.18), channel_id=1, source_target_pairs={{0,8},{8,16},{16,24},{24,28},{28,20},{20,12},{12,4},{4,0},{1,9},{9... | collective-permute-start | bytes 393224 | tf_op jit(solution)/shard_map/ppermute | solution.py:511
  57.0 2.6 collective-permute-done.9.refs_8_
  63.7 3.0 %fusion = (f32[1024,128]{1,0:T(8,128)}, f32[1024,128]{1,0:T(8,128)}) fusion(f32[128]{0:T(128)S(1)} %compare_select_fusion.2, f32[128]{0:T(128)S(1)} %mul.109, f32[1024]{0:T(1024)S(1)} %iota_convert_fusion), kind=kLoop, calls=%fused_computation.7 | loop fusion | flops 262144 | bytes 1053696 | tf_op jit(solution)/shard_map/mul | solution.py:654
  66.7 7.3 %qkv.1 = (bf16[1024,256]{1,0:T(8,128)(2,1)}, bf16[1024,256]{1,0:T(8,128)(2,1)}, bf16[1024,256]{1,0:T(8,128)(2,1)}, bf16[3,1024,256]{2,1,0:T(8,128)(2,1)}, bf16[256,1024]{1,0:T(8,128)(2,1)}) custom-call(s32[12]{0:T(128)} %pad_add_fusion.place, bf16[1024,1024]{1,0:T(8,128)(2,1)} %get-tuple-element.116.norm, bf16[16,1024]{1,0:T(8,128)(2,1)} %dynamic-slice_bitcast_fusion.2.down, ...), custom_call_target="tpu_custom_call" | custom-call | flops 1000000000 | bytes 8970288 | tf_op jit(solution)/shard_map/qkv/pallas_call | solution.py:40
  79.6 15.1 %attend.1 = (bf16[256,256]{1,0:T(8,128)(2,1)}, bf16[256,256]{1,0:T(8,128)(2,1)}, bf16[256,256]{1,0:T(8,128)(2,1)}, bf16[256,256]{1,0:T(8,128)(2,1)}, f32[4,1024]{1,0:T(4,128)}) custom-call(s32[4]{0:T(128)} %iota_xor_fusion.order, bf16[1024,256]{1,0:T(8,128)(2,1)} %get-tuple-element.124.query, bf16[1024,256]{1,0:T(8,128)(2,1)} %get-tuple-element.125.key, ...), custom_call_target="tpu_custom_call" | custom-call | flops 1000000000 | bytes 2121744 | tf_op jit(solution)/shard_map/attend/pallas_call | solution.py:40
  105.4 3.5 %collective-permute-done.17.refs_5_ = bf16[656,384]{1,0:T(8,128)(2,1)S(1)} collective-permute-done((bf16[656,384]{1,0:T(8,128)(2,1)}, bf16[656,384]{1,0:T(8,128)(2,1)S(1)}, u32[]{:S(2)}, u32[]{:S(2)}) %collective-permute-start.17) | collective-permute-done | bytes 503840 | tf_op jit(solution)/shard_map/ppermute | solution.py:511
  111.5 4.2 %out.1 = (f32[256,1024]{1,0:T(8,128)}, bf16[256,1024]{1,0:T(8,128)(2,1)}, bf16[256,16]{1,0:T(8,128)(2,1)}) custom-call(s32[4]{0:T(128)} %iota_xor_fusion.order, bf16[256,1024]{1,0:T(8,128)(2,1)} %bitcast.38, f32[2,1024]{1,0:T(2,128)} %get-tuple-element.111.gain, bf16[4,16,256]{2,1,0:T(8,128)(2,1)} %bitcast.40, ...), custom_call_target="tpu_custom_call" | custom-call | flops 1000000000 | bytes 4800528 | tf_op jit(solution)/shard_map/out/pallas_call | solution.py:40
  115.7 13.3 %collective-permute-done.26.refs_0_.refs_7_ = bf16[256,1024]{1,0:T(8,128)(2,1)S(1)} collective-permute-done((bf16[256,1024]{1,0:T(8,128)(2,1)}, bf16[256,1024]{1,0:T(8,128)(2,1)S(1)}, u32[]{:S(2)}, u32[]{:S(2)}) %collective-permute-start.26) | collective-permute-done | bytes 524320 | tf_op jit(solution)/shard_map/ppermute | solution.py:452
  135.1 3.8 %collective-permute-done.23.refs_7_ = bf16[320,384]{1,0:T(8,128)(2,1)S(1)} collective-permute-done((bf16[320,384]{1,0:T(8,128)(2,1)S(1)}, bf16[320,384]{1,0:T(8,128)(2,1)S(1)}, u32[]{:S(2)}, u32[]{:S(2)}) %collective-permute-start.23) | collective-permute-done | bytes 245792 | tf_op jit(solution)/shard_map/ppermute | solution.py:511
  139.7 7.9 %mlp_pre.1 = (bf16[2,656,1024]{2,1,0:T(8,128)(2,1)}, bf16[656,1024]{1,0:T(8,128)(2,1)}, f32[4,256,656]{2,1,0:T(8,128)}) custom-call(s32[4]{0:T(128)} %iota_xor_fusion.order, s32[9]{0:T(128)} %copy-done.42, bf16[16,1024]{1,0:T(8,128)(2,1)} %get-tuple-element.212.down_in, bf16[2,16,656]{2,1,0:T(8,128)(2,1)} %pad_maximum_fusion.2.up_in, ...), custom_call_target="tpu_custom_call" | custom-call | flops 1000000000 | bytes 12973620 | tf_op jit(solution)/shard_map/mlp_pre/pallas_call | solution.py:40
  148.4 7.6 %mlp.3 = (bf16[256,1024]{1,0:T(8,128)(2,1)}, bf16[256,1024]{1,0:T(8,128)(2,1)}, bf16[2,256,656]{2,1,0:T(8,128)(2,1)}, bf16[2,2,256,656]{3,2,1,0:T(8,128)(2,1)}) custom-call(bf16[2,656,1024]{2,1,0:T(8,128)(2,1)} %get-tuple-element.154.w_in, f32[4,256,656]{2,1,0:T(8,128)} %get-tuple-element.155.grad_act, bf16[256,1024]{1,0:T(8,128)(2,1)} %copy-done.4, ...), custom_call_target="tpu_custom_call" | custom-call | flops 1000000000 | bytes 9486336 | tf_op jit(solution)/shard_map/mlp/pallas_call | solution.py:40
  156.8 7.6 %mlp.2 = (bf16[256,1024]{1,0:T(8,128)(2,1)}, bf16[256,1024]{1,0:T(8,128)(2,1)}, bf16[2,256,656]{2,1,0:T(8,128)(2,1)}, bf16[2,2,256,656]{3,2,1,0:T(8,128)(2,1)}) custom-call(bf16[2,656,1024]{2,1,0:T(8,128)(2,1)} %get-tuple-element.154.w_in, f32[4,256,656]{2,1,0:T(8,128)} %get-tuple-element.155.grad_act, bf16[256,1024]{1,0:T(8,128)(2,1)} %get-tuple-element.156.refs_0_.refs_5_, ...), custom_call_target="tpu_custom_call" | custom-call | flops 1000000000 | bytes 9486336 | tf_op jit(solution)/shard_map/mlp/pallas_call | solution.py:40
  165.5 13.0 %mlp_post.1 = (bf16[256,1024]{1,0:T(8,128)(2,1)}, bf16[256,1024]{1,0:T(8,128)(2,1)}, bf16[256,1024]{1,0:T(8,128)(2,1)}, bf16[256,1024]{1,0:T(8,128)(2,1)}, bf16[35,16,128]{2,1,0:T(8,128)(2,1)}) custom-call(s32[4]{0:T(128)} %iota_xor_fusion.order, s32[1]{0:T(128)} %copy.42.pick, bf16[16,1024]{1,0:T(8,128)(2,1)} %get-tuple-element.212.down_in, ...), custom_call_target="tpu_custom_call" | custom-call | flops 1000000000 | bytes 11937300 | tf_op jit(solution)/shard_map/mlp_post/pallas_call | solution.py:40
  181.2 5.3 %out_back.1 = (f32[256,1024]{1,0:T(8,128)}, bf16[256,256]{1,0:T(8,128)(2,1)}, bf16[256,256]{1,0:T(8,128)(2,1)}, bf16[256,256]{1,0:T(8,128)(2,1)}, bf16[256,256]{...) custom-call(s32[4]{0:T(128)} %iota_xor_fusion.order, f32[256,1024]{1,0:T(8,128)} %get-tuple-element.149.middle, ...), custom_call_target="tpu_custom_call" | custom-call | flops 1000000000 | bytes 7487504 | tf_op jit(solution)/shard_map/out_back/pallas_call | solution.py:40
  186.8 4.2 %collective-permute-done.44.refs_3_ = bf16[16,16,128]{2,1,0:T(8,128)(2,1)S(1)} collective-permute-done((bf16[16,16,128]{2,1,0:T(8,128)(2,1)}, bf16[16,16,128]{2,1,0:T(8,128)(2,1)S(1)}, u32[]{:S(2)}, u32[]{:S(2)}) %collective-permute-start.44) | collective-permute-done | bytes 65568 | tf_op jit(solution)/shard_map/ppermute | solution.py:452
  195.5 4.5 %collective-permute-done.35.refs_2_ = bf16[256,256]{1,0:T(8,128)(2,1)S(1)} collective-permute-done((bf16[256,256]{1,0:T(8,128)(2,1)S(1)}, bf16[256,256]{1,0:T(8,128)(2,1)S(1)}, u32[]{:S(2)}, u32[]{:S(2)}) %collective-permute-start.35) | collective-permute-done | bytes 131104 | tf_op jit(solution)/shard_map/ppermute | solution.py:452
  202.5 22.4 %attend_back.1 = (bf16[256,1024]{1,0:T(8,128)(2,1)}, bf16[256,1024]{1,0:T(8,128)(2,1)}, bf16[256,1024]{1,0:T(8,128)(2,1)}, bf16[256,1024]{1,0:T(8,128)(2,1)}, bf16[3,1024,256]{2,1,0:T(8,128)(2,1)}) custom-call(s32[4]{0:T(128)} %iota_xor_fusion.order, bf16[1024,256]{1,0:T(8,128)(2,1)} %get-tuple-element.124.query, bf16[1024,256]{1,0:T(8,128)(2,1)} %get-tuple-element.125.key, ...), custom_call_target="tpu_custom_call" | custom-call | flops 1000000000 | bytes 8413200 | tf_op jit(solution)/shard_map/attend_back/pallas_call | solution.py:40
  225.2 4.5 %qkv_terms.1.refs_0_ = bf16[15,16,128]{2,1,0:T(8,128)(2,1)} custom-call(s32[1]{0:T(128)} %copy.42.pick, bf16[1024,1024]{1,0:T(8,128)(2,1)} %get-tuple-element.116.norm, bf16[3,1024,256]{2,1,0:T(8,128)(2,1)} %get-tuple-element.176.grad_qkv, bf16[16,1024]{1,0:T(8,128)(2,1)} %dynamic-slice_bitcast_fusion.2.down, bf16[3,16,256]{2,1,0:T(8,128)(2,1)} %pad_maximum_fusion.3.ups), custom_call_target="tpu_custom_call" | custom-call | flops 1000000000 | bytes 3788804 | tf_op jit(solution)/shard_map/qkv_terms/pallas_call | solution.py:40
  230.2 3.9 %collective-permute-done.38.refs_1_ = bf16[15,16,128]{2,1,0:T(8,128)(2,1)S(1)} collective-permute-done((bf16[15,16,128]{2,1,0:T(8,128)(2,1)}, bf16[15,16,128]{2,1,0:T(8,128)(2,1)S(1)}, u32[]{:S(2)}, u32[]{:S(2)}) %collective-permute-start.38) | collective-permute-done | bytes 61472 | tf_op jit(solution)/shard_map/ppermute | solution.py:452
  238.3 4.2 %collective-permute-done.39.refs_1_ = bf16[22,16,128]{2,1,0:T(8,128)(2,1)S(1)} collective-permute-done((bf16[22,16,128]{2,1,0:T(8,128)(2,1)}, bf16[22,16,128]{2,1,0:T(8,128)(2,1)S(1)}, u32[]{:S(2)}, u32[]{:S(2)}) %collective-permute-start.39) | collective-permute-done | bytes 90144 | tf_op jit(solution)/shard_map/ppermute | solution.py:511
  242.5 2.4 collective-permute-start.40
  245.3 2.5 collective-permute-done.40.refs_3_
  250.7 5.1 %collective-permute-done.29 = bf16[256,1024]{1,0:T(8,128)(2,1)S(1)} collective-permute-done((bf16[256,1024]{1,0:T(8,128)(2,1)}, bf16[256,1024]{1,0:T(8,128)(2,1)S(1)}, u32[]{:S(2)}, u32[]{:S(2)}) %collective-permute-start.29) | collective-permute-done | bytes 524320 | tf_op jit(solution)/shard_map/ppermute | solution.py:452
  260.8 7.3 %spread.2 = (f32[8,16,5248]{2,1,0:T(8,128)}, f32[8,16,2624]{2,1,0:T(8,128)}, f32[8,16,1024]{2,1,0:T(8,128)}, f32[8,16,1024]{2,1,0:T(8,128)}, f32[8,16,1024]{2,1,0:T(8,128)}, /*index=5*/f32[8,16,1024]{2,1,0:T(8,128)}) custom-call(s32[1]{0:T(128)} %bitcast.17.core, bf16[8,70,16,128]{3,2,1,0:T(8,128)(2,1)} %bitcast.34, bf16[8,70,16,128]{3,2,1,0:T(8,128)(2,1)} %copy-done.3), custom_call_target="tpu_custom_call" | custom-call | flops 1000000000 | bytes 10715140 | tf_op jit(solution)/shard_map/spread/pallas_call | solution.py:40
  270.3 3.5 %last.1 = bf16[256,1024]{1,0:T(8,128)(2,1)} custom-call(bf16[256,1024]{1,0:T(8,128)(2,1)} %bitcast.39, f32[256,1024]{1,0:T(8,128)} %get-tuple-element.189.grad_mid, f32[2,1024]{1,0:T(2,128)} %get-tuple-element.111.gain, bf16[256,1024]{1,0:T(8,128)(2,1)} %get-tuple-element.190.refs_0_, bf16[256,1024]{1,0:T(8,128)(2,1)} %collective-permute-done.51.refs_1_, ...), custom_call_target="tpu_custom_call" | custom-call | flops 1000000000 | bytes 3678208 | tf_op jit(solution)/shard_map/last/pallas_call | solution.py:40
  277.1 2.2 fusion.1
  280.4 4.0 %spread.3 = (f32[8,16,3072]{2,1,0:T(8,128)}, f32[8,16,1024]{2,1,0:T(8,128)}) custom-call(s32[1]{0:T(128)} %bitcast.17.core, bf16[8,22,16,128]{3,2,1,0:T(8,128)(2,1)} %stack.21.mine, bf16[8,22,16,128]{3,2,1,0:T(8,128)(2,1)} %copy-done.43), custom_call_target="tpu_custom_call" | custom-call | flops 1000000000 | bytes 3538948 | tf_op jit(solution)/shard_map/spread/pallas_call | solution.py:40
  (254 shorter events, 78.7 us)
Async XLA Ops:
  7.2 34.9 %all-gather.7.cloned.1.call-start = ((), (), s32[]{:S(2)}) async-start(), calls=%async_computation | async-start | bytes 2785280 | tf_op jit(solution)/shard_map/all_gather | solution.py:585
  10.6 128.3 %all-gather.9.cloned.1.call-start = ((), (), s32[]{:S(2)}) async-start(), calls=%async_computation.1 | async-start | bytes 2621440 | tf_op jit(solution)/shard_map/all_gather | solution.py:593
  11.4 13.3 %collective-permute-start.1 = (bf16[256,128]{1,0:T(8,128)(2,1)S(1)}, bf16[256,128]{1,0:T(8,128)(2,1)S(1)}, u32[]{:S(2)}, u32[]{:S(2)}) collective-permute-start(bf16[256,128]{1,0:T(8,128)(2,1)S(1)} %constant_dynamic-slice_fusion.7), channel_id=1, source_target_pairs={{0,1},{1,5},{2,9},{3,13},{4,17},{5,21},{6,25},{7,29},{8,0},{9,4},{... | collective-permute-start | bytes 196616 | tf_op jit(solution)/shard_map/ppermute | solution.py:606
  39.4 7.9 %collective-permute-start.6 = (bf16[256,512]{1,0:T(8,128)(2,1)S(1)}, bf16[256,512]{1,0:T(8,128)(2,1)S(1)}, u32[]{:S(2)}, u32[]{:S(2)}) collective-permute-start(bf16[256,512]{1,0:T(8,128)(2,1)S(1)} %collective-permute-done.3.refs_3_), channel_id=1, source_target_pairs={{0,8},{8,16},{16,24},{24,28},{28,20},{20,12},{12,4},{4,0},{1,9},{9... | collective-permute-start | bytes 786440 | tf_op jit(solution)/shard_map/ppermute | solution.py:511
  41.4 13.5 %collective-permute-start.10 = (bf16[656,256]{1,0:T(8,128)(2,1)S(1)}, bf16[656,256]{1,0:T(8,128)(2,1)S(1)}, u32[]{:S(2)}, u32[]{:S(2)}) collective-permute-start(bf16[656,256]{1,0:T(8,128)(2,1)S(1)} %bitcast.44), channel_id=1, source_target_pairs={{0,0},{1,4},{2,8},{3,12},{4,1},{5,5},{6,9},{7,13},{8,2},{9,6},{10,... | collective-permute-start | bytes 1007624 | tf_op jit(solution)/shard_map/ppermute | solution.py:616
  42.2 207.5 %all-gather.11.cloned.1.call-start = ((), (), s32[]{:S(2)}) async-start(), calls=%async_computation.2 | async-start | bytes 2580480 | tf_op jit(solution)/shard_map/all_gather | solution.py:828
  47.5 9.5 %collective-permute-start.8 = (bf16[128,512]{1,0:T(8,128)(2,1)S(1)}, bf16[128,512]{1,0:T(8,128)(2,1)S(1)}, u32[]{:S(2)}, u32[]{:S(2)}) collective-permute-start(bf16[128,512]{1,0:T(8,128)(2,1)S(1)} %slice.18), channel_id=1, source_target_pairs={{0,8},{8,16},{16,24},{24,28},{28,20},{20,12},{12,4},{4,0},{1,9},{9... | collective-permute-start | bytes 393224 | tf_op jit(solution)/shard_map/ppermute | solution.py:511
  59.6 16.4 %collective-permute-start.11 = (bf16[656,384]{1,0:T(8,128)(2,1)S(1)}, bf16[656,384]{1,0:T(8,128)(2,1)S(1)}, u32[]{:S(2)}, u32[]{:S(2)}) collective-permute-start(bf16[656,384]{1,0:T(8,128)(2,1)S(1)} %pad_maximum_fusion.1.refs_0_), channel_id=1, source_target_pairs={{0,8},{8,16},{16,24},{24,28},{28,20},{20,12},{12,4},{4,0},{1,9},{9... | collective-permute-start | bytes 1511432 | tf_op jit(solution)/shard_map/ppermute | solution.py:511
  60.9 15.1 %collective-permute-start.12 = (bf16[656,384]{1,0:T(8,128)(2,1)S(1)}, bf16[656,384]{1,0:T(8,128)(2,1)}, u32[]{:S(2)}, u32[]{:S(2)}) collective-permute-start(bf16[656,384]{1,0:T(8,128)(2,1)S(1)} %pad_maximum_fusion.1.refs_0_), channel_id=1, source_target_pairs={{8,0},{16,8},{24,16},{28,24},{20,28},{12,20},{4,12},{0,4},{9,1},{1... | collective-permute-start | bytes 1511432 | tf_op jit(solution)/shard_map/ppermute | solution.py:512
  74.1 20.6 %collective-permute-start.15 = (bf16[256,1024]{1,0:T(8,128)(2,1)}, bf16[256,1024]{1,0:T(8,128)(2,1)S(1)}, u32[]{:S(2)}, u32[]{:S(2)}) collective-permute-start(bf16[256,1024]{1,0:T(8,128)(2,1)} %get-tuple-element.146.refs_4_.refs_7_), channel_id=1, source_target_pairs={{0,1},{1,0},{2,3},{3,2},{4,5},{5,4},{6,7},{7,6},{8,9},{9,8},{10,11... | collective-permute-start | bytes 1572872 | tf_op jit(solution)/shard_map/ppermute | solution.py:452
  74.2 20.6 %collective-permute-start.16 = (bf16[256,1024]{1,0:T(8,128)(2,1)}, bf16[256,1024]{1,0:T(8,128)(2,1)S(1)}, u32[]{:S(2)}, u32[]{:S(2)}) collective-permute-start(bf16[256,1024]{1,0:T(8,128)(2,1)} %get-tuple-element.146.refs_4_.refs_7_), channel_id=1, source_target_pairs={{0,2},{1,3},{2,0},{3,1},{4,6},{5,7},{6,4},{7,5},{8,10},{9,11},{10,... | collective-permute-start | bytes 1572872 | tf_op jit(solution)/shard_map/ppermute | solution.py:452
  76.0 18.8 %collective-permute-start.13 = (bf16[656,384]{1,0:T(8,128)(2,1)S(1)}, bf16[656,384]{1,0:T(8,128)(2,1)}, u32[]{:S(2)}, u32[]{:S(2)}) collective-permute-start(bf16[656,384]{1,0:T(8,128)(2,1)S(1)} %collective-permute-done.11.refs_1_), channel_id=1, source_target_pairs={{0,8},{8,16},{16,24},{24,28},{28,20},{20,12},{12,4},{4,0},{1,9},{9... | collective-permute-start | bytes 1511432 | tf_op jit(solution)/shard_map/ppermute | solution.py:511
  78.0 16.8 %collective-permute-start.14 = (bf16[656,384]{1,0:T(8,128)(2,1)}, bf16[656,384]{1,0:T(8,128)(2,1)}, u32[]{:S(2)}, u32[]{:S(2)}) collective-permute-start(bf16[656,384]{1,0:T(8,128)(2,1)} %collective-permute-done.12.refs_2_), channel_id=1, source_target_pairs={{8,0},{16,8},{24,16},{28,24},{20,28},{12,20},{4,12},{0,4},{9,1},{1... | collective-permute-start | bytes 1511432 | tf_op jit(solution)/shard_map/ppermute | solution.py:512
  94.8 15.9 %collective-permute-start.22 = (bf16[256,1024]{1,0:T(8,128)(2,1)S(1)}, bf16[256,1024]{1,0:T(8,128)(2,1)S(1)}, u32[]{:S(2)}, u32[]{:S(2)}) collective-permute-start(bf16[256,1024]{1,0:T(8,128)(2,1)S(1)} %collective-permute-done.16.refs_6_.refs_9_), channel_id=1, source_target_pairs={{0,1},{1,0},{2,3},{3,2},{4,5},{5,4},{6,7},{7,6},{8,9},{9,8},{10,11... | collective-permute-start | bytes 1572872 | tf_op jit(solution)/shard_map/ppermute | solution.py:452
  94.9 14.1 %collective-permute-start.17 = (bf16[656,384]{1,0:T(8,128)(2,1)}, bf16[656,384]{1,0:T(8,128)(2,1)S(1)}, u32[]{:S(2)}, u32[]{:S(2)}) collective-permute-start(bf16[656,384]{1,0:T(8,128)(2,1)} %collective-permute-done.13.refs_3_), channel_id=1, source_target_pairs={{0,8},{8,16},{16,24},{24,28},{28,20},{20,12},{12,4},{4,0},{1,9},{9... | collective-permute-start | bytes 1511432 | tf_op jit(solution)/shard_map/ppermute | solution.py:511
  96.9 13.8 %collective-permute-start.18 = (bf16[656,384]{1,0:T(8,128)(2,1)}, bf16[656,384]{1,0:T(8,128)(2,1)S(1)}, u32[]{:S(2)}, u32[]{:S(2)}) collective-permute-start(bf16[656,384]{1,0:T(8,128)(2,1)} %collective-permute-done.14.refs_4_), channel_id=1, source_target_pairs={{8,0},{16,8},{24,16},{28,24},{20,28},{12,20},{4,12},{0,4},{9,1},{1... | collective-permute-start | bytes 1511432 | tf_op jit(solution)/shard_map/ppermute | solution.py:512
  115.7 13.4 %collective-permute-start.26 = (bf16[256,1024]{1,0:T(8,128)(2,1)}, bf16[256,1024]{1,0:T(8,128)(2,1)S(1)}, u32[]{:S(2)}, u32[]{:S(2)}) collective-permute-start(bf16[256,1024]{1,0:T(8,128)(2,1)} %get-tuple-element.156.refs_0_.refs_5_), channel_id=1, source_target_pairs={{0,2},{1,3},{2,0},{3,1},{4,6},{5,7},{6,4},{7,5},{8,10},{9,11},{10,... | collective-permute-start | bytes 1572872 | tf_op jit(solution)/shard_map/ppermute | solution.py:452
  129.1 18.5 %collective-permute-start.27 = (bf16[256,1024]{1,0:T(8,128)(2,1)S(1)}, bf16[256,1024]{1,0:T(8,128)(2,1)S(1)}, u32[]{:S(2)}, u32[]{:S(2)}) collective-permute-start(bf16[256,1024]{1,0:T(8,128)(2,1)S(1)} %collective-permute-done.26.refs_0_.refs_7_), channel_id=1, source_target_pairs={{0,1},{1,0},{2,3},{3,2},{4,5},{5,4},{6,7},{7,6},{8,9},{9,8},{10,11... | collective-permute-start | bytes 1572872 | tf_op jit(solution)/shard_map/ppermute | solution.py:452
  130.0 8.9 %collective-permute-start.24 = (bf16[336,384]{1,0:T(8,128)(2,1)S(1)}, bf16[336,384]{1,0:T(8,128)(2,1)S(1)}, u32[]{:S(2)}, u32[]{:S(2)}) collective-permute-start(bf16[336,384]{1,0:T(8,128)(2,1)S(1)} %slice.21), channel_id=1, source_target_pairs={{8,0},{16,8},{24,16},{28,24},{20,28},{12,20},{4,12},{0,4},{9,1},{1... | collective-permute-start | bytes 774152 | tf_op jit(solution)/shard_map/ppermute | solution.py:512
  130.6 8.3 %collective-permute-start.23 = (bf16[320,384]{1,0:T(8,128)(2,1)S(1)}, bf16[320,384]{1,0:T(8,128)(2,1)S(1)}, u32[]{:S(2)}, u32[]{:S(2)}) collective-permute-start(bf16[320,384]{1,0:T(8,128)(2,1)S(1)} %slice.20), channel_id=1, source_target_pairs={{0,8},{8,16},{16,24},{24,28},{28,20},{20,12},{12,4},{4,0},{1,9},{9... | collective-permute-start | bytes 737288 | tf_op jit(solution)/shard_map/ppermute | solution.py:511
  135.1 21.0 %collective-permute-start.25 = (bf16[256,1024]{1,0:T(8,128)(2,1)}, bf16[256,1024]{1,0:T(8,128)(2,1)S(1)}, u32[]{:S(2)}, u32[]{:S(2)}) collective-permute-start(bf16[256,1024]{1,0:T(8,128)(2,1)} %get-tuple-element.156.refs_0_.refs_5_), channel_id=1, source_target_pairs={{0,1},{1,0},{2,3},{3,2},{4,5},{5,4},{6,7},{7,6},{8,9},{9,8},{10,11... | collective-permute-start | bytes 1572872 | tf_op jit(solution)/shard_map/ppermute | solution.py:452
  156.0 8.9 %collective-permute-start.32 = (bf16[256,1024]{1,0:T(8,128)(2,1)}, bf16[256,1024]{1,0:T(8,128)(2,1)S(1)}, u32[]{:S(2)}, u32[]{:S(2)}) collective-permute-start(bf16[256,1024]{1,0:T(8,128)(2,1)} %get-tuple-element.171), channel_id=1, source_target_pairs={{0,1},{1,0},{2,3},{3,2},{4,5},{5,4},{6,7},{7,6},{8,9},{9,8},{10,11... | collective-permute-start | bytes 1572872 | tf_op jit(solution)/shard_map/ppermute | solution.py:452
  164.4 15.8 %collective-permute-start.31 = (bf16[256,1024]{1,0:T(8,128)(2,1)}, bf16[256,1024]{1,0:T(8,128)(2,1)S(1)}, u32[]{:S(2)}, u32[]{:S(2)}) collective-permute-start(bf16[256,1024]{1,0:T(8,128)(2,1)} %get-tuple-element.169), channel_id=1, source_target_pairs={{0,1},{1,0},{2,3},{3,2},{4,5},{5,4},{6,7},{7,6},{8,9},{9,8},{10,11... | collective-permute-start | bytes 1572872 | tf_op jit(solution)/shard_map/ppermute | solution.py:452
  165.2 15.1 %collective-permute-start.33 = (bf16[256,1024]{1,0:T(8,128)(2,1)S(1)}, bf16[256,1024]{1,0:T(8,128)(2,1)S(1)}, u32[]{:S(2)}, u32[]{:S(2)}) collective-permute-start(bf16[256,1024]{1,0:T(8,128)(2,1)S(1)} %add_convert_fusion.1), channel_id=1, source_target_pairs={{0,2},{1,3},{2,0},{3,1},{4,6},{5,7},{6,4},{7,5},{8,10},{9,11},{10,... | collective-permute-start | bytes 1572872 | tf_op jit(solution)/shard_map/ppermute | solution.py:452
  178.5 8.3 %collective-permute-start.43 = (bf16[35,16,128]{2,1,0:T(8,128)(2,1)}, bf16[35,16,128]{2,1,0:T(8,128)(2,1)S(1)}, u32[]{:S(2)}, u32[]{:S(2)}) collective-permute-start(bf16[35,16,128]{2,1,0:T(8,128)(2,1)} %get-tuple-element.180.refs_0_), channel_id=1, source_target_pairs={{0,2},{1,3},{2,0},{3,1},{4,6},{5,7},{6,4},{7,5},{8,10},{9,11},{10,... | collective-permute-start | bytes 430088 | tf_op jit(solution)/shard_map/ppermute | solution.py:452
  234.1 15.6 %collective-permute-start.45 = (bf16[256,1024]{1,0:T(8,128)(2,1)S(1)}, bf16[256,1024]{1,0:T(8,128)(2,1)}, u32[]{:S(2)}, u32[]{:S(2)}) collective-permute-start(bf16[256,1024]{1,0:T(8,128)(2,1)S(1)} %add_convert_fusion), channel_id=1, source_target_pairs={{0,2},{1,3},{2,0},{3,1},{4,6},{5,7},{6,4},{7,5},{8,10},{9,11},{10,... | collective-permute-start | bytes 1572872 | tf_op jit(solution)/shard_map/ppermute | solution.py:452
  249.7 9.8 %collective-permute-start.48 = (bf16[8,70,16,128]{3,2,1,0:T(8,128)(2,1)}, bf16[8,70,16,128]{3,2,1,0:T(8,128)(2,1)S(1)}, u32[]{:S(2)}, u32[]{:S(2)}) collective-permute-start(bf16[8,70,16,128]{3,2,1,0:T(8,128)(2,1)} %bitcast.33), channel_id=1, source_target_pairs={{0,1},{1,0},{2,3},{3,2},{4,5},{5,4},{6,7},{7,6},{8,9},{9,8},{10,11... | collective-permute-start | bytes 6881288 | tf_op jit(solution)/shard_map/ppermute | solution.py:452
  250.2 20.1 %collective-permute-start.51 = (bf16[256,1024]{1,0:T(8,128)(2,1)}, bf16[256,1024]{1,0:T(8,128)(2,1)}, u32[]{:S(2)}, u32[]{:S(2)}) collective-permute-start(bf16[256,1024]{1,0:T(8,128)(2,1)} %get-tuple-element.191), channel_id=1, source_target_pairs={{0,1},{1,0},{2,3},{3,2},{4,5},{5,4},{6,7},{7,6},{8,9},{9,8},{10,11... | collective-permute-start | bytes 1572872 | tf_op jit(solution)/shard_map/ppermute | solution.py:452
  250.3 26.9 %collective-permute-start.28 = (bf16[256,1024]{1,0:T(8,128)(2,1)}, bf16[256,1024]{1,0:T(8,128)(2,1)}, u32[]{:S(2)}, u32[]{:S(2)}) collective-permute-start(bf16[256,1024]{1,0:T(8,128)(2,1)} %get-tuple-element.162), channel_id=1, source_target_pairs={{0,1},{1,0},{2,3},{3,2},{4,5},{5,4},{6,7},{7,6},{8,9},{9,8},{10,11... | collective-permute-start | bytes 1572872 | tf_op jit(solution)/shard_map/ppermute | solution.py:452
  256.0 21.1 %collective-permute-start.30 = (bf16[256,1024]{1,0:T(8,128)(2,1)S(1)}, bf16[256,1024]{1,0:T(8,128)(2,1)S(1)}, u32[]{:S(2)}, u32[]{:S(2)}) collective-permute-start(bf16[256,1024]{1,0:T(8,128)(2,1)S(1)} %add_convert_fusion.3), channel_id=1, source_target_pairs={{0,2},{1,3},{2,0},{3,1},{4,6},{5,7},{6,4},{7,5},{8,10},{9,11},{10,... | collective-permute-start | bytes 1572872 | tf_op jit(solution)/shard_map/ppermute | solution.py:452
  257.4 10.7 %collective-permute-start.46 = (bf16[22,16,128]{2,1,0:T(8,128)(2,1)}, bf16[22,16,128]{2,1,0:T(8,128)(2,1)S(1)}, u32[]{:S(2)}, u32[]{:S(2)}) collective-permute-start(bf16[22,16,128]{2,1,0:T(8,128)(2,1)} %collective-permute-done.40.refs_3_), channel_id=1, source_target_pairs={{0,8},{8,16},{16,24},{24,28},{28,20},{20,12},{12,4},{4,0},{1,9},{9... | collective-permute-start | bytes 270344 | tf_op jit(solution)/shard_map/ppermute | solution.py:511
  259.4 8.7 %collective-permute-start.47 = (bf16[22,16,128]{2,1,0:T(8,128)(2,1)}, bf16[22,16,128]{2,1,0:T(8,128)(2,1)S(1)}, u32[]{:S(2)}, u32[]{:S(2)}) collective-permute-start(bf16[22,16,128]{2,1,0:T(8,128)(2,1)} %collective-permute-done.42.refs_4_), channel_id=1, source_target_pairs={{8,0},{16,8},{24,16},{28,24},{20,28},{12,20},{4,12},{0,4},{9,1},{1... | collective-permute-start | bytes 270344 | tf_op jit(solution)/shard_map/ppermute | solution.py:512
  (80 other events, 805.1 us)
Sparse Core Ops, SparseCore 0:
  10.7 26.0 all-gather.6
  42.3 26.5 all-gather.8
  193.6 52.2 all-gather.10

commit v2 on v1

v2 whole, which is shorter than its diff:
```python
import functools

import jax
import jax.numpy as jnp
from jax import lax
from jax.experimental import pallas as pl
from jax.experimental.pallas import tpu as pltpu
from jax.sharding import PartitionSpec as P

HEADS = 16
HEAD_DIM = 64
EPS = 1e-05
THETA = 160000.0
F32 = jnp.float32
BF16 = jnp.bfloat16
MIB = 1024 * 1024
RING = (0, 2, 4, 6, 7, 5, 3, 1)


def nn(a, b):
    return lax.dot_general(a, b, (((1,), (0,)), ((), ())), preferred_element_type=F32)


def nt(a, b):
    return lax.dot_general(a, b, (((1,), (1,)), ((), ())), preferred_element_type=F32)


def tn(a, b):
    return lax.dot_general(a, b, (((0,), (0,)), ((), ())), preferred_element_type=F32)


def shape(dims, dtype):
    return jax.ShapeDtypeStruct(tuple(dims), dtype)


PIECE = 256 * 1024


def cuts(dims, item):
    size = item
    for n in dims:
        size *= n
    if size <= PIECE * 3 // 2 or len(dims) == 1:
        return [()]
    if len(dims) == 2:
        step = max(dims[0] * PIECE // size // 16 * 16, 16)
        return [(pl.ds(n, min(step, dims[0] - n)),) for n in range(0, dims[0], step)]
    return [(n,) + rest for n in range(dims[0]) for rest in cuts(dims[1:], item)]


def start_copies(source, target, semaphore):
    for at in cuts(target.shape, target.dtype.itemsize):
        one, two = (source.at[at], target.at[at]) if at else (source, target)
        pltpu.make_async_copy(one, two, semaphore).start()
    return pltpu.make_async_copy(source, target, semaphore)


class Late:
    def __init__(self, source, target, semaphore):
        self.target, self.there = target, False
        self.copy = start_copies(source, target, semaphore)

    def get(self):
        if not self.there:
            self.copy.wait()
            self.there = True
        return self.target


class Here:
    def __init__(self, ref):
        self.ref = ref

    def get(self):
        return self.ref

    def send(self):
        pass


class Early:
    def __init__(self, target, source, semaphore):
        self.ref, self.sent = source, False
        self.ends = (source, target, semaphore)

    def send(self):
        if not self.sent:
            self.copy = start_copies(*self.ends)
            self.sent = True


class Pick:
    def __init__(self, table, pick, start=None, size=None):
        self.table, self.pick = table, pick
        self.start, self.size = start, table.shape[2] if size is None else size


def call(kernel, out_shape, args, scratch=(), smem=(), early=(), name=None):
    picks = {n: a for n, a in enumerate(args) if isinstance(a, Pick)}
    operands = [a.table if isinstance(a, Pick) else a for a in args]
    chosen = [next(iter(picks.values())).pick] if picks else []
    late = list(picks)
    buffers = [
        pltpu.VMEM((args[n].table.shape[1], args[n].size), args[n].table.dtype) for n in late
    ]
    buffers += [pltpu.VMEM(out_shape[n].shape, out_shape[n].dtype) for n in early]
    first_in = len(chosen)

    def body(*refs):
        pick, refs = refs[:first_in], refs[first_in:]
        ins, refs = list(refs[: len(args)]), refs[len(args) :]
        outs, refs = list(refs[: len(out_shape)]), refs[len(out_shape) :]
        own, refs = refs[: len(scratch)], refs[len(scratch) :]
        semaphores = refs[-1]
        for at, n in enumerate(late):
            entry = picks[n]
            columns = slice(None) if entry.start is None else pl.ds(entry.start(), entry.size)
            source = ins[n].at[pick[0][0], :, columns]
            ins[n] = Late(source, refs[at], semaphores.at[at])
        for n in range(len(args)):
            if n not in picks and n not in smem:
                ins[n] = Here(ins[n])
        for at, n in enumerate(early, len(late)):
            outs[n] = Early(outs[n], refs[at], semaphores.at[at])
        kernel(*ins, *outs, *own)
        for n in late:
            ins[n].get()
        for n in early:
            outs[n].send()
            outs[n].copy.wait()

    spaces = [pltpu.SMEM] * first_in + [
        pltpu.SMEM if n in smem else pl.ANY if n in picks else pltpu.VMEM
        for n in range(len(args))
    ]
    return pl.pallas_call(
        body,
        out_shape=list(out_shape),
        in_specs=[pl.BlockSpec(memory_space=space) for space in spaces],
        out_specs=[
            pl.BlockSpec(memory_space=pl.ANY if n in early else pltpu.VMEM)
            for n in range(len(out_shape))
        ],
        scratch_shapes=list(scratch)
        + buffers
        + [pltpu.SemaphoreType.DMA((max(len(late) + len(early), 1),))],
        compiler_params=pltpu.CompilerParams(vmem_limit_bytes=60 * MIB),
        cost_estimate=pl.CostEstimate(flops=1, bytes_accessed=1, transcendentals=0),
        name=name,
    )(*chosen, *operands)


def owner(n, direct):
    return jnp.bitwise_xor(lax.axis_index("tok"), n) if direct else n


def rows_of(n, size):
    if isinstance(n, int):
        return pl.ds(n * size, size)
    return pl.ds(pl.multiple_of(n * size, size), size)


def came_from(n):
    own, size = lax.axis_index("seq"), len(RING)
    place = jnp.where(lax.rem(own, 2) == 0, own // 2, size - 1 - own // 2)
    shift = (0, -1, 1, -2, 2, -3, 3, -4, 4)[n]
    came = lax.rem(place + shift + size, size)
    return jnp.where(came < size // 2, 2 * came, 2 * (size - 1 - came) + 1)


def to_slot(refs, index, value):
    for n, ref in enumerate(refs):

        @pl.when(index == n)
        def _(ref=ref):
            ref[...] = value


def normalized(rows):
    mean = jnp.mean(rows, axis=-1, keepdims=True)
    centered = rows - mean
    scale = lax.rsqrt(jnp.mean(centered * centered, axis=-1, keepdims=True) + EPS)
    return centered * scale, scale


def norm_back(rows, gain, grad):
    unit, scale = normalized(rows)
    weighted = grad * gain
    first = jnp.mean(weighted, axis=-1, keepdims=True)
    second = jnp.mean(weighted * unit, axis=-1, keepdims=True)
    return (weighted - first - unit * second) * scale


def swapped(rows):
    width = rows.shape[1]
    if width % 128:
        half = HEAD_DIM // 2
        parts = []
        for start in range(0, width, HEAD_DIM):
            parts += [rows[:, start + half : start + HEAD_DIM], rows[:, start : start + half]]
        return jnp.concatenate(parts, axis=1)
    lane = lax.broadcasted_iota(jnp.int32, rows.shape, 1)
    ahead = pltpu.roll(rows, width - HEAD_DIM // 2, 1)
    behind = pltpu.roll(rows, HEAD_DIM // 2, 1)
    return jnp.where(lane % HEAD_DIM < HEAD_DIM // 2, ahead, behind)


def widened(table, width):
    if width <= table.shape[1]:
        return table[:, :width]
    return jnp.concatenate([table] * (width // table.shape[1]), axis=1)


def head_part(rows, head):
    lane = lax.broadcasted_iota(jnp.int32, rows.shape, 1)
    return jnp.where(lane // HEAD_DIM == head, rows, jnp.zeros_like(rows))


def chunked(ref, base, value):
    count = -(-value.shape[1] // 128)
    for n in range(count):
        part = value[:, n * 128 : (n + 1) * 128].astype(ref.dtype)
        if part.shape[1] < 128:
            ref[base + n] = jnp.zeros(ref.shape[1:], ref.dtype)
            ref[base + n, :, : part.shape[1]] = part
        else:
            ref[base + n] = part
    return base + count


def halves(keep, at, send, first, value):
    core = lax.rem(lax.axis_index("tok"), 2)
    half = value.shape[1] // 256
    for n in range(2 * half):
        part = value[:, n * 128 : (n + 1) * 128].astype(keep.dtype)

        @pl.when(core == n // half)
        def _(part=part, n=n):
            keep[at + n % half] = part

        @pl.when(core != n // half)
        def _(part=part, n=n):
            send[first + n % half] = part


def labelled(ref, at, pick):
    ref[at] = jnp.full(ref.shape[1:], pick[0].astype(F32)).astype(ref.dtype)


def document_range(block, rows, seg_scalar, seg_row):
    first = seg_scalar[0, block * rows].astype(F32)
    last = seg_scalar[0, block * rows + rows - 1].astype(F32)
    below = jnp.sum(jnp.where(seg_row < first, 1.0, 0.0)).astype(jnp.int32)
    upto = jnp.sum(jnp.where(seg_row <= last, 1.0, 0.0)).astype(jnp.int32)
    return below // rows, (upto + rows - 1) // rows


def prepare_kernel(tokens, gain_one, gain_two, weight, token_out, double, single):
    weight, odd = weight.get(), lax.rem(lax.axis_index("seq"), 2)
    unit = single.shape[1]

    @pl.when(odd == 0)
    def _():
        double[...] = weight[:, : 2 * unit]
        single[...] = weight[:, 2 * unit :]

    @pl.when(odd == 1)
    def _():
        double[...] = weight[:, unit:]
        single[...] = weight[:, :unit]

    tokens = tokens.get()
    rows, part = tokens.shape[0], gain_one.get().shape[0]
    token_out[:rows] = tokens[...]
    token_out[rows:] = jnp.zeros((16, tokens.shape[1]), BF16)
    both = [gain.get()[...].astype(F32).reshape(1, part) for gain in (gain_one, gain_two)]
    token_out[rows : rows + 2, :part] = jnp.concatenate(both, axis=0).astype(BF16)


def adapters_kernel(tok, *refs):
    tables, outs = refs[:8], refs[8:]
    down_one, up_one, down_attn, up_attn, down_two, up_two, down_last, up_last = outs
    for n in (1, 5, 6):
        tables[n].get()
    for table, out in ((0, down_one), (2, down_attn), (3, up_attn), (4, down_two), (7, up_last)):
        out[...] = tables[table].get()[...]
    own = lax.axis_index("tok")
    for n in range(tok):

        @pl.when(own == n)
        def _(n=n):
            down_last[...] = tables[6].get()[:, columns_of(n, 0, down_last.shape[1], tok)]
            for kind in range(3):
                size = up_one.shape[2]
                up_one[kind] = tables[1].get()[:, columns_of(n, kind, size, tok)]
            for kind in range(2):
                size = up_two.shape[2]
                up_two[kind] = tables[5].get()[:, columns_of(n, kind, size, tok)]


def columns_of(own, group, size, tok):
    start = (group * tok + own) * size
    return slice(start, start + size)


def qkv_kernel(pieces, kinds, tokens, down, ups, cosine, sine, *refs):
    weights, refs = refs[:pieces], refs[pieces:]
    norm, gain, query, key, value, whole = refs[:6]
    width = query.shape[1]
    if pieces == 1:
        whole[...] = weights[0].get()[...]
    else:
        out_weight = refs[6]
        unit = width // 2
        own = lax.axis_index("tok")
        first = 0
        for n in range(pieces):
            piece = weights[n].get()
            depth = piece.shape[0]
            spot = came_from(n)
            half, part = spot // 4, lax.rem(spot, 4)
            down_at = pl.ds(pl.multiple_of(part * width + first, depth), depth)
            double, single = kinds[3 * own + half], kinds[3 * own + 2]
            whole[double, down_at, :] = piece[:, :width]
            across = pl.ds(pl.multiple_of(half * unit, unit), unit)
            whole[single, down_at, across] = piece[:, width : width + unit]
            across = pl.ds(pl.multiple_of(spot * unit, unit), unit)
            out_weight[first : first + depth, across] = piece[:, width + unit :]
            first = (first + depth) % width
    for kind in range(3):
        product = tn(down.get()[...], ups.get()[kind])
        whole[kind] = (whole[kind].astype(F32) + product).astype(BF16)
    tokens, cosine, sine = tokens.get(), cosine.get(), sine.get()
    count, block = tokens.shape[0], tokens.shape[1] - 16
    for n in range(count):
        part = gain.shape[1] // count
        gain[:, n * part : (n + 1) * part] = tokens[n, block:, :part].astype(F32)[:2]

    def step(n, _):
        at = rows_of(n, block)
        unit, _ = normalized(tokens[n, :block].astype(F32))
        rows = (unit * gain[0:1, :]).astype(BF16)
        norm[at, :] = rows
        cos, sin = widened(cosine[at, :], width), widened(sine[at, :], width)
        for kind, out in enumerate((query, key, value)):
            part = nn(rows, whole[kind])
            if kind < 2:
                part = part * cos + swapped(part) * sin
            if kind == 0:
                part = part.astype(BF16).astype(F32) * 0.125
            out[at, :] = part.astype(BF16)
        return 0

    lax.fori_loop(0, count, step, 0)


def attend_kernel(count, direct, seg_scalar, query, key, value, segments, *refs):
    outs, (log_total, mixed_t, value_t, seg_t) = refs[:count], refs[count:]
    segments = segments.get()
    seg_row = segments[...].astype(F32)
    seg_t[...] = jnp.broadcast_to(seg_row, (128, seg_row.shape[1])).T
    query, key, value = query.get(), key.get(), value.get()
    block = outs[0].shape[0]
    width = query.shape[1]
    heads = width // HEAD_DIM
    value_t[...] = value[...].T
    parts = [slice(head * HEAD_DIM, (head + 1) * HEAD_DIM) for head in range(heads)]

    def step(n, _):
        place = owner(n, direct)
        at = rows_of(place, block)
        rows = query[at, :]
        own = [head_part(rows, head) for head in range(heads)]
        seg_here = segments[:, at].astype(F32)

        def against(m, carry):
            tops, sums, mixed = carry
            keys = rows_of(m, block)
            column = widened(seg_t[keys, :], block)
            bias = jnp.where(column == seg_here, 0.0, -1e30)
            near = key[keys, :]
            scores = [nt(near, part) + bias for part in own]
            now = [
                jnp.maximum(top, jnp.max(part, axis=0, keepdims=True))
                for top, part in zip(tops, scores)
            ]
            raised = [jnp.exp(part - top) for part, top in zip(scores, now)]
            scale = [jnp.exp(before - top) for before, top in zip(tops, now)]
            added = [nn(value_t[part, keys], up.astype(BF16)) for part, up in zip(parts, raised)]
            sums = [
                total * by + jnp.sum(up, axis=0, keepdims=True)
                for total, by, up in zip(sums, scale, raised)
            ]
            mixed = [old * by + new for old, by, new in zip(mixed, scale, added)]
            return now, sums, mixed

        start = (
            [jnp.full((1, block), -2e30, F32)] * heads,
            [jnp.zeros((1, block), F32)] * heads,
            [jnp.zeros((HEAD_DIM, block), F32)] * heads,
        )
        first, last = document_range(place, block, seg_scalar, seg_row)
        tops, sums, mixed = lax.fori_loop(first, last, against, start)
        for head in range(heads):
            log_total[head : head + 1, at] = tops[head] + jnp.log(sums[head])
            mixed_t[n, parts[head], :] = mixed[head] * (1.0 / sums[head])
        to_slot(outs, n, mixed_t[n].T.astype(BF16))
        return 0

    lax.fori_loop(0, count, step, 0)


def features(n, width, direct):
    if not direct:
        return slice(n * width, (n + 1) * width)
    return pl.ds(pl.multiple_of(owner(n, direct) * width, width), width)


def out_kernel(count, direct, inputs, gain, down, up, *refs):
    attn, weights = refs[:count], refs[count : 2 * count]
    middle, norm, narrow = refs[2 * count :]
    down = down.get()
    total = inputs.get()[...].astype(F32)
    thin = jnp.zeros(narrow.shape, F32)
    for n in range(count):
        rows = attn[n].get()[...]
        total = total + nn(rows, weights[n].get()[...])
        thin = thin + nt(rows, down[:, features(n, rows.shape[1], direct)])
    thin = thin.astype(BF16)
    total = total + nn(thin, up.get()[...])
    middle[...] = total
    narrow[...] = thin
    norm[...] = (normalized(total)[0] * gain.get()[1:2, :]).astype(BF16)


def mlp_pre_kernel(packed, direct, down_in, up_in, down_out, up_out, grads, *refs):
    pieces = 9 if packed else 2
    weights, refs = refs[:pieces], refs[pieces:]
    w_in, w_out, grad_early, grad_late = refs
    hidden, width = w_out.shape
    if packed:
        depth, thin = width // 4, width // 8
        first = 0
        for n in range(pieces):
            piece = weights[n].get()
            rows = slice(first, first + piece.shape[0])
            spot = came_from(n)
            across = pl.ds(pl.multiple_of(lax.rem(spot, 4) * depth, depth), depth)
            w_in[spot // 4, rows, across] = piece[:, :depth]
            across = pl.ds(pl.multiple_of(spot * thin, thin), thin)
            w_out[rows, across] = piece[:, depth:]
            first = rows.stop % hidden
    else:
        w_in[...] = weights[0].get()[...]
        w_out[...] = weights[1].get()[...]
    for n in range(2):
        w_in[n] = (w_in[n].astype(F32) + tn(up_in.get()[n], down_in.get()[...])).astype(BF16)
    w_out[...] = (w_out[...].astype(F32) + tn(down_out.get()[...], up_out.get()[...])).astype(BF16)
    grads = grads.get()
    for n in range(grads.shape[0]):
        target = grad_early if n < 2 else grad_late
        target[n if n < 2 else n - 2] = nt(grads[owner(n, direct)], w_out[...])


def mlp_kernel(count, first, w_in, grad_act, *refs):
    norms, backs, (act_out, grad_out) = refs[:count], refs[count : 2 * count], refs[2 * count :]
    w_in, grad_act = w_in.get(), grad_act.get()
    for n in range(count):
        norm = norms[n].get()[...]
        inputs, gate = nt(norm, w_in[0]), nt(norm, w_in[1])
        phi = 0.5 + 0.5 * lax.erf(inputs * (0.5**0.5))
        gelu = inputs * phi
        act_out[n] = (gelu * gate).astype(BF16)
        back_act = grad_act[first + n]
        slope = phi + inputs * (jnp.exp(-0.5 * inputs * inputs) * 0.3989422804014327)
        grad_inputs = (back_act * gate * slope).astype(BF16)
        grad_gate = (back_act * gelu).astype(BF16)
        grad_out[0, n] = grad_inputs
        grad_out[1, n] = grad_gate
        backs[n][...] = (nn(grad_inputs, w_in[0]) + nn(grad_gate, w_in[1])).astype(BF16)


def mlp_terms_kernel(count, first, direct, pick, down_in, up_in, down_out, up_out, *refs):
    acts, grads, out_grad, refs = refs[:2], refs[2:4], refs[4], refs[5:]
    norms, terms = refs[:count], refs[count]
    down_in_grad = down_out_grad = up_out_grad = 0.0
    up_in_grad = [0.0, 0.0]
    down_in, up_in, down_out, up_out = down_in.get(), up_in.get(), down_out.get(), up_out.get()
    for n in range(count):
        norm = norms[n].get()[...]
        narrow = nt(norm, down_in[...]).astype(BF16)
        back = [grads[n // 2].get()[h, n % 2] for h in range(2)]
        inner_in = (nt(back[0], up_in[0]) + nt(back[1], up_in[1])).astype(BF16)
        down_in_grad = down_in_grad + tn(inner_in, norm)
        for h in range(2):
            up_in_grad[h] = up_in_grad[h] + tn(narrow, back[h])
        act = acts[n // 2].get()[n % 2]
        grad = out_grad.get()[owner(first + n, direct)]
        narrow_two = nt(act, down_out[...]).astype(BF16)
        inner = nt(grad, up_out[...]).astype(BF16)
        down_out_grad = down_out_grad + tn(inner, act)
        up_out_grad = up_out_grad + tn(narrow_two, grad)
    at = chunked(terms, 0, up_in_grad[0])
    at = chunked(terms, at, up_in_grad[1])
    at = chunked(terms, at, down_out_grad)
    labelled(terms, at, pick)
    at = chunked(terms, at + 1, down_in_grad)
    chunked(terms, at, up_out_grad)


def mlp_out_kernel(count, w_out, *refs):
    acts, outs = refs[: count // 2], refs[count // 2 :]
    w_out = w_out.get()
    for n in range(count):
        outs[n].ref[...] = nn(acts[n // 2].get()[n % 2], w_out[...]).astype(BF16)
        outs[n].send()


def out_back_kernel(count, parts, direct, middle, out_grad, gain, down, up, narrow, *refs):
    back, refs = refs[:parts], refs[parts:]
    attn, weights = refs[:count], refs[count : 2 * count]
    grad_mid, refs = refs[2 * count], refs[2 * count + 1 :]
    slots, (keep, send, down_grad) = refs[:count], refs[count:]
    total = sum(ref.get()[...].astype(F32) for ref in back)
    grad = out_grad.get()[...].astype(F32)
    grad = grad + norm_back(middle.get()[...], gain.get()[1:2, :], total)
    grad_mid[...] = grad
    low = grad.astype(BF16)
    down = down.get()
    inner = nt(low, up.get()[...]).astype(BF16)
    for n in range(count):
        rows = attn[n].get()[...]
        own = features(n, rows.shape[1], direct)
        slots[n][...] = (nt(low, weights[n].get()[...]) + nn(inner, down[:, own])).astype(BF16)
        down_grad[:, own] = tn(inner, rows)
    half = grad.shape[1] // 256
    halves(keep, half, send, half, tn(narrow.get()[...], low))
    halves(keep, 0, send, 0, down_grad[...])


def attend_back_kernel(
    count, direct, seg_scalar, pick, query, key, value, segments, log_total, mixed_t, cosine, sine,
    down, ups, norm, *refs
):
    grads, (grad_qkv, keep, send) = refs[:count], refs[count : count + 3]
    key_t, seg_t, grad_q, grad_k, grad_v, query_t, grad_all = refs[count + 3 :]
    segments = segments.get()
    seg_row = segments[...].astype(F32)
    seg_t[...] = jnp.broadcast_to(seg_row, (128, seg_row.shape[1])).T
    for ref in (grad_k, grad_v):
        ref[...] = jnp.zeros_like(ref)
    query, key, value = query.get(), key.get(), value.get()
    log_total, mixed_t = log_total.get(), mixed_t.get()
    block = grads[0].get().shape[0]
    width = query.shape[1]
    heads = width // HEAD_DIM
    key_t[...] = key[...].T
    for n in range(count):
        grad_all[n] = grads[n].get()[...]
    parts = [slice(head * HEAD_DIM, (head + 1) * HEAD_DIM) for head in range(heads)]

    def step(n, _):
        place = owner(n, direct)
        at = rows_of(place, block)
        rows, grad = query[at, :], grad_all[n]
        own = [head_part(rows, head) for head in range(heads)]
        own_grad = [head_part(grad, head) for head in range(heads)]
        product = grad.astype(F32).T * mixed_t[n]
        dots = [jnp.sum(product[part], axis=0, keepdims=True) for part in parts]
        query_t[...] = jnp.zeros_like(query_t)
        seg_here = segments[:, at].astype(F32)

        def against(m, _):
            keys = rows_of(m, block)
            column = widened(seg_t[keys, :], block)
            bias = jnp.where(column == seg_here, 0.0, -1e30)
            near, near_value = key[keys, :], value[keys, :]
            probs = [
                jnp.exp(nt(near, own[head]) + bias - log_total[head : head + 1, at])
                for head in range(heads)
            ]
            grad_probs = [nt(near_value, part) for part in own_grad]
            grad_s = [
                (prob * (grad_prob - dot)).astype(BF16)
                for prob, grad_prob, dot in zip(probs, grad_probs, dots)
            ]
            sum_v = sum(nn(prob.astype(BF16), part) for prob, part in zip(probs, own_grad))
            sum_k = sum(nn(part, mine) for part, mine in zip(grad_s, own))
            for head in range(heads):
                query_t[parts[head], :] += nn(key_t[parts[head], keys], grad_s[head])
            grad_k[keys, :] += sum_k
            grad_v[keys, :] += sum_v
            return 0

        first, last = document_range(place, block, seg_scalar, seg_row)
        lax.fori_loop(first, last, against, 0)
        grad_q[at, :] = query_t[...].T * 0.125
        return 0

    lax.fori_loop(0, count, step, 0)
    cosine, sine = cosine.get(), sine.get()

    def finish(n, _):
        at = rows_of(n, block)
        cos, sin = widened(cosine[at, :], width), widened(sine[at, :], width)
        for kind, ref in enumerate((grad_q, grad_k)):
            part = ref[at, :]
            grad_qkv[kind, at, :] = (part * cos - swapped(part) * sin).astype(BF16)
        grad_qkv[2, at, :] = grad_v[at, :].astype(BF16)
        return 0

    lax.fori_loop(0, count, finish, 0)
    norm = norm.get()
    inner = sum(nt(grad_qkv[kind], ups.get()[kind]) for kind in range(3))
    narrow = nt(norm[...], down.get()[...]).astype(BF16)
    at = 0
    for kind in range(3):
        at = chunked(keep, at, tn(narrow, grad_qkv[kind]))
    labelled(keep, at, pick)
    halves(keep, at + 1, send, 0, tn(inner.astype(BF16), norm[...]))


def qkv_back_kernel(count, direct, grad_qkv, weights, *outs):
    block = outs[0].ref.shape[0]
    grad_qkv, weights = grad_qkv.get(), weights.get()
    for n in list(range(1, count, 2)) + list(range(0, count, 2)):
        at = rows_of(owner(n, direct), block)
        total = sum(nt(grad_qkv[kind, at, :], weights[kind]) for kind in range(3))
        outs[n].ref[...] = total.astype(BF16)
        outs[n].send()


def last_kernel(parts, out_parts, inputs, grad_mid, middle, gain, *refs):
    backs, outs = refs[:parts], refs[parts : parts + out_parts]
    input_grad, layer_out = refs[parts + out_parts :]
    total = middle.get()[...] + sum(ref.get()[...].astype(F32) for ref in outs)
    layer_out.ref[...] = total.astype(BF16)
    layer_out.send()
    total = sum(ref.get()[...].astype(F32) for ref in backs)
    back = norm_back(inputs.get()[...].astype(F32), gain.get()[0:1, :], total)
    input_grad.ref[...] = (grad_mid.get()[...] + back).astype(BF16)


def add_kernel(one, two, out):
    out[...] = (one.get()[...].astype(F32) + two.get()[...].astype(F32)).astype(out.dtype)


def pair_kernel(local, own, came, out):
    own, came = own.get(), came.get()
    across = lax.axis_index("tok") // 2
    out[pl.ds(across * local, local)] = own[:local]
    out[pl.ds((1 - across) * local, local)] = came[:local]
    out[2 * local :] = (own[local:].astype(F32) + came[local:].astype(F32)).astype(BF16)


def late_kernel(local, keep, came, out_keep, out_came, out):
    keep, out_keep = keep.get(), out_keep.get()
    out[:local] = keep[:local]
    half = keep.shape[0] - local
    total = keep[local:].astype(F32) + came.get()[...].astype(F32)
    out[local : local + half] = total.astype(BF16)
    total = out_keep[...].astype(F32) + out_came.get()[...].astype(F32)
    out[local + half :] = total.astype(BF16)


def merge_kernel(local, own, across, beside, diagonal, out):
    row, place = lax.axis_index("tok") // 2, lax.rem(lax.axis_index("seq"), 2)
    for n, one, two in ((place, own, across), (1 - place, beside, diagonal)):
        one, two = one.get(), two.get()
        out[n, pl.ds(row * local, local)] = one[:local]
        out[n, pl.ds((1 - row) * local, local)] = two[:local]
        out[n, 2 * local :] = (one[local:].astype(F32) + two[local:].astype(F32)).astype(BF16)


def stack_kernel(*refs):
    out = refs[-1]
    own = lax.axis_index("seq") // 2
    for n, ref in enumerate(refs[:-1]):
        block = ref.get()
        size = block.shape[0]
        out[pl.ds(jnp.bitwise_xor(own, n) * size, size)] = block[...]


def spread_kernel(widths, local, mine, other, *refs):
    outs, both = refs[: len(widths)], refs[len(widths)]
    core = lax.rem(lax.axis_index("tok"), 2)
    for out in outs:
        out[...] = jnp.zeros_like(out)
    mine, other = mine.get(), other.get()
    both[core] = mine[...]
    both[1 - core] = other[...]

    def step(n, _):
        pick = jnp.max(both[0, n, local - 1].astype(F32)).astype(jnp.int32)
        at, rest = 0, 2 * local
        for out, width in zip(outs, widths):
            if width <= 0:
                chunks = out.shape[2] // 128
                for m in range(chunks):
                    if width == 0:
                        term = both[0, n, rest + m].astype(F32) + both[1, n, rest + m].astype(F32)
                    else:
                        term = both[2 * m // chunks, n, rest + m % (chunks // 2)].astype(F32)
                    out[pick, :, m * 128 : (m + 1) * 128] += term
                rest += chunks if width == 0 else chunks // 2
                continue
            blocks = -(-width // 128)
            for group in range(out.shape[2] // (4 * width)):
                for tok in range(4):
                    first = (group * 4 + tok) * width
                    base = (tok // 2) * local + at
                    parts = [both[tok % 2, n, base + m] for m in range(blocks)]
                    term = jnp.concatenate(parts, axis=1)[:, :width].astype(F32)
                    out[pick, :, first : first + width] += term
                at += blocks
        return 0

    lax.fori_loop(0, mine.shape[0], step, 0)


class Exchange:
    def __init__(self, size):
        self.size = size
        self.direct = size == 4

    def swap(self, block, bits):
        pairs = [(n, n ^ bits) for n in range(self.size)]
        return lax.ppermute(block, "tok", pairs)

    def hop(self, block):
        if not self.direct:
            whole = lax.all_gather(block, "tok", axis=0)
            return [whole[n] for n in range(self.size)]
        return [block, self.swap(block, 1), self.swap(block, 2)]

    def land(self, parts):
        if not self.direct:
            return parts
        return parts + [self.swap(parts[2], 1)]

    def turn(self, slots):
        if not self.direct:
            whole = lax.all_to_all(jnp.stack(slots), "tok", 0, 0)
            return [whole[n] for n in range(self.size)]
        return [slots[0]] + [self.swap(slots[n], n) for n in range(1, self.size)]

    def halve(self, slots):
        near, far = self.swap(slots[1], 1), self.swap(slots[3], 1)
        both = call(add_kernel, [shape(far.shape, far.dtype)], [slots[2], far], name="add")[0]
        return near, both

    def reduce(self, slots):
        if not self.direct:
            return [lax.psum_scatter(jnp.stack(slots), "tok", scatter_dimension=0)]
        near, both = self.halve(slots)
        return [slots[0], near, self.swap(both, 2)]


def meet(*arrays):
    return lax.optimization_barrier(arrays)


class Ring:
    def __init__(self, block):
        self.blocks = [block]
        self.right = self.left = block
        self.half = block.shape[0] // 32 * 16
        self.ahead = [(RING[n], RING[(n + 1) % len(RING)]) for n in range(len(RING))]
        self.behind = [(b, a) for a, b in self.ahead]

    def step(self):
        step = len(self.blocks) // 2 + 1
        if step == len(RING) // 2:
            self.right, self.left = self.right[: self.half], self.left[self.half :]
        self.right = lax.ppermute(self.right, "seq", self.ahead)
        self.left = lax.ppermute(self.left, "seq", self.behind)
        self.blocks += [self.right, self.left]

    def meet(self, *arrays):
        self.right, self.left, *arrays = meet(self.right, self.left, *arrays)
        if len(self.blocks) > 1:
            self.blocks[-2:] = [self.right, self.left]
        return arrays


def owner_of_columns(seq, tok):
    double, single, seen = [], [], [0] * tok
    kinds = [[0, 0, 0] for _ in range(tok)]
    for s in range(seq):
        first = 3 * s + s % 2
        own = first % seq // 2
        double.append((own, seen[own]))
        kinds[own][seen[own]] = first // seq
        seen[own] += 1
        last = 3 * s + 2 * (1 - s % 2)
        single.append((last % seq // 2, last % 2))
        kinds[last % seq // 2][2] = last // seq
    return double, single, kinds


def body(
    tokens,
    out_grad,
    segments,
    adapter_index,
    qkv_weight,
    out_weight,
    in_weight,
    out2_weight,
    attn_gain,
    mlp_gain,
    qkv_down,
    qkv_up,
    out_down,
    out_up,
    in_down,
    in_up,
    out2_down,
    out2_up,
):
    seq, tok = lax.axis_size("seq"), lax.axis_size("tok")
    own_tok = lax.axis_index("tok")
    move = Exchange(tok)
    direct = move.direct
    fast = direct and seq == 8
    adapters, rank, width = qkv_down.shape
    length = segments.shape[1]
    rows = tokens.shape[1]
    heads = HEADS // tok
    lanes = heads * HEAD_DIM
    hidden = out2_weight.shape[0]
    hidden_all = hidden * tok
    inputs, out_grad = tokens[0], out_grad[0]
    pick = adapter_index[0]
    pieces = lambda columns: -(-columns // 128)
    early_local, late_local = 3 * pieces(hidden) + 1, 3 * pieces(lanes) + 1
    wide = pieces(width)

    sizes = ((width, 0), (lanes, 3), (width, 0), (width, 0), (width, 0), (hidden, 2), (hidden, 1), (width, 0))
    tables = (qkv_down, qkv_up, out_down, out_up, in_down, in_up, out2_down, out2_up)
    if fast:
        adapters_own = call(
            functools.partial(adapters_kernel, tok),
            [
                shape((groups,) * (groups > 1) + (rank, columns), BF16)
                for columns, groups in sizes
            ],
            [Pick(table, adapter_index) for table in tables],
            name="adapters",
        )
    else:

        def chosen(table, columns, groups):
            parts = []
            for group in range(max(groups, 1)):
                start = (group * tok + own_tok) * columns if groups else 0
                parts.append(lax.dynamic_slice(table, (pick, 0, start), (1, rank, columns))[0])
            return jnp.stack(parts) if groups > 1 else parts[0]

        adapters_own = [chosen(table, *size) for table, size in zip(tables, sizes)]

    exponent = jnp.arange(0, HEAD_DIM, 2).astype(F32) / HEAD_DIM
    inverse = 1.0 / THETA**exponent
    phases = jnp.arange(length).astype(F32)[:, None] * jnp.tile(inverse, 4)[None, :]
    sign = jnp.where(jnp.arange(2 * HEAD_DIM) % HEAD_DIM < HEAD_DIM // 2, -1.0, 1.0)
    cosine, sine = jnp.cos(phases), jnp.sin(phases) * sign[None, :]

    if fast:
        unit = width // seq
        double, single, kinds = owner_of_columns(seq, tok)
        kinds = jnp.array(sum(kinds, []), jnp.int32)
        token_block, *parts = call(
            prepare_kernel,
            [
                shape((rows + 16, width), BF16),
                shape((qkv_weight.shape[0], 2 * unit), BF16),
                shape((qkv_weight.shape[0], unit), BF16),
            ],
            [inputs, attn_gain, mlp_gain, qkv_weight],
            name="prepare",
        )
        for n, owners in enumerate((double, single)):
            pairs = [
                (s * tok + t, (owners[s][1] * tok + t) * tok + owners[s][0])
                for s in range(seq)
                for t in range(tok)
            ]
            parts[n] = lax.ppermute(parts[n], ("seq", "tok"), pairs)
        together = meet(token_block, cosine, sine, *adapters_own, *parts)
        token_block, cosine, sine, adapters_own = *together[:3], together[3:11]
        parts = list(together[11:])
        ring = Ring(jnp.concatenate(parts + [out_weight], axis=1))
        ring.step()
        ring.step()
        in_piece, out_grad_in = ring.meet(in_weight.T, out_grad)
        pairs = [
            (s * tok + t, ((s // tok) * tok + t) * tok + s % tok)
            for s in range(seq)
            for t in range(tok)
        ]
        in_piece = lax.ppermute(in_piece, ("seq", "tok"), pairs)
        ring.step()
        ring.step()
        mlp_piece = jnp.concatenate([in_piece, out2_weight], axis=1)
        (mlp_piece,) = ring.meet(mlp_piece)
        qkv_pieces = ring.blocks
        mlp_ring = Ring(mlp_piece)
        mlp_ring.step()
    else:

        def columns(weight, count):
            block = lax.all_gather(weight, "seq", axis=1, tiled=True)
            split = block.reshape(block.shape[0], count, tok, -1).transpose(2, 1, 0, 3)
            turned = lax.all_to_all(split, "tok", 0, 0)
            return turned.transpose(1, 0, 2, 3).reshape(count, width, -1)

        gain_rows = jnp.stack([attn_gain, mlp_gain])
        gain_rows = jnp.pad(gain_rows, ((0, 14), (0, width - width // tok)))
        token_block = jnp.concatenate([inputs, gain_rows], axis=0)
        out_grad_in = out_grad
        qkv_pieces = [columns(qkv_weight, 3)]
        kinds = jnp.zeros((1,), jnp.int32)
        own_out = lax.all_gather(out_weight, "seq", axis=1, tiled=True)
        mlp_weights = [
            columns(in_weight, 2).transpose(0, 2, 1),
            lax.all_gather(out2_weight, "seq", axis=1, tiled=True),
        ]
    token_all = lax.all_gather(token_block, "tok", axis=0)
    grad_all = lax.all_gather(out_grad_in, "tok", axis=0)

    down_one, up_one, down_attn, up_attn, down_two, up_two, down_last, up_last = adapters_own

    norm_one, gain, query, key, value, w_qkv, *own_row = call(
        functools.partial(qkv_kernel, len(qkv_pieces)),
        [shape((length, width), BF16), shape((2, width), F32)]
        + [shape((length, lanes), BF16)] * 3
        + [shape((3, width, lanes), BF16)]
        + [shape((lanes, width), BF16)] * fast,
        [kinds, token_all, down_one, up_one, cosine, sine] + qkv_pieces,
        smem=(0,),
        name="qkv",
    )
    if fast:
        query, key, value = mlp_ring.meet(query, key, value)
        mlp_ring.step()
    out_parts = move.hop(own_row[0] if fast else own_out)
    *attn_slots, log_total, mixed_t = call(
        functools.partial(attend_kernel, tok, direct),
        [shape((rows, lanes), BF16)] * tok
        + [shape((heads, length), F32), shape((tok, lanes, rows), F32)],
        [segments, query, key, value, segments],
        smem=(0,),
        scratch=[pltpu.VMEM((lanes, length), BF16), pltpu.VMEM((length, 128), F32)],
        name="attend",
    )
    attn_slots, out_parts = meet(attn_slots, out_parts)
    if fast:
        attn_slots = mlp_ring.meet(*attn_slots)
        mlp_ring.step()
    attn = move.turn(attn_slots)
    out_weights = move.land(out_parts)
    middle, norm_two, narrow_attn = call(
        functools.partial(out_kernel, tok, direct),
        [shape((rows, width), F32), shape((rows, width), BF16), shape((rows, rank), BF16)],
        [inputs, gain, down_attn, up_attn] + attn + out_weights,
        name="out",
    )
    if fast:
        (norm_two,) = mlp_ring.meet(norm_two)
        mlp_ring.step()
        mlp_weights = mlp_ring.blocks
    norm_slots = move.hop(norm_two)
    w_in, w_out, *grad_acts = call(
        functools.partial(mlp_pre_kernel, fast, direct),
        [
            shape((2, hidden, width), BF16),
            shape((hidden, width), BF16),
            shape((2, rows, hidden), F32),
            shape((tok - 2, rows, hidden), F32),
        ],
        [down_two, up_two, down_last, up_last, grad_all] + mlp_weights,
        name="mlp_pre",
    )
    back_slots, acts, grads_z = [], [], []
    for first in range(0, tok, 2):
        *backs, act, grad_z = call(
            functools.partial(mlp_kernel, 2, max(first - 2, 0)),
            [shape((rows, width), BF16)] * 2
            + [shape((2, rows, hidden), BF16), shape((2, 2, rows, hidden), BF16)],
            [w_in, grad_acts[min(first, 1)]] + norm_slots[first : first + 2],
            name="mlp",
        )
        if first == 0:
            *backs, norm_slots[2] = meet(*backs, norm_slots[2])
            norm_slots = move.land(norm_slots)
        back_slots += backs
        acts.append(act)
        grads_z.append(grad_z)
    back_two = move.reduce(back_slots)
    out_slots, early = [], []
    for first in range(0, tok, 4):
        pair = slice(first // 2, first // 2 + 2)
        terms = call(
            functools.partial(mlp_terms_kernel, 4, first, direct),
            [shape((early_local + 2 * wide, rank, 128), BF16 if fast else F32)],
            [adapter_index, down_two, up_two, down_last, up_last]
            + acts[pair]
            + grads_z[pair]
            + [grad_all]
            + norm_slots[first : first + 4],
            smem=(0,),
            name="mlp_terms",
        )[0]
        early.append(terms)
        terms, *acts[pair] = meet(terms, *acts[pair])
        out_slots += call(
            functools.partial(mlp_out_kernel, 4),
            [shape((rows, width), BF16)] * 4,
            [w_out] + acts[pair],
            early=(0, 1, 2, 3),
            name="mlp_out",
        )
    early = sum(early[1:], early[0])
    if fast:
        back_two[2], *out_slots = meet(back_two[2], *out_slots)
        early = call(
            functools.partial(pair_kernel, early_local),
            [shape((early_local + early.shape[0], rank, 128), BF16)],
            [early, move.swap(early, 2)],
            name="pair",
        )[0]
        back_two[2], early = meet(back_two[2], early)
        early = lax.all_gather(early, "seq", axis=0)
    grad_mid, *rest = call(
        functools.partial(out_back_kernel, tok, len(back_two), direct),
        [shape((rows, width), F32)]
        + [shape((rows, lanes), BF16)] * tok
        + [shape((wide, rank, 128), BF16)] * 2,
        [middle, out_grad, gain, down_attn, up_attn, narrow_attn] + back_two + attn + out_weights,
        scratch=[pltpu.VMEM((rank, width), F32)],
        name="out_back",
    )
    out_keep, out_send = rest[tok:]
    attn_grads = move.turn(rest[:tok])
    if fast:
        attn_grads, out_slots = meet(attn_grads, out_slots)
    out_parts = move.turn(out_slots) if fast else move.reduce(out_slots)
    grad_qkv, keep, send = call(
        functools.partial(attend_back_kernel, tok, direct),
        [
            shape((3, length, lanes), BF16),
            shape((late_local + wide // 2, rank, 128), BF16),
            shape((wide // 2, rank, 128), BF16),
        ],
        [segments, adapter_index, query, key, value, segments, log_total, mixed_t, cosine, sine]
        + [down_one, up_one, norm_one]
        + attn_grads,
        smem=(0, 1),
        scratch=[
            pltpu.VMEM((lanes, length), BF16),
            pltpu.VMEM((length, 128), F32),
            pltpu.VMEM((length, lanes), F32),
            pltpu.VMEM((length, lanes), F32),
            pltpu.VMEM((length, lanes), F32),
            pltpu.VMEM((lanes, rows), F32),
            pltpu.VMEM((tok, rows, lanes), BF16),
        ],
        name="attend_back",
    )

    def slots_of_one(grad_qkv):
        return call(
            functools.partial(qkv_back_kernel, tok, direct),
            [shape((rows, width), BF16)] * tok,
            [grad_qkv, w_qkv],
            early=tuple(range(tok)),
            name="qkv_back",
        )

    def last_of(back_one):
        return call(
            functools.partial(last_kernel, len(back_one), len(out_parts)),
            [shape((rows, width), BF16)] * 2,
            [inputs, grad_mid, middle, gain] + back_one + out_parts,
            early=(0, 1),
            name="last",
        )

    grads = lambda columns: shape((adapters, rank, columns), F32)
    if fast:

        def spread(whole, local, widths, columns):
            return call(
                functools.partial(spread_kernel, widths, local),
                [grads(size) for size in columns],
                [whole, move.swap(whole, 1)],
                scratch=[pltpu.VMEM((2,) + whole.shape, BF16)],
                name="spread",
            )

        keep, early, *out_parts = meet(keep, early, *out_parts)
        late = call(
            functools.partial(late_kernel, late_local),
            [shape((late_local + 3 * wide // 2, rank, 128), BF16)],
            [keep, move.swap(send, 1), out_keep, move.swap(out_send, 1)],
            name="late",
        )[0]
        diagonal = [(s * tok + t, (s ^ 1) * tok + (t ^ 2)) for s in range(seq) for t in range(tok)]
        came = [
            late,
            move.swap(late, 2),
            lax.ppermute(late, "seq", [(s, s ^ 1) for s in range(seq)]),
            lax.ppermute(late, ("seq", "tok"), diagonal),
        ]
        late, grad_qkv = meet(late, grad_qkv)
        one_slots = slots_of_one(grad_qkv)
        near, both = move.halve(one_slots)
        both, *came = meet(both, *came)
        back_one = [one_slots[0], near, move.swap(both, 2)]
        merged = call(
            functools.partial(merge_kernel, late_local),
            [shape((2, late_local + late.shape[0], rank, 128), BF16)],
            came,
            name="merge",
        )[0]
        blocks = [merged]
        for bits in (2, 4, 6):
            pairs = [(s, s ^ bits) for s in range(seq)]
            blocks.append(lax.ppermute(merged, "seq", pairs))
        in_up_grad, out2_down_grad, in_down_grad, out2_up_grad = spread(
            early, early_local, (hidden, hidden, 0, 0), (2 * hidden_all, hidden_all, width, width)
        )
        input_grad, layer_out = last_of(back_one)
        in_up_grad, input_grad, *blocks = meet(in_up_grad, input_grad, *blocks)
        late = call(
            stack_kernel, [shape((seq,) + merged.shape[1:], BF16)], blocks, name="stack"
        )[0]
        qkv_up_grad, qkv_down_grad, out_down_grad, out_up_grad = spread(
            late, late_local, (lanes, -1, -1, -1), (3 * width, width, width, width)
        )
    else:
        input_grad, layer_out = last_of(move.reduce(slots_of_one(grad_qkv)))
        picked = (pick == jnp.arange(adapters)).astype(F32)[:, None, None]

        def term(blocks, columns):
            return blocks.astype(F32).transpose(1, 0, 2).reshape(rank, -1)[:, :columns]

        def placed(terms, first, groups, columns):
            total = jnp.zeros((rank, groups * tok * columns), F32)
            for group in range(groups):
                at = first + group * pieces(columns)
                part = term(terms[at : at + pieces(columns)], columns)
                start = (group * tok + own_tok) * columns
                total = lax.dynamic_update_slice(total, part, (0, start))
            return total

        whole = lambda terms, at: term(terms[at : at + wide], width)

        def joined(kept, at, sent, first):
            half = wide // 2
            mine, other = kept[at : at + half], sent[first : first + half]
            swap = own_tok % 2 == 1
            low, high = jnp.where(swap, other, mine), jnp.where(swap, mine, other)
            return term(jnp.concatenate([low, high]), width)

        sums = (
            joined(keep, late_local, send, 0),
            placed(keep, 0, 3, lanes),
            joined(out_keep, 0, out_send, 0),
            joined(out_keep, wide // 2, out_send, wide // 2),
            whole(early, early_local),
            placed(early, 0, 2, hidden),
            placed(early, 2 * pieces(hidden), 1, hidden),
            whole(early, early_local + wide),
        )
        summed = lax.psum(tuple(picked * part[None] for part in sums), ("seq", "tok"))
        qkv_down_grad, qkv_up_grad, out_down_grad, out_up_grad = summed[:4]
        in_down_grad, in_up_grad, out2_down_grad, out2_up_grad = summed[4:]
    return (
        layer_out[None],
        input_grad[None],
        qkv_down_grad,
        qkv_up_grad,
        out_down_grad,
        out_up_grad,
        in_down_grad,
        in_up_grad,
        out2_down_grad,
        out2_up_grad,
    )


def solution(mesh):
    grid = P("tok", "seq")
    split = P("seq", "tok", None)
    return jax.shard_map(
        body,
        mesh=mesh,
        in_specs=(split, split, P("seq", None), P("seq"), grid, grid, grid, grid, P("tok"), P("tok"))
        + (P(),) * 8,
        out_specs=(split, split) + (P(),) * 8,
        check_vma=False,
    )
```

time: 292 us -> 277 us (0.949)
  local copies, waits for them, and re-layouts: 23.1 us -> 11.1 us
  waiting for transfers between devices: 76 us -> 86.5 us
  other arithmetic: 10.2 us -> 3.11 us
  Pallas kernels: 120 us -> 117 us
    ppermute x12 -> x8, starting transfers between devices: 26 us -> 11.4 us  [step(): self.right = lax.ppermute(self.right, 'seq', self.ahead)]
    ppermute x12 -> x8, waiting for transfers between devices: 7.8 us -> 19.4 us  [step(): self.left = lax.ppermute(self.left, 'seq', self.behind)]
    ppermute x2 -> x7, waiting for transfers between devices: 8.9 us -> 1.11 us  [the longest x1 1.09 us: body(): lax.ppermute(late, 'seq', [(s, s ^ 1) for s in range(seq)])]
    ppermute x12 -> x8, starting transfers between devices: 4.36 us -> 10.5 us  [step(): self.left = lax.ppermute(self.left, 'seq', self.behind)]
    squeeze x5 -> x0, local copies, waits for them, and re-layouts: 5.54 us -> none  [the longest x4 4.85 us: chosen(): return lax.dynamic_slice(table, (pick, 0, start), (1, rank, size))[0]]
    ppermute x26 -> x27, waiting for transfers between devices: 35.6 us -> 40.8 us  [swap(): return lax.ppermute(block, 'tok', pairs)]
    ppermute x2 -> x7, starting transfers between devices: 5.05 us -> 9.44 us  [the longest x3 4.45 us: body(): blocks.append(lax.ppermute(merged, 'seq', pairs))]
    another operation x4 -> x0, local copies, waits for them, and re-layouts: 4.17 us -> none  [the longest x2 2.75 us: body(): down_attn = chosen(out_down).reshape(rank, tok, lanes).transpose(1, 0, 2)]
  transfers between devices with their start and end apart: 56 -> 54, of which waited for: 23 -> 28; matrix products, arithmetic and copies ran while one was open for 7% -> 1% of each run, Pallas kernels for 39% -> 36%
where the time goes in v2:
time: 277 us
  Pallas kernels  117 us (42%)
  waiting for transfers between devices  86.5 us (31%)
  starting transfers between devices  44.4 us (16%)
  between operations  15.3 us (6%)
  local copies, waits for them, and re-layouts  11.1 us (4%)
  other arithmetic  3.11 us (1%)
    pallas_call x22, Pallas kernels, call(): pl.pallas_call(body, out_shape=list(out_shape), in_specs=[pl.BlockSpec(me...  117 us
    ppermute x27, waiting for transfers between devices, swap(): return lax.ppermute(block, 'tok', pairs)  40.8 us
    ppermute x8, waiting for transfers between devices, step(): self.right = lax.ppermute(self.right, 'seq', self.ahead)  22 us
    ppermute x8, waiting for transfers between devices, step(): self.left = lax.ppermute(self.left, 'seq', self.behind)  19.4 us
    ppermute x27, starting transfers between devices, swap(): return lax.ppermute(block, 'tok', pairs)  12.3 us
    ppermute x8, starting transfers between devices, step(): self.right = lax.ppermute(self.right, 'seq', self.ahead)  11.4 us
    unnamed x114, local copies, waits for them, and re-layouts  10.9 us
    ppermute x8, starting transfers between devices, step(): self.left = lax.ppermute(self.left, 'seq', self.behind)  10.5 us
  transfers between devices with their start and end apart: 54, of which 28 were waited for; matrix products, arithmetic and copies ran while one was open for 1% of the time, Pallas kernels for 36%

profile of v2, /device:TPU:0, one launch (start us, length us, event | category | flops | bytes accessed | tf_op | source)
XLA Modules:
  0.0 277.3 jit_solution(13698699019781423580)
XLA Ops:
  11.4 3.0 %fusion = (f32[1024,128]{1,0:T(8,128)}, f32[1024,128]{1,0:T(8,128)}) fusion(f32[128]{0:T(128)S(1)} %compare_select_fusion, f32[128]{0:T(128)S(1)} %mul.46, f32[1024]{0:T(1024)S(1)} %iota_convert_fusion), kind=kLoop, calls=%fused_computation.2 | loop fusion | flops 262144 | bytes 1053696 | tf_op jit(solution)/shard_map/mul | solution.py:866
  17.3 5.4 %collective-permute-start.3 = (bf16[256,512]{1,0:T(8,128)(2,1)S(1)}, bf16[256,512]{1,0:T(8,128)(2,1)S(1)}, u32[]{:S(2)}, u32[]{:S(2)}) collective-permute-start(bf16[256,512]{1,0:T(8,128)(2,1)S(1)} %constant_dynamic-update-slice_fusion.refs_6_), channel_id=1, source_target_pairs={{8,0},{16,8},{24,16},{28,24},{20,28},{12,20},{4,12},{0,4},{9,1},{1... | collective-permute-start | bytes 786440 | tf_op jit(solution)/shard_map/ppermute | solution.py:776
  23.4 5.6 %collective-permute-done.3.refs_8_ = bf16[256,512]{1,0:T(8,128)(2,1)S(1)} collective-permute-done((bf16[256,512]{1,0:T(8,128)(2,1)S(1)}, bf16[256,512]{1,0:T(8,128)(2,1)S(1)}, u32[]{:S(2)}, u32[]{:S(2)}) %collective-permute-start.3) | collective-permute-done | bytes 262176 | tf_op jit(solution)/shard_map/ppermute | solution.py:776
  31.4 6.8 %collective-permute-done.5.refs_10_ = bf16[256,512]{1,0:T(8,128)(2,1)S(1)} collective-permute-done((bf16[256,512]{1,0:T(8,128)(2,1)S(1)}, bf16[256,512]{1,0:T(8,128)(2,1)S(1)}, u32[]{:S(2)}, u32[]{:S(2)}) %collective-permute-start.5) | collective-permute-done | bytes 262176 | tf_op jit(solution)/shard_map/ppermute | solution.py:776
  40.7 5.1 %collective-permute-start.6 = (bf16[256,512]{1,0:T(8,128)(2,1)S(1)}, bf16[256,512]{1,0:T(8,128)(2,1)S(1)}, u32[]{:S(2)}, u32[]{:S(2)}) collective-permute-start(bf16[256,512]{1,0:T(8,128)(2,1)S(1)} %collective-permute-done.4.refs_9_), channel_id=1, source_target_pairs={{0,8},{8,16},{16,24},{24,28},{28,20},{20,12},{12,4},{4,0},{1,9},{9... | collective-permute-start | bytes 786440 | tf_op jit(solution)/shard_map/ppermute | solution.py:775
  45.9 8.4 %collective-permute-done.6.refs_11_ = bf16[256,512]{1,0:T(8,128)(2,1)S(1)} collective-permute-done((bf16[256,512]{1,0:T(8,128)(2,1)S(1)}, bf16[256,512]{1,0:T(8,128)(2,1)S(1)}, u32[]{:S(2)}, u32[]{:S(2)}) %collective-permute-start.6) | collective-permute-done | bytes 262176 | tf_op jit(solution)/shard_map/ppermute | solution.py:775
  54.4 4.6 %collective-permute-done.7.refs_12_ = bf16[256,512]{1,0:T(8,128)(2,1)S(1)} collective-permute-done((bf16[256,512]{1,0:T(8,128)(2,1)S(1)}, bf16[256,512]{1,0:T(8,128)(2,1)S(1)}, u32[]{:S(2)}, u32[]{:S(2)}) %collective-permute-start.7) | collective-permute-done | bytes 262176 | tf_op jit(solution)/shard_map/ppermute | solution.py:776
  59.2 2.6 collective-permute-done.8.refs_13_
  61.8 2.2 collective-permute-done.9.refs_14_
  66.8 8.9 %qkv.1 = (bf16[1024,1024]{1,0:T(8,128)(2,1)}, f32[2,1024]{1,0:T(2,128)}, bf16[1024,256]{1,0:T(8,128)(2,1)}, bf16[1024,256]{1,0:T(8,128)(2,1)}, bf16[1024,256]{1,...) custom-call(s32[12]{0:T(128)} %constant.32.clone.refs_0_, bf16[4,272,1024]{2,1,0:T(8,128)(2,1)} %bitcast.13, ...), custom_call_target="tpu_custom_call" | custom-call | flops 1 | bytes 1 | tf_op jit(solution)/shard_map/qkv/pallas_call | solution.py:136
  79.1 9.9 %attend.1 = (bf16[256,256]{1,0:T(8,128)(2,1)}, bf16[256,256]{1,0:T(8,128)(2,1)}, bf16[256,256]{1,0:T(8,128)(2,1)}, bf16[256,256]{1,0:T(8,128)(2,1)}, f32[4,1024]{1,0:T(4,128)}, /*index=5*/f32[4,256,256]{2,1,0:T(8,128)}) custom-call(s32[1,1024]{1,0:T(1,128)} %refs_5_.3, bf16[1024,256]{1,0:T(8,128)(2,1)} %get-tuple-element.188.refs_1_.refs_2_, ...), custom_call_target="tpu_custom_call" | custom-call | flops 1 | bytes 1 | tf_op jit(solution)/shard_map/attend/pallas_call | solution.py:136
  95.3 4.5 %collective-permute-done.18.refs_6_.refs_11_ = bf16[256,256]{1,0:T(8,128)(2,1)S(1)} collective-permute-done((bf16[256,256]{1,0:T(8,128)(2,1)}, bf16[256,256]{1,0:T(8,128)(2,1)S(1)}, u32[]{:S(2)}, u32[]{:S(2)}) %collective-permute-start.18) | collective-permute-done | bytes 131104 | tf_op jit(solution)/shard_map/ppermute | solution.py:728
  102.7 4.2 %out.1 = (f32[256,1024]{1,0:T(8,128)}, bf16[256,1024]{1,0:T(8,128)(2,1)}, bf16[256,16]{1,0:T(8,128)(2,1)}) custom-call(bf16[256,1024]{1,0:T(8,128)(2,1)} %bitcast.11, f32[2,1024]{1,0:T(2,128)} %get-tuple-element.179.refs_1_.refs_2_.refs_3_, bf16[16,1024]{1,0:T(8,128)(2,1)} %get-tuple-element.180.refs_2_.refs_3_, ...), custom_call_target="tpu_custom_call" | custom-call | flops 1 | bytes 1 | tf_op jit(solution)/shard_map/out/pallas_call | solution.py:136
  110.5 7.0 %collective-permute-done.23.refs_12_ = bf16[320,384]{1,0:T(8,128)(2,1)S(1)} collective-permute-done((bf16[320,384]{1,0:T(8,128)(2,1)S(1)}, bf16[320,384]{1,0:T(8,128)(2,1)S(1)}, u32[]{:S(2)}, u32[]{:S(2)}) %collective-permute-start.23) | collective-permute-done | bytes 245792 | tf_op jit(solution)/shard_map/ppermute | solution.py:775
  118.4 7.4 %mlp_pre.1 = (bf16[2,656,1024]{2,1,0:T(8,128)(2,1)}, bf16[656,1024]{1,0:T(8,128)(2,1)}, f32[2,256,656]{2,1,0:T(8,128)}, f32[2,256,656]{2,1,0:T(8,128)}) custom-call(bf16[16,1024]{1,0:T(8,128)(2,1)} %get-tuple-element.209.refs_0_.refs_1_, bf16[2,16,656]{2,1,0:T(8,128)(2,1)} %get-tuple-element.210.refs_1_.refs_2_, ...), custom_call_target="tpu_custom_call" | custom-call | flops 1 | bytes 1 | tf_op jit(solution)/shard_map/mlp_pre/pallas_call | solution.py:136
  126.6 7.2 %mlp.2 = (bf16[256,1024]{1,0:T(8,128)(2,1)}, bf16[256,1024]{1,0:T(8,128)(2,1)}, bf16[2,256,656]{2,1,0:T(8,128)(2,1)}, bf16[2,2,256,656]{3,2,1,0:T(8,128)(2,1)}) custom-call(bf16[2,656,1024]{2,1,0:T(8,128)(2,1)} %get-tuple-element.219.refs_0_, f32[2,256,656]{2,1,0:T(8,128)} %get-tuple-element.220.refs_1_, ...), custom_call_target="tpu_custom_call" | custom-call | flops 1 | bytes 1 | tf_op jit(solution)/shard_map/mlp/pallas_call | solution.py:136
  136.6 7.2 %mlp.3 = (bf16[256,1024]{1,0:T(8,128)(2,1)}, bf16[256,1024]{1,0:T(8,128)(2,1)}, bf16[2,256,656]{2,1,0:T(8,128)(2,1)}, bf16[2,2,256,656]{3,2,1,0:T(8,128)(2,1)}) custom-call(bf16[2,656,1024]{2,1,0:T(8,128)(2,1)} %get-tuple-element.219.refs_0_, f32[2,256,656]{2,1,0:T(8,128)} %get-tuple-element.226.refs_1_, bf16[256,1024]{1,0:T(8,128)(2,1)} %copy-done.4, ...), custom_call_target="tpu_custom_call" | custom-call | flops 1 | bytes 1 | tf_op jit(solution)/shard_map/mlp/pallas_call | solution.py:136
  150.1 9.2 %mlp_terms.1.refs_0_ = bf16[35,16,128]{2,1,0:T(8,128)(2,1)} custom-call(s32[1]{0:T(128)S(6)} %copy.31.refs_0_.refs_1_, bf16[16,1024]{1,0:T(8,128)(2,1)} %get-tuple-element.209.refs_0_.refs_1_, bf16[2,16,656]{2,1,0:T(8,128)(2,1)} %get-tuple-element.210.refs_1_.refs_2_, bf16[16,656]{1,0:T(8,128)(2,1)} %get-tuple-element.211.refs_2_.refs_3_, ...), custom_call_target="tpu_custom_call" | custom-call | flops 1 | bytes 1 | tf_op jit(solution)/shard_map/mlp_terms/pallas_call | solution.py:136
  160.2 4.5 %mlp_out.1 = (bf16[256,1024]{1,0:T(8,128)(2,1)}, bf16[256,1024]{1,0:T(8,128)(2,1)}, bf16[256,1024]{1,0:T(8,128)(2,1)}, bf16[256,1024]{1,0:T(8,128)(2,1)}) custom-call(bf16[656,1024]{1,0:T(8,128)(2,1)} %get-tuple-element.230.refs_0_, bf16[2,256,656]{2,1,0:T(8,128)(2,1)} %get-tuple-element.235.refs_5_.refs_1_, ...), custom_call_target="tpu_custom_call" | custom-call | flops 1 | bytes 1 | tf_op jit(solution)/shard_map/mlp_out/pallas_call | solution.py:136
  171.3 5.9 %out_back.1 = (f32[256,1024]{1,0:T(8,128)}, bf16[256,256]{1,0:T(8,128)(2,1)}, bf16[256,256]{1,0:T(8,128)(2,1)}, bf16[256,256]{1,0:T(8,128)(2,1)}, bf16[256,256]{...) custom-call(f32[256,1024]{1,0:T(8,128)} %get-tuple-element.207.refs_0_.refs_2_, ...), custom_call_target="tpu_custom_call" | custom-call | flops 1 | bytes 1 | tf_op jit(solution)/shard_map/out_back/pallas_call | solution.py:136
  179.1 4.8 %collective-permute-done.33.refs_15_ = bf16[256,256]{1,0:T(8,128)(2,1)S(1)} collective-permute-done((bf16[256,256]{1,0:T(8,128)(2,1)}, bf16[256,256]{1,0:T(8,128)(2,1)S(1)}, u32[]{:S(2)}, u32[]{:S(2)}) %collective-permute-start.33) | collective-permute-done | bytes 131104 | tf_op jit(solution)/shard_map/ppermute | solution.py:728
  187.5 16.5 %attend_back.1 = (bf16[3,1024,256]{2,1,0:T(8,128)(2,1)}, bf16[11,16,128]{2,1,0:T(8,128)(2,1)}, bf16[4,16,128]{2,1,0:T(8,128)(2,1)}) custom-call(s32[1,1024]{1,0:T(1,128)} %refs_5_.3, s32[1]{0:T(128)S(6)} %copy.31.refs_0_.refs_1_, bf16[1024,256]{1,0:T(8,128)(2,1)} %get-tuple-element.188.refs_1_.refs_2_, bf16[1024,256]{1,0:T(8,128)(2,1)} %get-tuple-element.189.refs_2_.refs_3_, ...), custom_call_target="tpu_custom_call" | custom-call | flops 1 | bytes 1 | tf_op jit(solution)/shard_map/attend_back/pallas_call | solution.py:136
  204.1 6.3 %collective-permute-done.37.refs_10_ = bf16[256,1024]{1,0:T(8,128)(2,1)S(1)} collective-permute-done((bf16[256,1024]{1,0:T(8,128)(2,1)S(1)}, bf16[256,1024]{1,0:T(8,128)(2,1)S(1)}, u32[]{:S(2)}, u32[]{:S(2)}) %collective-permute-start.37) | collective-permute-done | bytes 524320 | tf_op jit(solution)/shard_map/ppermute | solution.py:728
  210.4 3.0 %all-gather.11.cloned.1.call-done = bf16[432,16,128]{2,1,0:T(8,128)(2,1)} async-done(((bf16[54,16,128]{2,1,0:T(8,128)(2,1)}), bf16[432,16,128]{2,1,0:T(8,128)(2,1)}) %all-gather.11.cloned.1.call-update) | async-done | bytes 1769488 | tf_op jit(solution)/shard_map/all_gather | solution.py:1033
  214.0 2.9 %collective-permute-done.39.refs_3_ = bf16[8,16,128]{2,1,0:T(8,128)(2,1)S(1)} collective-permute-done((bf16[8,16,128]{2,1,0:T(8,128)(2,1)S(1)}, bf16[8,16,128]{2,1,0:T(8,128)(2,1)S(1)}, u32[]{:S(2)}, u32[]{:S(2)}) %collective-permute-start.39) | collective-permute-done | bytes 32800 | tf_op jit(solution)/shard_map/ppermute | solution.py:728
  219.5 4.6 %qkv_back.1 = (bf16[256,1024]{1,0:T(8,128)(2,1)}, bf16[256,1024]{1,0:T(8,128)(2,1)}, bf16[256,1024]{1,0:T(8,128)(2,1)}, bf16[256,1024]{1,0:T(8,128)(2,1)}) custom-call(bf16[3,1024,256]{2,1,0:T(8,128)(2,1)} %get-tuple-element.270.refs_0_, bf16[3,1024,256]{2,1,0:T(8,128)(2,1)} %get-tuple-element.271.refs_1_), custom_call_target="tpu_custom_call" | custom-call | flops 1 | bytes 1 | tf_op jit(solution)/shard_map/qkv_back/pallas_call | solution.py:136
  234.4 2.4 collective-permute-start.49
  238.9 6.9 %collective-permute-done.45.refs_6_ = bf16[256,1024]{1,0:T(8,128)(2,1)S(1)} collective-permute-done((bf16[256,1024]{1,0:T(8,128)(2,1)}, bf16[256,1024]{1,0:T(8,128)(2,1)S(1)}, u32[]{:S(2)}, u32[]{:S(2)}) %collective-permute-start.45) | collective-permute-done | bytes 524320 | tf_op jit(solution)/shard_map/ppermute | solution.py:728
  246.6 5.2 %last.1 = (bf16[256,1024]{1,0:T(8,128)(2,1)}, bf16[256,1024]{1,0:T(8,128)(2,1)}) custom-call(bf16[256,1024]{1,0:T(8,128)(2,1)} %bitcast.12, f32[256,1024]{1,0:T(8,128)} %get-tuple-element.243.refs_1_, f32[256,1024]{1,0:T(8,128)} %get-tuple-element.207.refs_0_.refs_2_, f32[2,1024]{1,0:T(2,128)} %get-tuple-element.179.refs_1_.refs_2_.refs_3_, ...), custom_call_target="tpu_custom_call" | custom-call | flops 1 | bytes 1 | tf_op jit(solution)/shard_map/last/pallas_call | solution.py:136
  253.0 6.4 %spread.2 = (f32[8,16,5248]{2,1,0:T(8,128)}, f32[8,16,2624]{2,1,0:T(8,128)}, f32[8,16,1024]{2,1,0:T(8,128)}, f32[8,16,1024]{2,1,0:T(8,128)}) custom-call(bf16[8,54,16,128]{3,2,1,0:T(8,128)(2,1)} %bitcast.17, bf16[8,54,16,128]{3,2,1,0:T(8,128)(2,1)} %copy-done.7), custom_call_target="tpu_custom_call" | custom-call | flops 1 | bytes 1 | tf_op jit(solution)/shard_map/spread/pallas_call | solution.py:136
  262.6 2.6 collective-permute-done.50.refs_1_
  266.1 4.6 %spread.3 = (f32[8,16,3072]{2,1,0:T(8,128)}, f32[8,16,1024]{2,1,0:T(8,128)}, f32[8,16,1024]{2,1,0:T(8,128)}, f32[8,16,1024]{2,1,0:T(8,128)}) custom-call(bf16[8,26,16,128]{3,2,1,0:T(8,128)(2,1)} %stack.1.refs_0_, bf16[8,26,16,128]{3,2,1,0:T(8,128)(2,1)} %copy-done.10), custom_call_target="tpu_custom_call" | custom-call | flops 1 | bytes 1 | tf_op jit(solution)/shard_map/spread/pallas_call | solution.py:136
  (227 shorter events, 76.1 us)
Async XLA Ops:
  7.2 59.6 %all-gather.7.cloned.1.call-start = ((), (), s32[]{:S(2)}) async-start(), calls=%async_computation | async-start | bytes 2785280 | tf_op jit(solution)/shard_map/all_gather | solution.py:928
  17.2 93.3 %all-gather.9.cloned.1.call-start = ((), (), s32[]{:S(2)}) async-start(), calls=%async_computation.1 | async-start | bytes 2621440 | tf_op jit(solution)/shard_map/all_gather | solution.py:929
  17.3 11.6 %collective-permute-start.3 = (bf16[256,512]{1,0:T(8,128)(2,1)S(1)}, bf16[256,512]{1,0:T(8,128)(2,1)S(1)}, u32[]{:S(2)}, u32[]{:S(2)}) collective-permute-start(bf16[256,512]{1,0:T(8,128)(2,1)S(1)} %constant_dynamic-update-slice_fusion.refs_6_), channel_id=1, source_target_pairs={{8,0},{16,8},{24,16},{28,24},{20,28},{12,20},{4,12},{0,4},{9,1},{1... | collective-permute-start | bytes 786440 | tf_op jit(solution)/shard_map/ppermute | solution.py:776
  22.7 8.3 %collective-permute-start.2 = (bf16[256,512]{1,0:T(8,128)(2,1)S(1)}, bf16[256,512]{1,0:T(8,128)(2,1)S(1)}, u32[]{:S(2)}, u32[]{:S(2)}) collective-permute-start(bf16[256,512]{1,0:T(8,128)(2,1)S(1)} %constant_dynamic-update-slice_fusion.refs_6_), channel_id=1, source_target_pairs={{0,8},{8,16},{16,24},{24,28},{28,20},{20,12},{12,4},{4,0},{1,9},{9... | collective-permute-start | bytes 786440 | tf_op jit(solution)/shard_map/ppermute | solution.py:775
  29.0 9.2 %collective-permute-start.5 = (bf16[256,512]{1,0:T(8,128)(2,1)S(1)}, bf16[256,512]{1,0:T(8,128)(2,1)S(1)}, u32[]{:S(2)}, u32[]{:S(2)}) collective-permute-start(bf16[256,512]{1,0:T(8,128)(2,1)S(1)} %collective-permute-done.3.refs_8_), channel_id=1, source_target_pairs={{8,0},{16,8},{24,16},{28,24},{20,28},{12,20},{4,12},{0,4},{9,1},{1... | collective-permute-start | bytes 786440 | tf_op jit(solution)/shard_map/ppermute | solution.py:776
  31.0 9.0 %collective-permute-start.4 = (bf16[256,512]{1,0:T(8,128)(2,1)S(1)}, bf16[256,512]{1,0:T(8,128)(2,1)S(1)}, u32[]{:S(2)}, u32[]{:S(2)}) collective-permute-start(bf16[256,512]{1,0:T(8,128)(2,1)S(1)} %collective-permute-done.2.refs_7_), channel_id=1, source_target_pairs={{0,8},{8,16},{16,24},{24,28},{28,20},{20,12},{12,4},{4,0},{1,9},{9... | collective-permute-start | bytes 786440 | tf_op jit(solution)/shard_map/ppermute | solution.py:775
  40.0 173.5 %all-gather.11.cloned.1.call-start = ((), (), s32[]{:S(2)}) async-start(), calls=%async_computation.2 | async-start | bytes 1990656 | tf_op jit(solution)/shard_map/all_gather | solution.py:1033
  40.0 19.1 %collective-permute-start.10 = (bf16[656,256]{1,0:T(8,128)(2,1)S(1)}, bf16[656,256]{1,0:T(8,128)(2,1)S(1)}, u32[]{:S(2)}, u32[]{:S(2)}) collective-permute-start(bf16[656,256]{1,0:T(8,128)(2,1)S(1)} %bitcast.20), channel_id=1, source_target_pairs={{0,0},{1,4},{2,8},{3,12},{4,1},{5,5},{6,9},{7,13},{8,2},{9,6},{10,... | collective-permute-start | bytes 1007624 | tf_op jit(solution)/shard_map/ppermute | solution.py:901
  40.7 13.6 %collective-permute-start.6 = (bf16[256,512]{1,0:T(8,128)(2,1)S(1)}, bf16[256,512]{1,0:T(8,128)(2,1)S(1)}, u32[]{:S(2)}, u32[]{:S(2)}) collective-permute-start(bf16[256,512]{1,0:T(8,128)(2,1)S(1)} %collective-permute-done.4.refs_9_), channel_id=1, source_target_pairs={{0,8},{8,16},{16,24},{24,28},{28,20},{20,12},{12,4},{4,0},{1,9},{9... | collective-permute-start | bytes 786440 | tf_op jit(solution)/shard_map/ppermute | solution.py:775
  45.9 13.1 %collective-permute-start.7 = (bf16[256,512]{1,0:T(8,128)(2,1)S(1)}, bf16[256,512]{1,0:T(8,128)(2,1)S(1)}, u32[]{:S(2)}, u32[]{:S(2)}) collective-permute-start(bf16[256,512]{1,0:T(8,128)(2,1)S(1)} %collective-permute-done.5.refs_10_), channel_id=1, source_target_pairs={{8,0},{16,8},{24,16},{28,24},{20,28},{12,20},{4,12},{0,4},{9,1},{1... | collective-permute-start | bytes 786440 | tf_op jit(solution)/shard_map/ppermute | solution.py:776
  64.7 12.3 %collective-permute-start.12 = (bf16[656,384]{1,0:T(8,128)(2,1)S(1)}, bf16[656,384]{1,0:T(8,128)(2,1)S(1)}, u32[]{:S(2)}, u32[]{:S(2)}) collective-permute-start(bf16[656,384]{1,0:T(8,128)(2,1)S(1)} %pad_maximum_fusion.refs_5_), channel_id=1, source_target_pairs={{8,0},{16,8},{24,16},{28,24},{20,28},{12,20},{4,12},{0,4},{9,1},{1... | collective-permute-start | bytes 1511432 | tf_op jit(solution)/shard_map/ppermute | solution.py:776
  64.7 12.3 %collective-permute-start.11 = (bf16[656,384]{1,0:T(8,128)(2,1)S(1)}, bf16[656,384]{1,0:T(8,128)(2,1)S(1)}, u32[]{:S(2)}, u32[]{:S(2)}) collective-permute-start(bf16[656,384]{1,0:T(8,128)(2,1)S(1)} %pad_maximum_fusion.refs_5_), channel_id=1, source_target_pairs={{0,8},{8,16},{16,24},{24,28},{28,20},{20,12},{12,4},{4,0},{1,9},{9... | collective-permute-start | bytes 1511432 | tf_op jit(solution)/shard_map/ppermute | solution.py:775
  75.7 13.3 %collective-permute-start.16 = (bf16[256,1024]{1,0:T(8,128)(2,1)}, bf16[256,1024]{1,0:T(8,128)(2,1)S(1)}, u32[]{:S(2)}, u32[]{:S(2)}) collective-permute-start(bf16[256,1024]{1,0:T(8,128)(2,1)} %get-tuple-element.204.refs_8_.refs_13_), channel_id=1, source_target_pairs={{0,2},{1,3},{2,0},{3,1},{4,6},{5,7},{6,4},{7,5},{8,10},{9,11},{10,... | collective-permute-start | bytes 1572872 | tf_op jit(solution)/shard_map/ppermute | solution.py:728
  77.0 12.1 %collective-permute-start.15 = (bf16[256,1024]{1,0:T(8,128)(2,1)}, bf16[256,1024]{1,0:T(8,128)(2,1)S(1)}, u32[]{:S(2)}, u32[]{:S(2)}) collective-permute-start(bf16[256,1024]{1,0:T(8,128)(2,1)} %get-tuple-element.204.refs_8_.refs_13_), channel_id=1, source_target_pairs={{0,1},{1,0},{2,3},{3,2},{4,5},{5,4},{6,7},{7,6},{8,9},{9,8},{10,11... | collective-permute-start | bytes 1572872 | tf_op jit(solution)/shard_map/ppermute | solution.py:728
  77.0 14.0 %collective-permute-start.13 = (bf16[656,384]{1,0:T(8,128)(2,1)S(1)}, bf16[656,384]{1,0:T(8,128)(2,1)}, u32[]{:S(2)}, u32[]{:S(2)}) collective-permute-start(bf16[656,384]{1,0:T(8,128)(2,1)S(1)} %collective-permute-done.11.refs_6_), channel_id=1, source_target_pairs={{0,8},{8,16},{16,24},{24,28},{28,20},{20,12},{12,4},{4,0},{1,9},{9... | collective-permute-start | bytes 1511432 | tf_op jit(solution)/shard_map/ppermute | solution.py:775
  77.7 13.5 %collective-permute-start.14 = (bf16[656,384]{1,0:T(8,128)(2,1)S(1)}, bf16[656,384]{1,0:T(8,128)(2,1)}, u32[]{:S(2)}, u32[]{:S(2)}) collective-permute-start(bf16[656,384]{1,0:T(8,128)(2,1)S(1)} %collective-permute-done.12.refs_7_), channel_id=1, source_target_pairs={{8,0},{16,8},{24,16},{28,24},{20,28},{12,20},{4,12},{0,4},{9,1},{1... | collective-permute-start | bytes 1511432 | tf_op jit(solution)/shard_map/ppermute | solution.py:776
  89.1 12.8 %collective-permute-start.20 = (bf16[256,1024]{1,0:T(8,128)(2,1)S(1)}, bf16[256,1024]{1,0:T(8,128)(2,1)S(1)}, u32[]{:S(2)}, u32[]{:S(2)}) collective-permute-start(bf16[256,1024]{1,0:T(8,128)(2,1)S(1)} %collective-permute-done.16.refs_10_.refs_15_), channel_id=1, source_target_pairs={{0,1},{1,0},{2,3},{3,2},{4,5},{5,4},{6,7},{7,6},{8,9},{9,8},{10,11... | collective-permute-start | bytes 1572872 | tf_op jit(solution)/shard_map/ppermute | solution.py:728
  91.2 15.7 %collective-permute-start.21 = (bf16[656,384]{1,0:T(8,128)(2,1)}, bf16[656,384]{1,0:T(8,128)(2,1)S(1)}, u32[]{:S(2)}, u32[]{:S(2)}) collective-permute-start(bf16[656,384]{1,0:T(8,128)(2,1)} %collective-permute-done.13.refs_8_), channel_id=1, source_target_pairs={{0,8},{8,16},{16,24},{24,28},{28,20},{20,12},{12,4},{4,0},{1,9},{9... | collective-permute-start | bytes 1511432 | tf_op jit(solution)/shard_map/ppermute | solution.py:775
  93.0 13.9 %collective-permute-start.22 = (bf16[656,384]{1,0:T(8,128)(2,1)}, bf16[656,384]{1,0:T(8,128)(2,1)S(1)}, u32[]{:S(2)}, u32[]{:S(2)}) collective-permute-start(bf16[656,384]{1,0:T(8,128)(2,1)} %collective-permute-done.14.refs_9_), channel_id=1, source_target_pairs={{8,0},{16,8},{24,16},{28,24},{20,28},{12,20},{4,12},{0,4},{9,1},{1... | collective-permute-start | bytes 1511432 | tf_op jit(solution)/shard_map/ppermute | solution.py:776
  106.9 18.9 %collective-permute-start.25 = (bf16[256,1024]{1,0:T(8,128)(2,1)}, bf16[256,1024]{1,0:T(8,128)(2,1)S(1)}, u32[]{:S(2)}, u32[]{:S(2)}) collective-permute-start(bf16[256,1024]{1,0:T(8,128)(2,1)} %get-tuple-element.221.refs_2_.refs_10_), channel_id=1, source_target_pairs={{0,1},{1,0},{2,3},{3,2},{4,5},{5,4},{6,7},{7,6},{8,9},{9,8},{10,11... | collective-permute-start | bytes 1572872 | tf_op jit(solution)/shard_map/ppermute | solution.py:728
  107.5 26.3 %collective-permute-start.26 = (bf16[256,1024]{1,0:T(8,128)(2,1)}, bf16[256,1024]{1,0:T(8,128)(2,1)S(1)}, u32[]{:S(2)}, u32[]{:S(2)}) collective-permute-start(bf16[256,1024]{1,0:T(8,128)(2,1)} %get-tuple-element.221.refs_2_.refs_10_), channel_id=1, source_target_pairs={{0,2},{1,3},{2,0},{3,1},{4,6},{5,7},{6,4},{7,5},{8,10},{9,11},{10,... | collective-permute-start | bytes 1572872 | tf_op jit(solution)/shard_map/ppermute | solution.py:728
  108.2 9.4 %collective-permute-start.24 = (bf16[336,384]{1,0:T(8,128)(2,1)S(1)}, bf16[336,384]{1,0:T(8,128)(2,1)S(1)}, u32[]{:S(2)}, u32[]{:S(2)}) collective-permute-start(bf16[336,384]{1,0:T(8,128)(2,1)S(1)} %slice.15), channel_id=1, source_target_pairs={{8,0},{16,8},{24,16},{28,24},{20,28},{12,20},{4,12},{0,4},{9,1},{1... | collective-permute-start | bytes 774152 | tf_op jit(solution)/shard_map/ppermute | solution.py:776
  148.8 19.7 %collective-permute-start.30 = (bf16[256,1024]{1,0:T(8,128)(2,1)}, bf16[256,1024]{1,0:T(8,128)(2,1)S(1)}, u32[]{:S(2)}, u32[]{:S(2)}) collective-permute-start(bf16[256,1024]{1,0:T(8,128)(2,1)} %add.16), channel_id=1, source_target_pairs={{0,2},{1,3},{2,0},{3,1},{4,6},{5,7},{6,4},{7,5},{8,10},{9,11},{10,... | collective-permute-start | bytes 1572872 | tf_op jit(solution)/shard_map/ppermute | solution.py:728
  185.6 18.4 %collective-permute-start.35 = (bf16[256,1024]{1,0:T(8,128)(2,1)}, bf16[256,1024]{1,0:T(8,128)(2,1)S(1)}, u32[]{:S(2)}, u32[]{:S(2)}) collective-permute-start(bf16[256,1024]{1,0:T(8,128)(2,1)} %get-tuple-element.262), channel_id=1, source_target_pairs={{0,1},{1,0},{2,3},{3,2},{4,5},{5,4},{6,7},{7,6},{8,9},{9,8},{10,11... | collective-permute-start | bytes 1572872 | tf_op jit(solution)/shard_map/ppermute | solution.py:728
  186.0 18.1 %collective-permute-start.36 = (bf16[256,1024]{1,0:T(8,128)(2,1)S(1)}, bf16[256,1024]{1,0:T(8,128)(2,1)S(1)}, u32[]{:S(2)}, u32[]{:S(2)}) collective-permute-start(bf16[256,1024]{1,0:T(8,128)(2,1)S(1)} %copy-done.52), channel_id=1, source_target_pairs={{0,2},{1,3},{2,0},{3,1},{4,6},{5,7},{6,4},{7,5},{8,10},{9,11},{10,... | collective-permute-start | bytes 1572872 | tf_op jit(solution)/shard_map/ppermute | solution.py:728
  187.2 23.2 %collective-permute-start.37 = (bf16[256,1024]{1,0:T(8,128)(2,1)S(1)}, bf16[256,1024]{1,0:T(8,128)(2,1)S(1)}, u32[]{:S(2)}, u32[]{:S(2)}) collective-permute-start(bf16[256,1024]{1,0:T(8,128)(2,1)S(1)} %copy-done.51), channel_id=1, source_target_pairs={{0,3},{1,2},{2,1},{3,0},{4,7},{5,6},{6,5},{7,4},{8,11},{9,10},{10,... | collective-permute-start | bytes 1572872 | tf_op jit(solution)/shard_map/ppermute | solution.py:728
  213.5 38.3 %collective-permute-start.46 = (bf16[8,54,16,128]{3,2,1,0:T(8,128)(2,1)}, bf16[8,54,16,128]{3,2,1,0:T(8,128)(2,1)S(1)}, u32[]{:S(2)}, u32[]{:S(2)}) collective-permute-start(bf16[8,54,16,128]{3,2,1,0:T(8,128)(2,1)} %bitcast.16), channel_id=1, source_target_pairs={{0,1},{1,0},{2,3},{3,2},{4,5},{5,4},{6,7},{7,6},{8,9},{9,8},{10,11... | collective-permute-start | bytes 5308424 | tf_op jit(solution)/shard_map/ppermute | solution.py:728
  224.3 13.7 %collective-permute-start.40 = (bf16[256,1024]{1,0:T(8,128)(2,1)}, bf16[256,1024]{1,0:T(8,128)(2,1)S(1)}, u32[]{:S(2)}, u32[]{:S(2)}) collective-permute-start(bf16[256,1024]{1,0:T(8,128)(2,1)} %get-tuple-element.273), channel_id=1, source_target_pairs={{0,1},{1,0},{2,3},{3,2},{4,5},{5,4},{6,7},{7,6},{8,9},{9,8},{10,11... | collective-permute-start | bytes 1572872 | tf_op jit(solution)/shard_map/ppermute | solution.py:728
  232.0 13.8 %collective-permute-start.45 = (bf16[256,1024]{1,0:T(8,128)(2,1)}, bf16[256,1024]{1,0:T(8,128)(2,1)S(1)}, u32[]{:S(2)}, u32[]{:S(2)}) collective-permute-start(bf16[256,1024]{1,0:T(8,128)(2,1)} %add.17), channel_id=1, source_target_pairs={{0,2},{1,3},{2,0},{3,1},{4,6},{5,7},{6,4},{7,5},{8,10},{9,11},{10,... | collective-permute-start | bytes 1572872 | tf_op jit(solution)/shard_map/ppermute | solution.py:728
  234.4 25.0 %collective-permute-start.49 = (bf16[2,26,16,128]{3,2,1,0:T(8,128)(2,1)}, bf16[2,26,16,128]{3,2,1,0:T(8,128)(2,1)S(1)}, u32[]{:S(2)}, u32[]{:S(2)}) collective-permute-start(bf16[2,26,16,128]{3,2,1,0:T(8,128)(2,1)} %merge.1.refs_0_), channel_id=1, source_target_pairs={{0,24},{4,28},{8,16},{12,20},{16,8},{20,12},{24,0},{28,4},{1,25},{... | collective-permute-start | bytes 638984 | tf_op jit(solution)/shard_map/ppermute | solution.py:1129
  236.8 22.7 %collective-permute-start.48 = (bf16[2,26,16,128]{3,2,1,0:T(8,128)(2,1)}, bf16[2,26,16,128]{3,2,1,0:T(8,128)(2,1)S(1)}, u32[]{:S(2)}, u32[]{:S(2)}) collective-permute-start(bf16[2,26,16,128]{3,2,1,0:T(8,128)(2,1)} %merge.1.refs_0_), channel_id=1, source_target_pairs={{0,16},{4,20},{8,24},{12,28},{16,0},{20,4},{24,8},{28,12},{1,17},{... | collective-permute-start | bytes 638984 | tf_op jit(solution)/shard_map/ppermute | solution.py:1129
  238.0 21.5 %collective-permute-start.47 = (bf16[2,26,16,128]{3,2,1,0:T(8,128)(2,1)}, bf16[2,26,16,128]{3,2,1,0:T(8,128)(2,1)S(1)}, u32[]{:S(2)}, u32[]{:S(2)}) collective-permute-start(bf16[2,26,16,128]{3,2,1,0:T(8,128)(2,1)} %merge.1.refs_0_), channel_id=1, source_target_pairs={{0,8},{4,12},{8,0},{12,4},{16,24},{20,28},{24,16},{28,20},{1,9},{5... | collective-permute-start | bytes 638984 | tf_op jit(solution)/shard_map/ppermute | solution.py:1129
  (78 other events, 670.6 us)
Sparse Core Ops, SparseCore 0:
  17.3 27.8 all-gather.6
  46.8 29.7 all-gather.8
  168.7 44.7 all-gather.10

commit v3 on v2

--- a/solution.py
+++ b/solution.py
@@ -630,19 +630,15 @@
         outs[n].send()
 
 
-def last_kernel(parts, out_parts, inputs, grad_mid, middle, gain, *refs):
-    backs, outs = refs[:parts], refs[parts : parts + out_parts]
-    input_grad, layer_out = refs[parts + out_parts :]
-    total = middle.get()[...] + sum(ref.get()[...].astype(F32) for ref in outs)
-    layer_out.ref[...] = total.astype(BF16)
-    layer_out.send()
-    total = sum(ref.get()[...].astype(F32) for ref in backs)
+def layer_kernel(middle, *refs):
+    total = middle.get()[...] + sum(ref.get()[...].astype(F32) for ref in refs[:-1])
+    refs[-1][...] = total.astype(BF16)
+
+
+def last_kernel(inputs, grad_mid, gain, *refs):
+    total = sum(ref.get()[...].astype(F32) for ref in refs[:-1])
     back = norm_back(inputs.get()[...].astype(F32), gain.get()[0:1, :], total)
-    input_grad.ref[...] = (grad_mid.get()[...] + back).astype(BF16)
-
-
-def add_kernel(one, two, out):
-    out[...] = (one.get()[...].astype(F32) + two.get()[...].astype(F32)).astype(out.dtype)
+    refs[-1][...] = (grad_mid.get()[...] + back).astype(BF16)
 
 
 def pair_kernel(local, own, came, out):
@@ -663,32 +659,28 @@
     out[local + half :] = total.astype(BF16)
 
 
-def merge_kernel(local, own, across, beside, diagonal, out):
-    row, place = lax.axis_index("tok") // 2, lax.rem(lax.axis_index("seq"), 2)
-    for n, one, two in ((place, own, across), (1 - place, beside, diagonal)):
-        one, two = one.get(), two.get()
-        out[n, pl.ds(row * local, local)] = one[:local]
-        out[n, pl.ds((1 - row) * local, local)] = two[:local]
-        out[n, 2 * local :] = (one[local:].astype(F32) + two[local:].astype(F32)).astype(BF16)
-
-
 def stack_kernel(*refs):
     out = refs[-1]
-    own = lax.axis_index("seq") // 2
+    first = 0
     for n, ref in enumerate(refs[:-1]):
         block = ref.get()
         size = block.shape[0]
-        out[pl.ds(jnp.bitwise_xor(own, n) * size, size)] = block[...]
-
-
-def spread_kernel(widths, local, mine, other, *refs):
+        out[came_from(n), first : first + size] = block[...]
+        first = (first + size) % out.shape[1]
+
+
+def spread_kernel(widths, local, count, *refs):
+    mine, other, refs = refs[:count], refs[count : 2 * count], refs[2 * count :]
     outs, both = refs[: len(widths)], refs[len(widths)]
     core = lax.rem(lax.axis_index("tok"), 2)
+    own = lax.axis_index("seq") // 2
+    for n in range(count):
+        size = mine[n].get().shape[0]
+        at = pl.ds(jnp.bitwise_xor(own, n) * size, size) if count > 1 else slice(None)
+        both[core, at] = mine[n].get()[...]
+        both[1 - core, at] = other[n].get()[...]
     for out in outs:
         out[...] = jnp.zeros_like(out)
-    mine, other = mine.get(), other.get()
-    both[core] = mine[...]
-    both[1 - core] = other[...]
 
     def step(n, _):
         pick = jnp.max(both[0, n, local - 1].astype(F32)).astype(jnp.int32)
@@ -715,7 +707,7 @@
                 at += blocks
         return 0
 
-    lax.fori_loop(0, mine.shape[0], step, 0)
+    lax.fori_loop(0, both.shape[1], step, 0)
 
 
 class Exchange:
@@ -746,7 +738,7 @@
 
     def halve(self, slots):
         near, far = self.swap(slots[1], 1), self.swap(slots[3], 1)
-        both = call(add_kernel, [shape(far.shape, far.dtype)], [slots[2], far], name="add")[0]
+        both = (slots[2].astype(F32) + far.astype(F32)).astype(far.dtype)
         return near, both
 
     def reduce(self, slots):
@@ -764,7 +756,7 @@
     def __init__(self, block):
         self.blocks = [block]
         self.right = self.left = block
-        self.half = block.shape[0] // 32 * 16
+        self.half = block.shape[0] // 32 * 16 if block.ndim == 2 else block.shape[0] // 2
         self.ahead = [(RING[n], RING[(n + 1) % len(RING)]) for n in range(len(RING))]
         self.behind = [(b, a) for a, b in self.ahead]
 
@@ -886,19 +878,19 @@
                 for t in range(tok)
             ]
             parts[n] = lax.ppermute(parts[n], ("seq", "tok"), pairs)
-        together = meet(token_block, cosine, sine, *adapters_own, *parts)
-        token_block, cosine, sine, adapters_own = *together[:3], together[3:11]
-        parts = list(together[11:])
-        ring = Ring(jnp.concatenate(parts + [out_weight], axis=1))
-        ring.step()
-        ring.step()
-        in_piece, out_grad_in = ring.meet(in_weight.T, out_grad)
         pairs = [
             (s * tok + t, ((s // tok) * tok + t) * tok + s % tok)
             for s in range(seq)
             for t in range(tok)
         ]
-        in_piece = lax.ppermute(in_piece, ("seq", "tok"), pairs)
+        in_piece = lax.ppermute(in_weight.T, ("seq", "tok"), pairs)
+        together = meet(token_block, cosine, sine, *adapters_own, in_piece, *parts)
+        token_block, cosine, sine, adapters_own = *together[:3], together[3:11]
+        in_piece, *parts = together[11:]
+        ring = Ring(jnp.concatenate(parts + [out_weight], axis=1))
+        ring.step()
+        ring.step()
+        (out_grad_in,) = ring.meet(out_grad)
         ring.step()
         ring.step()
         mlp_piece = jnp.concatenate([in_piece, out2_weight], axis=1)
@@ -1029,8 +1021,6 @@
             [early, move.swap(early, 2)],
             name="pair",
         )[0]
-        back_two[2], early = meet(back_two[2], early)
-        early = lax.all_gather(early, "seq", axis=0)
     grad_mid, *rest = call(
         functools.partial(out_back_kernel, tok, len(back_two), direct),
         [shape((rows, width), F32)]
@@ -1043,7 +1033,8 @@
     out_keep, out_send = rest[tok:]
     attn_grads = move.turn(rest[:tok])
     if fast:
-        attn_grads, out_slots = meet(attn_grads, out_slots)
+        attn_grads, out_slots, early = meet(attn_grads, out_slots, early)
+        early = lax.all_gather(early, "seq", axis=0)
     out_parts = move.turn(out_slots) if fast else move.reduce(out_slots)
     grad_qkv, keep, send = call(
         functools.partial(attend_back_kernel, tok, direct),
@@ -1077,69 +1068,69 @@
             name="qkv_back",
         )
 
+    def layer_of(out_parts):
+        output = [shape((rows, width), BF16)]
+        return call(layer_kernel, output, [middle] + out_parts, name="layer")[0]
+
     def last_of(back_one):
         return call(
-            functools.partial(last_kernel, len(back_one), len(out_parts)),
-            [shape((rows, width), BF16)] * 2,
-            [inputs, grad_mid, middle, gain] + back_one + out_parts,
-            early=(0, 1),
+            last_kernel,
+            [shape((rows, width), BF16)],
+            [inputs, grad_mid, gain] + back_one,
             name="last",
-        )
+        )[0]
 
     grads = lambda columns: shape((adapters, rank, columns), F32)
     if fast:
 
-        def spread(whole, local, widths, columns):
+        def spread(parts, local, widths, columns):
             return call(
-                functools.partial(spread_kernel, widths, local),
+                functools.partial(spread_kernel, widths, local, len(parts)),
                 [grads(size) for size in columns],
-                [whole, move.swap(whole, 1)],
-                scratch=[pltpu.VMEM((2,) + whole.shape, BF16)],
+                parts + [move.swap(part, 1) for part in parts],
+                scratch=[pltpu.VMEM((2, seq) + parts[0].shape[1:], BF16)],
                 name="spread",
             )
 
-        keep, early, *out_parts = meet(keep, early, *out_parts)
+        keep, *out_parts = meet(keep, *out_parts)
+        layer_out = layer_of(out_parts)
         late = call(
             functools.partial(late_kernel, late_local),
             [shape((late_local + 3 * wide // 2, rank, 128), BF16)],
             [keep, move.swap(send, 1), out_keep, move.swap(out_send, 1)],
             name="late",
         )[0]
-        diagonal = [(s * tok + t, (s ^ 1) * tok + (t ^ 2)) for s in range(seq) for t in range(tok)]
-        came = [
-            late,
-            move.swap(late, 2),
-            lax.ppermute(late, "seq", [(s, s ^ 1) for s in range(seq)]),
-            lax.ppermute(late, ("seq", "tok"), diagonal),
-        ]
+        late_came = move.swap(late, 2)
         late, grad_qkv = meet(late, grad_qkv)
         one_slots = slots_of_one(grad_qkv)
         near, both = move.halve(one_slots)
-        both, *came = meet(both, *came)
+        both, late_came = meet(both, late_came)
         back_one = [one_slots[0], near, move.swap(both, 2)]
-        merged = call(
-            functools.partial(merge_kernel, late_local),
-            [shape((2, late_local + late.shape[0], rank, 128), BF16)],
-            came,
-            name="merge",
+        late = call(
+            functools.partial(pair_kernel, late_local),
+            [shape((late_local + late.shape[0], rank, 128), BF16)],
+            [late, late_came],
+            name="pair_late",
         )[0]
-        blocks = [merged]
-        for bits in (2, 4, 6):
-            pairs = [(s, s ^ bits) for s in range(seq)]
-            blocks.append(lax.ppermute(merged, "seq", pairs))
+        ring = Ring(late)
+        ring.step()
+        layer_out, back_one[2] = ring.meet(layer_out, back_one[2])
+        ring.step()
+        input_grad, early = ring.meet(last_of(back_one), early)
+        ring.step()
+        ring.step()
         in_up_grad, out2_down_grad, in_down_grad, out2_up_grad = spread(
-            early, early_local, (hidden, hidden, 0, 0), (2 * hidden_all, hidden_all, width, width)
+            [early], early_local, (hidden, hidden, 0, 0), (2 * hidden_all, hidden_all, width, width)
         )
-        input_grad, layer_out = last_of(back_one)
-        in_up_grad, input_grad, *blocks = meet(in_up_grad, input_grad, *blocks)
-        late = call(
-            stack_kernel, [shape((seq,) + merged.shape[1:], BF16)], blocks, name="stack"
-        )[0]
+        (in_up_grad,) = ring.meet(in_up_grad)
+        stacked = shape((seq,) + late.shape, BF16)
+        blocks = list(call(stack_kernel, [stacked], ring.blocks, name="stack"))
         qkv_up_grad, qkv_down_grad, out_down_grad, out_up_grad = spread(
-            late, late_local, (lanes, -1, -1, -1), (3 * width, width, width, width)
+            blocks, late_local, (lanes, -1, -1, -1), (3 * width, width, width, width)
         )
     else:
-        input_grad, layer_out = last_of(move.reduce(slots_of_one(grad_qkv)))
+        layer_out = layer_of(out_parts)
+        input_grad = last_of(move.reduce(slots_of_one(grad_qkv)))
         picked = (pick == jnp.arange(adapters)).astype(F32)[:, None, None]
 
         def term(blocks, columns):

time: 277 us -> 267 us (0.964)
  waiting for transfers between devices: 86.5 us -> 67.4 us
  starting transfers between devices: 44.4 us -> 47.9 us
  Pallas kernels: 117 us -> 120 us
    ppermute x27, waiting for transfers between devices: 40.8 us -> 23.2 us  [swap(): return lax.ppermute(block, 'tok', pairs)]
    ppermute x6 -> x1, starting transfers between devices: 8.06 us -> 1.63 us  [body(): in_piece = lax.ppermute(in_weight.T, ('seq', 'tok'), pairs)]
    ppermute x8 -> x12, starting transfers between devices: 11.4 us -> 17.6 us  [step(): self.right = lax.ppermute(self.right, 'seq', self.ahead)]
    ppermute x2, waiting for transfers between devices: 0.01 us -> 4.66 us  [body(): parts[n] = lax.ppermute(parts[n], ('seq', 'tok'), pairs)]
    all_gather x1, waiting for transfers between devices: 3.04 us -> 0.01 us  [body(): early = lax.all_gather(early, 'seq', axis=0)]
    ppermute x8 -> x12, waiting for transfers between devices: 22 us -> 19 us  [step(): self.right = lax.ppermute(self.right, 'seq', self.ahead)]
    ppermute x2, starting transfers between devices: 2.06 us -> 4.98 us  [body(): parts[n] = lax.ppermute(parts[n], ('seq', 'tok'), pairs)]
    pallas_call x22 -> x21, Pallas kernels: 117 us -> 120 us  [call(): pl.pallas_call(body, out_shape=list(out_shape), in_specs=[pl.BlockSpec(me...]
  transfers between devices with their start and end apart: 54 -> 57, of which waited for: 28 -> 24; matrix products, arithmetic and copies ran while one was open for 1% -> 2% of each run, Pallas kernels for 36% -> 40%
where the time goes in v3:
time: 267 us; the launch traced here: 266 us
  Pallas kernels  120 us (45%)
  waiting for transfers between devices  67.4 us (25%)
  starting transfers between devices  47.9 us (18%)
  between operations  15.3 us (6%)
  local copies, waits for them, and re-layouts  10.1 us (4%)
  other arithmetic  5.6 us (2%)
    pallas_call x21, Pallas kernels, call(): pl.pallas_call(body, out_shape=list(out_shape), in_specs=[pl.BlockSpec(me...  120 us
    ppermute x27, waiting for transfers between devices, swap(): return lax.ppermute(block, 'tok', pairs)  23.2 us
    ppermute x12, waiting for transfers between devices, step(): self.left = lax.ppermute(self.left, 'seq', self.behind)  20.5 us
    ppermute x12, waiting for transfers between devices, step(): self.right = lax.ppermute(self.right, 'seq', self.ahead)  19 us
    ppermute x12, starting transfers between devices, step(): self.right = lax.ppermute(self.right, 'seq', self.ahead)  17.6 us
    ppermute x27, starting transfers between devices, swap(): return lax.ppermute(block, 'tok', pairs)  14.8 us
    unnamed x116, local copies, waits for them, and re-layouts  9.96 us
    ppermute x12, starting transfers between devices, step(): self.left = lax.ppermute(self.left, 'seq', self.behind)  8.82 us
  transfers between devices with their start and end apart: 57, of which 24 were waited for; matrix products, arithmetic and copies ran while one was open for 2% of the time, Pallas kernels for 40%

profile of v3, /device:TPU:0, one launch (start us, length us, event | category | flops | bytes accessed | tf_op | source)
XLA Modules:
  0.0 266.1 jit_solution(13679286857739133378)
XLA Ops:
  10.9 3.4 %collective-permute-start.2 = (bf16[256,128]{1,0:T(8,128)(2,1)}, bf16[256,128]{1,0:T(8,128)(2,1)S(1)}, u32[]{:S(2)}, u32[]{:S(2)}) collective-permute-start(bf16[256,128]{1,0:T(8,128)(2,1)} %get-tuple-element.165), channel_id=1, source_target_pairs={{0,1},{1,5},{2,9},{3,13},{4,17},{5,21},{6,25},{7,29},{8,0},{9,4},{... | collective-permute-start | bytes 196616 | tf_op jit(solution)/shard_map/ppermute | solution.py:880
  16.0 3.1 %fusion = (f32[1024,128]{1,0:T(8,128)}, f32[1024,128]{1,0:T(8,128)}) fusion(f32[128]{0:T(128)S(1)} %compare_select_fusion, f32[128]{0:T(128)S(1)} %mul.46, f32[1024]{0:T(1024)S(1)} %iota_convert_fusion), kind=kLoop, calls=%fused_computation.4 | loop fusion | flops 262144 | bytes 1053696 | tf_op jit(solution)/shard_map/mul | solution.py:858
  21.7 4.7 %collective-permute-done.2 = bf16[256,128]{1,0:T(8,128)(2,1)S(1)} collective-permute-done((bf16[256,128]{1,0:T(8,128)(2,1)}, bf16[256,128]{1,0:T(8,128)(2,1)S(1)}, u32[]{:S(2)}, u32[]{:S(2)}) %collective-permute-start.2) | collective-permute-done | bytes 65568 | tf_op jit(solution)/shard_map/ppermute | solution.py:880
  29.9 6.0 %collective-permute-done.5.refs_8_ = bf16[256,512]{1,0:T(8,128)(2,1)S(1)} collective-permute-done((bf16[256,512]{1,0:T(8,128)(2,1)S(1)}, bf16[256,512]{1,0:T(8,128)(2,1)S(1)}, u32[]{:S(2)}, u32[]{:S(2)}) %collective-permute-start.5) | collective-permute-done | bytes 262176 | tf_op jit(solution)/shard_map/ppermute | solution.py:768
  38.0 5.3 %collective-permute-done.6.refs_10_ = bf16[256,512]{1,0:T(8,128)(2,1)S(1)} collective-permute-done((bf16[256,512]{1,0:T(8,128)(2,1)S(1)}, bf16[256,512]{1,0:T(8,128)(2,1)S(1)}, u32[]{:S(2)}, u32[]{:S(2)}) %collective-permute-start.6) | collective-permute-done | bytes 262176 | tf_op jit(solution)/shard_map/ppermute | solution.py:768
  47.6 5.0 %collective-permute-done.7.refs_11_ = bf16[256,512]{1,0:T(8,128)(2,1)S(1)} collective-permute-done((bf16[256,512]{1,0:T(8,128)(2,1)S(1)}, bf16[256,512]{1,0:T(8,128)(2,1)S(1)}, u32[]{:S(2)}, u32[]{:S(2)}) %collective-permute-start.7) | collective-permute-done | bytes 262176 | tf_op jit(solution)/shard_map/ppermute | solution.py:767
  54.9 2.8 %collective-permute-done.8.refs_13_ = bf16[128,512]{1,0:T(8,128)(2,1)S(1)} collective-permute-done((bf16[128,512]{1,0:T(8,128)(2,1)S(1)}, bf16[128,512]{1,0:T(8,128)(2,1)S(1)}, u32[]{:S(2)}, u32[]{:S(2)}) %collective-permute-start.8) | collective-permute-done | bytes 131104 | tf_op jit(solution)/shard_map/ppermute | solution.py:767
  57.7 4.1 %collective-permute-done.10.refs_14_ = bf16[128,512]{1,0:T(8,128)(2,1)S(1)} collective-permute-done((bf16[128,512]{1,0:T(8,128)(2,1)S(1)}, bf16[128,512]{1,0:T(8,128)(2,1)S(1)}, u32[]{:S(2)}, u32[]{:S(2)}) %collective-permute-start.10) | collective-permute-done | bytes 131104 | tf_op jit(solution)/shard_map/ppermute | solution.py:768
  64.6 8.9 %qkv.1 = (bf16[1024,1024]{1,0:T(8,128)(2,1)}, f32[2,1024]{1,0:T(2,128)}, bf16[1024,256]{1,0:T(8,128)(2,1)}, bf16[1024,256]{1,0:T(8,128)(2,1)}, bf16[1024,256]{1,...) custom-call(s32[12]{0:T(128)} %constant.32.clone.refs_0_, bf16[4,272,1024]{2,1,0:T(8,128)(2,1)} %bitcast.13, ...), custom_call_target="tpu_custom_call" | custom-call | flops 1 | bytes 1 | tf_op jit(solution)/shard_map/qkv/pallas_call | solution.py:136
  75.7 12.7 %attend.1 = (bf16[256,256]{1,0:T(8,128)(2,1)}, bf16[256,256]{1,0:T(8,128)(2,1)}, bf16[256,256]{1,0:T(8,128)(2,1)}, bf16[256,256]{1,0:T(8,128)(2,1)}, f32[4,1024]{1,0:T(4,128)}, /*index=5*/f32[4,256,256]{2,1,0:T(8,128)}) custom-call(s32[1,1024]{1,0:T(1,128)} %refs_5_.3, bf16[1024,256]{1,0:T(8,128)(2,1)} %get-tuple-element.182.refs_1_.refs_2_, ...), custom_call_target="tpu_custom_call" | custom-call | flops 1 | bytes 1 | tf_op jit(solution)/shard_map/attend/pallas_call | solution.py:136
  94.8 3.3 %collective-permute-done.18.refs_6_.refs_11_ = bf16[256,256]{1,0:T(8,128)(2,1)S(1)} collective-permute-done((bf16[256,256]{1,0:T(8,128)(2,1)}, bf16[256,256]{1,0:T(8,128)(2,1)S(1)}, u32[]{:S(2)}, u32[]{:S(2)}) %collective-permute-start.18) | collective-permute-done | bytes 131104 | tf_op jit(solution)/shard_map/ppermute | solution.py:720
  98.2 2.3 collective-permute-done.19.refs_7_.refs_12_
  101.3 4.2 %out.1 = (f32[256,1024]{1,0:T(8,128)}, bf16[256,1024]{1,0:T(8,128)(2,1)}, bf16[256,16]{1,0:T(8,128)(2,1)}) custom-call(bf16[256,1024]{1,0:T(8,128)(2,1)} %bitcast.11, f32[2,1024]{1,0:T(2,128)} %get-tuple-element.188.refs_1_.refs_2_, bf16[16,1024]{1,0:T(8,128)(2,1)} %get-tuple-element.189.refs_2_.refs_3_, ...), custom_call_target="tpu_custom_call" | custom-call | flops 1 | bytes 1 | tf_op jit(solution)/shard_map/out/pallas_call | solution.py:136
  110.2 5.6 %collective-permute-done.23.refs_12_ = bf16[320,384]{1,0:T(8,128)(2,1)S(1)} collective-permute-done((bf16[320,384]{1,0:T(8,128)(2,1)S(1)}, bf16[320,384]{1,0:T(8,128)(2,1)S(1)}, u32[]{:S(2)}, u32[]{:S(2)}) %collective-permute-start.23) | collective-permute-done | bytes 245792 | tf_op jit(solution)/shard_map/ppermute | solution.py:767
  116.8 7.4 %mlp_pre.1 = (bf16[2,656,1024]{2,1,0:T(8,128)(2,1)}, bf16[656,1024]{1,0:T(8,128)(2,1)}, f32[2,256,656]{2,1,0:T(8,128)}, f32[2,256,656]{2,1,0:T(8,128)}) custom-call(bf16[16,1024]{1,0:T(8,128)(2,1)} %get-tuple-element.211.refs_0_.refs_1_, bf16[2,16,656]{2,1,0:T(8,128)(2,1)} %get-tuple-element.212.refs_1_.refs_2_, ...), custom_call_target="tpu_custom_call" | custom-call | flops 1 | bytes 1 | tf_op jit(solution)/shard_map/mlp_pre/pallas_call | solution.py:136
  125.0 7.2 %mlp.2 = (bf16[256,1024]{1,0:T(8,128)(2,1)}, bf16[256,1024]{1,0:T(8,128)(2,1)}, bf16[2,256,656]{2,1,0:T(8,128)(2,1)}, bf16[2,2,256,656]{3,2,1,0:T(8,128)(2,1)}) custom-call(bf16[2,656,1024]{2,1,0:T(8,128)(2,1)} %get-tuple-element.221.refs_0_, f32[2,256,656]{2,1,0:T(8,128)} %get-tuple-element.222.refs_1_, ...), custom_call_target="tpu_custom_call" | custom-call | flops 1 | bytes 1 | tf_op jit(solution)/shard_map/mlp/pallas_call | solution.py:136
  135.0 7.1 %mlp.3 = (bf16[256,1024]{1,0:T(8,128)(2,1)}, bf16[256,1024]{1,0:T(8,128)(2,1)}, bf16[2,256,656]{2,1,0:T(8,128)(2,1)}, bf16[2,2,256,656]{3,2,1,0:T(8,128)(2,1)}) custom-call(bf16[2,656,1024]{2,1,0:T(8,128)(2,1)} %get-tuple-element.221.refs_0_, f32[2,256,656]{2,1,0:T(8,128)} %get-tuple-element.228.refs_1_, bf16[256,1024]{1,0:T(8,128)(2,1)} %copy-done.4, ...), custom_call_target="tpu_custom_call" | custom-call | flops 1 | bytes 1 | tf_op jit(solution)/shard_map/mlp/pallas_call | solution.py:136
  146.0 9.2 %mlp_terms.1.refs_0_ = bf16[35,16,128]{2,1,0:T(8,128)(2,1)} custom-call(s32[1]{0:T(128)S(6)} %copy.31.refs_0_.refs_1_, bf16[16,1024]{1,0:T(8,128)(2,1)} %get-tuple-element.211.refs_0_.refs_1_, bf16[2,16,656]{2,1,0:T(8,128)(2,1)} %get-tuple-element.212.refs_1_.refs_2_, bf16[16,656]{1,0:T(8,128)(2,1)} %get-tuple-element.213.refs_2_.refs_3_, ...), custom_call_target="tpu_custom_call" | custom-call | flops 1 | bytes 1 | tf_op jit(solution)/shard_map/mlp_terms/pallas_call | solution.py:136
  157.0 4.4 %mlp_out.1 = (bf16[256,1024]{1,0:T(8,128)(2,1)}, bf16[256,1024]{1,0:T(8,128)(2,1)}, bf16[256,1024]{1,0:T(8,128)(2,1)}, bf16[256,1024]{1,0:T(8,128)(2,1)}) custom-call(bf16[656,1024]{1,0:T(8,128)(2,1)} %get-tuple-element.232.refs_0_, bf16[2,256,656]{2,1,0:T(8,128)(2,1)} %get-tuple-element.237.refs_5_.refs_1_, ...), custom_call_target="tpu_custom_call" | custom-call | flops 1 | bytes 1 | tf_op jit(solution)/shard_map/mlp_out/pallas_call | solution.py:136
  162.4 5.9 %out_back.1 = (f32[256,1024]{1,0:T(8,128)}, bf16[256,256]{1,0:T(8,128)(2,1)}, bf16[256,256]{1,0:T(8,128)(2,1)}, bf16[256,256]{1,0:T(8,128)(2,1)}, bf16[256,256]{...) custom-call(f32[256,1024]{1,0:T(8,128)} %get-tuple-element.209.refs_0_, ...), custom_call_target="tpu_custom_call" | custom-call | flops 1 | bytes 1 | tf_op jit(solution)/shard_map/out_back/pallas_call | solution.py:136
  172.6 2.5 collective-permute-done.32.refs_15_
  179.3 19.7 %attend_back.1 = (bf16[3,1024,256]{2,1,0:T(8,128)(2,1)}, bf16[11,16,128]{2,1,0:T(8,128)(2,1)}, bf16[4,16,128]{2,1,0:T(8,128)(2,1)}) custom-call(s32[1,1024]{1,0:T(1,128)} %refs_5_.3, s32[1]{0:T(128)S(6)} %copy.31.refs_0_.refs_1_, bf16[1024,256]{1,0:T(8,128)(2,1)} %get-tuple-element.182.refs_1_.refs_2_, bf16[1024,256]{1,0:T(8,128)(2,1)} %get-tuple-element.183.refs_2_.refs_3_, ...), custom_call_target="tpu_custom_call" | custom-call | flops 1 | bytes 1 | tf_op jit(solution)/shard_map/attend_back/pallas_call | solution.py:136
  199.2 2.2 collective-permute-done.37.refs_4_
  203.7 4.6 %qkv_back.1 = (bf16[256,1024]{1,0:T(8,128)(2,1)}, bf16[256,1024]{1,0:T(8,128)(2,1)}, bf16[256,1024]{1,0:T(8,128)(2,1)}, bf16[256,1024]{1,0:T(8,128)(2,1)}) custom-call(bf16[3,1024,256]{2,1,0:T(8,128)(2,1)} %get-tuple-element.267.refs_0_, bf16[3,1024,256]{2,1,0:T(8,128)(2,1)} %get-tuple-element.268.refs_1_), custom_call_target="tpu_custom_call" | custom-call | flops 1 | bytes 1 | tf_op jit(solution)/shard_map/qkv_back/pallas_call | solution.py:136
  217.8 2.9 %layer.1 = bf16[256,1024]{1,0:T(8,128)(2,1)} custom-call(f32[256,1024]{1,0:T(8,128)} %get-tuple-element.209.refs_0_, bf16[256,1024]{1,0:T(8,128)(2,1)} %get-tuple-element.272.refs_1_, bf16[256,1024]{1,0:T(8,128)(2,1)} %copy-done.14, bf16[256,1024]{1,0:T(8,128)(2,1)} %copy-done.15, bf16[256,1024]{1,0:T(8,128)(2,1)} %copy-done.16), custom_call_target="tpu_custom_call" | custom-call | flops 1 | bytes 1 | tf_op jit(solution)/shard_map/layer/pallas_call | solution.py:136
  220.7 3.8 %collective-permute-done.43.refs_2_ = bf16[26,16,128]{2,1,0:T(8,128)(2,1)S(1)} collective-permute-done((bf16[26,16,128]{2,1,0:T(8,128)(2,1)}, bf16[26,16,128]{2,1,0:T(8,128)(2,1)S(1)}, u32[]{:S(2)}, u32[]{:S(2)}) %collective-permute-start.43) | collective-permute-done | bytes 106528 | tf_op jit(solution)/shard_map/ppermute | solution.py:768
  229.5 3.5 %last.1 = bf16[256,1024]{1,0:T(8,128)(2,1)} custom-call(bf16[256,1024]{1,0:T(8,128)(2,1)} %bitcast.12, f32[256,1024]{1,0:T(8,128)} %get-tuple-element.280.refs_1_, f32[2,1024]{1,0:T(2,128)} %get-tuple-element.188.refs_1_.refs_2_, bf16[256,1024]{1,0:T(8,128)(2,1)} %get-tuple-element.281.refs_3_, bf16[256,1024]{1,0:T(8,128)(2,1)} %copy-done.20, ...), custom_call_target="tpu_custom_call" | custom-call | flops 1 | bytes 1 | tf_op jit(solution)/shard_map/last/pallas_call | solution.py:136
  235.3 3.3 %collective-permute-done.48.refs_5_ = bf16[26,16,128]{2,1,0:T(8,128)(2,1)S(1)} collective-permute-done((bf16[26,16,128]{2,1,0:T(8,128)(2,1)S(1)}, bf16[26,16,128]{2,1,0:T(8,128)(2,1)S(1)}, u32[]{:S(2)}, u32[]{:S(2)}) %collective-permute-start.48) | collective-permute-done | bytes 106528 | tf_op jit(solution)/shard_map/ppermute | solution.py:767
  242.0 6.4 %spread.2 = (f32[8,16,5248]{2,1,0:T(8,128)}, f32[8,16,2624]{2,1,0:T(8,128)}, f32[8,16,1024]{2,1,0:T(8,128)}, f32[8,16,1024]{2,1,0:T(8,128)}) custom-call(bf16[8,54,16,128]{3,2,1,0:T(8,128)(2,1)} %bitcast.17, bf16[8,54,16,128]{3,2,1,0:T(8,128)(2,1)} %copy-done.7), custom_call_target="tpu_custom_call" | custom-call | flops 1 | bytes 1 | tf_op jit(solution)/shard_map/spread/pallas_call | solution.py:136
  249.1 2.2 stack.1.refs_0_
  251.4 2.6 collective-permute-done.53.refs_1_
  254.9 4.6 %spread.3 = (f32[8,16,3072]{2,1,0:T(8,128)}, f32[8,16,1024]{2,1,0:T(8,128)}, f32[8,16,1024]{2,1,0:T(8,128)}, f32[8,16,1024]{2,1,0:T(8,128)}) custom-call(bf16[8,26,16,128]{3,2,1,0:T(8,128)(2,1)} %stack.1.refs_0_, bf16[8,26,16,128]{3,2,1,0:T(8,128)(2,1)} %copy-done.10), custom_call_target="tpu_custom_call" | custom-call | flops 1 | bytes 1 | tf_op jit(solution)/shard_map/spread/pallas_call | solution.py:136
  (238 shorter events, 79.8 us)
Async XLA Ops:
  7.2 57.3 %all-gather.7.cloned.1.call-start = ((), (), s32[]{:S(2)}) async-start(), calls=%async_computation | async-start | bytes 2785280 | tf_op jit(solution)/shard_map/all_gather | solution.py:920
  7.2 19.2 %collective-permute-start = (bf16[656,256]{1,0:T(8,128)(2,1)}, bf16[656,256]{1,0:T(8,128)(2,1)S(1)}, u32[]{:S(2)}, u32[]{:S(2)}) collective-permute-start(bf16[656,256]{1,0:T(8,128)(2,1)} %bitcast.20), channel_id=1, source_target_pairs={{0,0},{1,4},{2,8},{3,12},{4,1},{5,5},{6,9},{7,13},{8,2},{9,6},{10,... | collective-permute-start | bytes 1007624 | tf_op jit(solution)/shard_map/ppermute | solution.py:886
  10.9 15.5 %collective-permute-start.2 = (bf16[256,128]{1,0:T(8,128)(2,1)}, bf16[256,128]{1,0:T(8,128)(2,1)S(1)}, u32[]{:S(2)}, u32[]{:S(2)}) collective-permute-start(bf16[256,128]{1,0:T(8,128)(2,1)} %get-tuple-element.165), channel_id=1, source_target_pairs={{0,1},{1,5},{2,9},{3,13},{4,17},{5,21},{6,25},{7,29},{8,0},{9,4},{... | collective-permute-start | bytes 196616 | tf_op jit(solution)/shard_map/ppermute | solution.py:880
  14.3 12.1 %collective-permute-start.1 = (bf16[256,256]{1,0:T(8,128)(2,1)}, bf16[256,256]{1,0:T(8,128)(2,1)S(1)}, u32[]{:S(2)}, u32[]{:S(2)}) collective-permute-start(bf16[256,256]{1,0:T(8,128)(2,1)} %get-tuple-element.164), channel_id=1, source_target_pairs={{0,0},{1,4},{2,8},{3,12},{4,2},{5,6},{6,10},{7,14},{8,3},{9,7},{10... | collective-permute-start | bytes 393224 | tf_op jit(solution)/shard_map/ppermute | solution.py:880
  26.4 83.8 %all-gather.9.cloned.1.call-start = ((), (), s32[]{:S(2)}) async-start(), calls=%async_computation.1 | async-start | bytes 2621440 | tf_op jit(solution)/shard_map/all_gather | solution.py:921
  26.6 9.4 %collective-permute-start.5 = (bf16[256,512]{1,0:T(8,128)(2,1)S(1)}, bf16[256,512]{1,0:T(8,128)(2,1)S(1)}, u32[]{:S(2)}, u32[]{:S(2)}) collective-permute-start(bf16[256,512]{1,0:T(8,128)(2,1)S(1)} %constant_dynamic-update-slice_fusion.refs_6_), channel_id=1, source_target_pairs={{8,0},{16,8},{24,16},{28,24},{20,28},{12,20},{4,12},{0,4},{9,1},{1... | collective-permute-start | bytes 786440 | tf_op jit(solution)/shard_map/ppermute | solution.py:768
  28.7 9.0 %collective-permute-start.3 = (bf16[256,512]{1,0:T(8,128)(2,1)S(1)}, bf16[256,512]{1,0:T(8,128)(2,1)S(1)}, u32[]{:S(2)}, u32[]{:S(2)}) collective-permute-start(bf16[256,512]{1,0:T(8,128)(2,1)S(1)} %constant_dynamic-update-slice_fusion.refs_6_), channel_id=1, source_target_pairs={{0,8},{8,16},{16,24},{24,28},{28,20},{20,12},{12,4},{4,0},{1,9},{9... | collective-permute-start | bytes 786440 | tf_op jit(solution)/shard_map/ppermute | solution.py:767
  45.5 187.7 %all-gather.11.cloned.1.call-start = ((), (), s32[]{:S(2)}) async-start(), calls=%async_computation.2 | async-start | bytes 1990656 | tf_op jit(solution)/shard_map/all_gather | solution.py:1037
  53.7 8.1 %collective-permute-start.10 = (bf16[128,512]{1,0:T(8,128)(2,1)S(1)}, bf16[128,512]{1,0:T(8,128)(2,1)S(1)}, u32[]{:S(2)}, u32[]{:S(2)}) collective-permute-start(bf16[128,512]{1,0:T(8,128)(2,1)S(1)} %slice.25), channel_id=1, source_target_pairs={{8,0},{16,8},{24,16},{28,24},{20,28},{12,20},{4,12},{0,4},{9,1},{1... | collective-permute-start | bytes 393224 | tf_op jit(solution)/shard_map/ppermute | solution.py:768
  62.4 11.2 %collective-permute-start.12 = (bf16[656,384]{1,0:T(8,128)(2,1)S(1)}, bf16[656,384]{1,0:T(8,128)(2,1)S(1)}, u32[]{:S(2)}, u32[]{:S(2)}) collective-permute-start(bf16[656,384]{1,0:T(8,128)(2,1)S(1)} %pad_maximum_fusion.refs_5_), channel_id=1, source_target_pairs={{8,0},{16,8},{24,16},{28,24},{20,28},{12,20},{4,12},{0,4},{9,1},{1... | collective-permute-start | bytes 1511432 | tf_op jit(solution)/shard_map/ppermute | solution.py:768
  62.5 11.2 %collective-permute-start.11 = (bf16[656,384]{1,0:T(8,128)(2,1)S(1)}, bf16[656,384]{1,0:T(8,128)(2,1)S(1)}, u32[]{:S(2)}, u32[]{:S(2)}) collective-permute-start(bf16[656,384]{1,0:T(8,128)(2,1)S(1)} %pad_maximum_fusion.refs_5_), channel_id=1, source_target_pairs={{0,8},{8,16},{16,24},{24,28},{28,20},{20,12},{12,4},{4,0},{1,9},{9... | collective-permute-start | bytes 1511432 | tf_op jit(solution)/shard_map/ppermute | solution.py:767
  73.5 15.0 %collective-permute-start.16 = (bf16[256,1024]{1,0:T(8,128)(2,1)}, bf16[256,1024]{1,0:T(8,128)(2,1)S(1)}, u32[]{:S(2)}, u32[]{:S(2)}) collective-permute-start(bf16[256,1024]{1,0:T(8,128)(2,1)} %get-tuple-element.206.refs_8_.refs_13_), channel_id=1, source_target_pairs={{0,2},{1,3},{2,0},{3,1},{4,6},{5,7},{6,4},{7,5},{8,10},{9,11},{10,... | collective-permute-start | bytes 1572872 | tf_op jit(solution)/shard_map/ppermute | solution.py:720
  73.5 14.9 %collective-permute-start.15 = (bf16[256,1024]{1,0:T(8,128)(2,1)}, bf16[256,1024]{1,0:T(8,128)(2,1)S(1)}, u32[]{:S(2)}, u32[]{:S(2)}) collective-permute-start(bf16[256,1024]{1,0:T(8,128)(2,1)} %get-tuple-element.206.refs_8_.refs_13_), channel_id=1, source_target_pairs={{0,1},{1,0},{2,3},{3,2},{4,5},{5,4},{6,7},{7,6},{8,9},{9,8},{10,11... | collective-permute-start | bytes 1572872 | tf_op jit(solution)/shard_map/ppermute | solution.py:720
  73.7 15.1 %collective-permute-start.13 = (bf16[656,384]{1,0:T(8,128)(2,1)S(1)}, bf16[656,384]{1,0:T(8,128)(2,1)}, u32[]{:S(2)}, u32[]{:S(2)}) collective-permute-start(bf16[656,384]{1,0:T(8,128)(2,1)S(1)} %collective-permute-done.11.refs_6_), channel_id=1, source_target_pairs={{0,8},{8,16},{16,24},{24,28},{28,20},{20,12},{12,4},{4,0},{1,9},{9... | collective-permute-start | bytes 1511432 | tf_op jit(solution)/shard_map/ppermute | solution.py:767
  75.7 13.8 %collective-permute-start.14 = (bf16[656,384]{1,0:T(8,128)(2,1)S(1)}, bf16[656,384]{1,0:T(8,128)(2,1)}, u32[]{:S(2)}, u32[]{:S(2)}) collective-permute-start(bf16[656,384]{1,0:T(8,128)(2,1)S(1)} %collective-permute-done.12.refs_7_), channel_id=1, source_target_pairs={{8,0},{16,8},{24,16},{28,24},{20,28},{12,20},{4,12},{0,4},{9,1},{1... | collective-permute-start | bytes 1511432 | tf_op jit(solution)/shard_map/ppermute | solution.py:768
  88.5 11.9 %collective-permute-start.20 = (bf16[256,1024]{1,0:T(8,128)(2,1)S(1)}, bf16[256,1024]{1,0:T(8,128)(2,1)S(1)}, u32[]{:S(2)}, u32[]{:S(2)}) collective-permute-start(bf16[256,1024]{1,0:T(8,128)(2,1)S(1)} %collective-permute-done.16.refs_10_.refs_15_), channel_id=1, source_target_pairs={{0,1},{1,0},{2,3},{3,2},{4,5},{5,4},{6,7},{7,6},{8,9},{9,8},{10,11... | collective-permute-start | bytes 1572872 | tf_op jit(solution)/shard_map/ppermute | solution.py:720
  89.5 16.0 %collective-permute-start.21 = (bf16[656,384]{1,0:T(8,128)(2,1)}, bf16[656,384]{1,0:T(8,128)(2,1)S(1)}, u32[]{:S(2)}, u32[]{:S(2)}) collective-permute-start(bf16[656,384]{1,0:T(8,128)(2,1)} %collective-permute-done.13.refs_8_), channel_id=1, source_target_pairs={{0,8},{8,16},{16,24},{24,28},{28,20},{20,12},{12,4},{4,0},{1,9},{9... | collective-permute-start | bytes 1511432 | tf_op jit(solution)/shard_map/ppermute | solution.py:767
  91.6 14.0 %collective-permute-start.22 = (bf16[656,384]{1,0:T(8,128)(2,1)}, bf16[656,384]{1,0:T(8,128)(2,1)S(1)}, u32[]{:S(2)}, u32[]{:S(2)}) collective-permute-start(bf16[656,384]{1,0:T(8,128)(2,1)} %collective-permute-done.14.refs_9_), channel_id=1, source_target_pairs={{8,0},{16,8},{24,16},{28,24},{20,28},{12,20},{4,12},{0,4},{9,1},{1... | collective-permute-start | bytes 1511432 | tf_op jit(solution)/shard_map/ppermute | solution.py:768
  105.6 18.6 %collective-permute-start.25 = (bf16[256,1024]{1,0:T(8,128)(2,1)}, bf16[256,1024]{1,0:T(8,128)(2,1)S(1)}, u32[]{:S(2)}, u32[]{:S(2)}) collective-permute-start(bf16[256,1024]{1,0:T(8,128)(2,1)} %get-tuple-element.223.refs_2_.refs_10_), channel_id=1, source_target_pairs={{0,1},{1,0},{2,3},{3,2},{4,5},{5,4},{6,7},{7,6},{8,9},{9,8},{10,11... | collective-permute-start | bytes 1572872 | tf_op jit(solution)/shard_map/ppermute | solution.py:720
  106.1 26.1 %collective-permute-start.26 = (bf16[256,1024]{1,0:T(8,128)(2,1)}, bf16[256,1024]{1,0:T(8,128)(2,1)S(1)}, u32[]{:S(2)}, u32[]{:S(2)}) collective-permute-start(bf16[256,1024]{1,0:T(8,128)(2,1)} %get-tuple-element.223.refs_2_.refs_10_), channel_id=1, source_target_pairs={{0,2},{1,3},{2,0},{3,1},{4,6},{5,7},{6,4},{7,5},{8,10},{9,11},{10,... | collective-permute-start | bytes 1572872 | tf_op jit(solution)/shard_map/ppermute | solution.py:720
  107.8 8.2 %collective-permute-start.24 = (bf16[336,384]{1,0:T(8,128)(2,1)S(1)}, bf16[336,384]{1,0:T(8,128)(2,1)S(1)}, u32[]{:S(2)}, u32[]{:S(2)}) collective-permute-start(bf16[336,384]{1,0:T(8,128)(2,1)S(1)} %slice.21), channel_id=1, source_target_pairs={{8,0},{16,8},{24,16},{28,24},{20,28},{12,20},{4,12},{0,4},{9,1},{1... | collective-permute-start | bytes 774152 | tf_op jit(solution)/shard_map/ppermute | solution.py:768
  145.6 15.7 %collective-permute-start.30 = (bf16[256,1024]{1,0:T(8,128)(2,1)S(1)}, bf16[256,1024]{1,0:T(8,128)(2,1)S(1)}, u32[]{:S(2)}, u32[]{:S(2)}) collective-permute-start(bf16[256,1024]{1,0:T(8,128)(2,1)S(1)} %add_convert_fusion.1), channel_id=1, source_target_pairs={{0,2},{1,3},{2,0},{3,1},{4,6},{5,7},{6,4},{7,5},{8,10},{9,11},{10,... | collective-permute-start | bytes 1572872 | tf_op jit(solution)/shard_map/ppermute | solution.py:720
  146.0 15.4 %collective-permute-start.27 = (bf16[256,1024]{1,0:T(8,128)(2,1)S(1)}, bf16[256,1024]{1,0:T(8,128)(2,1)S(1)}, u32[]{:S(2)}, u32[]{:S(2)}) collective-permute-start(bf16[256,1024]{1,0:T(8,128)(2,1)S(1)} %copy-done.55), channel_id=1, source_target_pairs={{0,1},{1,0},{2,3},{3,2},{4,5},{5,4},{6,7},{7,6},{8,9},{9,8},{10,11... | collective-permute-start | bytes 1572872 | tf_op jit(solution)/shard_map/ppermute | solution.py:720
  155.2 15.0 %collective-permute-start.34 = (bf16[35,16,128]{2,1,0:T(8,128)(2,1)}, bf16[35,16,128]{2,1,0:T(8,128)(2,1)S(1)}, u32[]{:S(2)}, u32[]{:S(2)}) collective-permute-start(bf16[35,16,128]{2,1,0:T(8,128)(2,1)} %mlp_terms.1.refs_0_), channel_id=1, source_target_pairs={{0,2},{1,3},{2,0},{3,1},{4,6},{5,7},{6,4},{7,5},{8,10},{9,11},{10,... | collective-permute-start | bytes 430088 | tf_op jit(solution)/shard_map/ppermute | solution.py:720
  176.7 22.5 %collective-permute-start.35 = (bf16[256,1024]{1,0:T(8,128)(2,1)S(1)}, bf16[256,1024]{1,0:T(8,128)(2,1)S(1)}, u32[]{:S(2)}, u32[]{:S(2)}) collective-permute-start(bf16[256,1024]{1,0:T(8,128)(2,1)S(1)} %copy-done.54), channel_id=1, source_target_pairs={{0,1},{1,0},{2,3},{3,2},{4,5},{5,4},{6,7},{7,6},{8,9},{9,8},{10,11... | collective-permute-start | bytes 1572872 | tf_op jit(solution)/shard_map/ppermute | solution.py:720
  177.2 22.0 %collective-permute-start.36 = (bf16[256,1024]{1,0:T(8,128)(2,1)S(1)}, bf16[256,1024]{1,0:T(8,128)(2,1)S(1)}, u32[]{:S(2)}, u32[]{:S(2)}) collective-permute-start(bf16[256,1024]{1,0:T(8,128)(2,1)S(1)} %copy-done.53), channel_id=1, source_target_pairs={{0,2},{1,3},{2,0},{3,1},{4,6},{5,7},{6,4},{7,5},{8,10},{9,11},{10,... | collective-permute-start | bytes 1572872 | tf_op jit(solution)/shard_map/ppermute | solution.py:720
  177.5 23.9 %collective-permute-start.37 = (bf16[256,1024]{1,0:T(8,128)(2,1)S(1)}, bf16[256,1024]{1,0:T(8,128)(2,1)S(1)}, u32[]{:S(2)}, u32[]{:S(2)}) collective-permute-start(bf16[256,1024]{1,0:T(8,128)(2,1)S(1)} %copy-done.52), channel_id=1, source_target_pairs={{0,3},{1,2},{2,1},{3,0},{4,7},{5,6},{6,5},{7,4},{8,11},{9,10},{10,... | collective-permute-start | bytes 1572872 | tf_op jit(solution)/shard_map/ppermute | solution.py:720
  178.6 22.8 %collective-permute-start.39 = (bf16[8,16,128]{2,1,0:T(8,128)(2,1)}, bf16[8,16,128]{2,1,0:T(8,128)(2,1)S(1)}, u32[]{:S(2)}, u32[]{:S(2)}) collective-permute-start(bf16[8,16,128]{2,1,0:T(8,128)(2,1)} %get-tuple-element.264), channel_id=1, source_target_pairs={{0,1},{1,0},{2,3},{3,2},{4,5},{5,4},{6,7},{7,6},{8,9},{9,8},{10,11... | collective-permute-start | bytes 98312 | tf_op jit(solution)/shard_map/ppermute | solution.py:720
  213.5 13.2 %collective-permute-start.44 = (bf16[256,1024]{1,0:T(8,128)(2,1)S(1)}, bf16[256,1024]{1,0:T(8,128)(2,1)S(1)}, u32[]{:S(2)}, u32[]{:S(2)}) collective-permute-start(bf16[256,1024]{1,0:T(8,128)(2,1)S(1)} %add_convert_fusion), channel_id=1, source_target_pairs={{0,2},{1,3},{2,0},{3,1},{4,6},{5,7},{6,4},{7,5},{8,10},{9,11},{10,... | collective-permute-start | bytes 1572872 | tf_op jit(solution)/shard_map/ppermute | solution.py:720
  213.9 14.7 %collective-permute-start.47 = (bf16[256,1024]{1,0:T(8,128)(2,1)S(1)}, bf16[256,1024]{1,0:T(8,128)(2,1)S(1)}, u32[]{:S(2)}, u32[]{:S(2)}) collective-permute-start(bf16[256,1024]{1,0:T(8,128)(2,1)S(1)} %copy-done.56), channel_id=1, source_target_pairs={{0,1},{1,0},{2,3},{3,2},{4,5},{5,4},{6,7},{7,6},{8,9},{9,8},{10,11... | collective-permute-start | bytes 1572872 | tf_op jit(solution)/shard_map/ppermute | solution.py:720
  215.7 8.8 %collective-permute-start.43 = (bf16[26,16,128]{2,1,0:T(8,128)(2,1)}, bf16[26,16,128]{2,1,0:T(8,128)(2,1)S(1)}, u32[]{:S(2)}, u32[]{:S(2)}) collective-permute-start(bf16[26,16,128]{2,1,0:T(8,128)(2,1)} %pair_late.1.refs_0_), channel_id=1, source_target_pairs={{8,0},{16,8},{24,16},{28,24},{20,28},{12,20},{4,12},{0,4},{9,1},{1... | collective-permute-start | bytes 319496 | tf_op jit(solution)/shard_map/ppermute | solution.py:768
  238.6 9.8 %collective-permute-start.50 = (bf16[13,16,128]{2,1,0:T(8,128)(2,1)S(1)}, bf16[13,16,128]{2,1,0:T(8,128)(2,1)S(1)}, u32[]{:S(2)}, u32[]{:S(2)}) collective-permute-start(bf16[13,16,128]{2,1,0:T(8,128)(2,1)S(1)} %slice.26), channel_id=1, source_target_pairs={{0,8},{8,16},{16,24},{24,28},{28,20},{20,12},{12,4},{4,0},{1,9},{9... | collective-permute-start | bytes 159752 | tf_op jit(solution)/shard_map/ppermute | solution.py:767
  (82 other events, 690.3 us)
Sparse Core Ops, SparseCore 0:
  26.5 25.6 all-gather.6
  53.8 24.5 all-gather.8
  176.8 48.4 all-gather.10

commit v4 on v3

--- a/solution.py
+++ b/solution.py
@@ -1004,17 +1004,8 @@
             name="mlp_terms",
         )[0]
         early.append(terms)
-        terms, *acts[pair] = meet(terms, *acts[pair])
-        out_slots += call(
-            functools.partial(mlp_out_kernel, 4),
-            [shape((rows, width), BF16)] * 4,
-            [w_out] + acts[pair],
-            early=(0, 1, 2, 3),
-            name="mlp_out",
-        )
     early = sum(early[1:], early[0])
     if fast:
-        back_two[2], *out_slots = meet(back_two[2], *out_slots)
         early = call(
             functools.partial(pair_kernel, early_local),
             [shape((early_local + early.shape[0], rank, 128), BF16)],
@@ -1030,6 +1021,15 @@
         scratch=[pltpu.VMEM((rank, width), F32)],
         name="out_back",
     )
+    rest[0], *acts = meet(rest[0], *acts)
+    for first in range(0, tok, 4):
+        out_slots += call(
+            functools.partial(mlp_out_kernel, 4),
+            [shape((rows, width), BF16)] * 4,
+            [w_out] + acts[first // 2 : first // 2 + 2],
+            early=(0, 1, 2, 3),
+            name="mlp_out",
+        )
     out_keep, out_send = rest[tok:]
     attn_grads = move.turn(rest[:tok])
     if fast:

time: 267 us -> 266 us (level)
  Pallas kernels: 120 us -> 114 us
  waiting for transfers between devices: 67.4 us -> 73.4 us
    pallas_call x21, Pallas kernels: 120 us -> 114 us  [call(): pl.pallas_call(body, out_shape=list(out_shape), in_specs=[pl.BlockSpec(me...]
    ppermute x27, waiting for transfers between devices: 23.2 us -> 26.8 us  [swap(): return lax.ppermute(block, 'tok', pairs)]
    unnamed x116 -> x112, local copies, waits for them, and re-layouts: 9.96 us -> 9.86 us
  transfers between devices with their start and end apart: 57 -> 57, of which waited for: 24 -> 25; matrix products, arithmetic and copies ran while one was open for 2% -> 2% of each run, Pallas kernels for 40% -> 37%
where the time goes in v4:
time: 266 us; the launch traced here: 265 us
  Pallas kernels  114 us (43%)
  waiting for transfers between devices  73.4 us (28%)
  starting transfers between devices  47.6 us (18%)
  between operations  15.3 us (6%)
  local copies, waits for them, and re-layouts  10 us (4%)
  other arithmetic  5.59 us (2%)
    pallas_call x21, Pallas kernels, call(): pl.pallas_call(body, out_shape=list(out_shape), in_specs=[pl.BlockSpec(me...  114 us
    ppermute x27, waiting for transfers between devices, swap(): return lax.ppermute(block, 'tok', pairs)  26.8 us
    ppermute x12, waiting for transfers between devices, step(): self.left = lax.ppermute(self.left, 'seq', self.behind)  21.3 us
    ppermute x12, waiting for transfers between devices, step(): self.right = lax.ppermute(self.right, 'seq', self.ahead)  20.5 us
    ppermute x12, starting transfers between devices, step(): self.right = lax.ppermute(self.right, 'seq', self.ahead)  17.4 us
    ppermute x27, starting transfers between devices, swap(): return lax.ppermute(block, 'tok', pairs)  14.5 us
    unnamed x112, local copies, waits for them, and re-layouts  9.86 us
    ppermute x12, starting transfers between devices, step(): self.left = lax.ppermute(self.left, 'seq', self.behind)  9.03 us
  transfers between devices with their start and end apart: 57, of which 25 were waited for; matrix products, arithmetic and copies ran while one was open for 2% of the time, Pallas kernels for 37%

profile of v4, /device:TPU:0, one launch (start us, length us, event | category | flops | bytes accessed | tf_op | source)
XLA Modules:
  0.0 265.5 jit_solution(944258989328601167)
XLA Ops:
  10.9 3.4 %collective-permute-start.2 = (bf16[256,128]{1,0:T(8,128)(2,1)}, bf16[256,128]{1,0:T(8,128)(2,1)S(1)}, u32[]{:S(2)}, u32[]{:S(2)}) collective-permute-start(bf16[256,128]{1,0:T(8,128)(2,1)} %get-tuple-element.161), channel_id=1, source_target_pairs={{0,1},{1,5},{2,9},{3,13},{4,17},{5,21},{6,25},{7,29},{8,0},{9,4},{... | collective-permute-start | bytes 196616 | tf_op jit(solution)/shard_map/ppermute | solution.py:880
  16.0 3.1 %fusion = (f32[1024,128]{1,0:T(8,128)}, f32[1024,128]{1,0:T(8,128)}) fusion(f32[128]{0:T(128)S(1)} %compare_select_fusion, f32[128]{0:T(128)S(1)} %mul.46, f32[1024]{0:T(1024)S(1)} %iota_convert_fusion), kind=kLoop, calls=%fused_computation.4 | loop fusion | flops 262144 | bytes 1053696 | tf_op jit(solution)/shard_map/mul | solution.py:858
  21.7 4.7 %collective-permute-done.2 = bf16[256,128]{1,0:T(8,128)(2,1)S(1)} collective-permute-done((bf16[256,128]{1,0:T(8,128)(2,1)}, bf16[256,128]{1,0:T(8,128)(2,1)S(1)}, u32[]{:S(2)}, u32[]{:S(2)}) %collective-permute-start.2) | collective-permute-done | bytes 65568 | tf_op jit(solution)/shard_map/ppermute | solution.py:880
  29.9 6.0 %collective-permute-done.5.refs_8_ = bf16[256,512]{1,0:T(8,128)(2,1)S(1)} collective-permute-done((bf16[256,512]{1,0:T(8,128)(2,1)S(1)}, bf16[256,512]{1,0:T(8,128)(2,1)S(1)}, u32[]{:S(2)}, u32[]{:S(2)}) %collective-permute-start.5) | collective-permute-done | bytes 262176 | tf_op jit(solution)/shard_map/ppermute | solution.py:768
  38.0 5.3 %collective-permute-done.6.refs_10_ = bf16[256,512]{1,0:T(8,128)(2,1)S(1)} collective-permute-done((bf16[256,512]{1,0:T(8,128)(2,1)S(1)}, bf16[256,512]{1,0:T(8,128)(2,1)S(1)}, u32[]{:S(2)}, u32[]{:S(2)}) %collective-permute-start.6) | collective-permute-done | bytes 262176 | tf_op jit(solution)/shard_map/ppermute | solution.py:768
  47.6 5.0 %collective-permute-done.7.refs_11_ = bf16[256,512]{1,0:T(8,128)(2,1)S(1)} collective-permute-done((bf16[256,512]{1,0:T(8,128)(2,1)S(1)}, bf16[256,512]{1,0:T(8,128)(2,1)S(1)}, u32[]{:S(2)}, u32[]{:S(2)}) %collective-permute-start.7) | collective-permute-done | bytes 262176 | tf_op jit(solution)/shard_map/ppermute | solution.py:767
  54.8 2.8 %collective-permute-done.8.refs_13_ = bf16[128,512]{1,0:T(8,128)(2,1)S(1)} collective-permute-done((bf16[128,512]{1,0:T(8,128)(2,1)S(1)}, bf16[128,512]{1,0:T(8,128)(2,1)S(1)}, u32[]{:S(2)}, u32[]{:S(2)}) %collective-permute-start.8) | collective-permute-done | bytes 131104 | tf_op jit(solution)/shard_map/ppermute | solution.py:767
  57.7 4.2 %collective-permute-done.10.refs_14_ = bf16[128,512]{1,0:T(8,128)(2,1)S(1)} collective-permute-done((bf16[128,512]{1,0:T(8,128)(2,1)S(1)}, bf16[128,512]{1,0:T(8,128)(2,1)S(1)}, u32[]{:S(2)}, u32[]{:S(2)}) %collective-permute-start.10) | collective-permute-done | bytes 131104 | tf_op jit(solution)/shard_map/ppermute | solution.py:768
  64.6 8.9 %qkv.1 = (bf16[1024,1024]{1,0:T(8,128)(2,1)}, f32[2,1024]{1,0:T(2,128)}, bf16[1024,256]{1,0:T(8,128)(2,1)}, bf16[1024,256]{1,0:T(8,128)(2,1)}, bf16[1024,256]{1,...) custom-call(s32[12]{0:T(128)} %constant.32.clone.refs_0_, bf16[4,272,1024]{2,1,0:T(8,128)(2,1)} %bitcast.13, ...), custom_call_target="tpu_custom_call" | custom-call | flops 1 | bytes 1 | tf_op jit(solution)/shard_map/qkv/pallas_call | solution.py:136
  75.8 10.0 %attend.1 = (bf16[256,256]{1,0:T(8,128)(2,1)}, bf16[256,256]{1,0:T(8,128)(2,1)}, bf16[256,256]{1,0:T(8,128)(2,1)}, bf16[256,256]{1,0:T(8,128)(2,1)}, f32[4,1024]{1,0:T(4,128)}, /*index=5*/f32[4,256,256]{2,1,0:T(8,128)}) custom-call(s32[1,1024]{1,0:T(1,128)} %refs_5_.3, bf16[1024,256]{1,0:T(8,128)(2,1)} %get-tuple-element.178.refs_1_.refs_2_, ...), custom_call_target="tpu_custom_call" | custom-call | flops 1 | bytes 1 | tf_op jit(solution)/shard_map/attend/pallas_call | solution.py:136
  94.8 3.3 %collective-permute-done.18.refs_6_.refs_11_ = bf16[256,256]{1,0:T(8,128)(2,1)S(1)} collective-permute-done((bf16[256,256]{1,0:T(8,128)(2,1)}, bf16[256,256]{1,0:T(8,128)(2,1)S(1)}, u32[]{:S(2)}, u32[]{:S(2)}) %collective-permute-start.18) | collective-permute-done | bytes 131104 | tf_op jit(solution)/shard_map/ppermute | solution.py:720
  98.2 2.3 collective-permute-done.19.refs_7_.refs_12_
  101.3 4.2 %out.1 = (f32[256,1024]{1,0:T(8,128)}, bf16[256,1024]{1,0:T(8,128)(2,1)}, bf16[256,16]{1,0:T(8,128)(2,1)}) custom-call(bf16[256,1024]{1,0:T(8,128)(2,1)} %bitcast.11, f32[2,1024]{1,0:T(2,128)} %get-tuple-element.184.refs_1_.refs_2_, bf16[16,1024]{1,0:T(8,128)(2,1)} %get-tuple-element.185.refs_2_.refs_3_, ...), custom_call_target="tpu_custom_call" | custom-call | flops 1 | bytes 1 | tf_op jit(solution)/shard_map/out/pallas_call | solution.py:136
  110.1 5.6 %collective-permute-done.23.refs_12_ = bf16[320,384]{1,0:T(8,128)(2,1)S(1)} collective-permute-done((bf16[320,384]{1,0:T(8,128)(2,1)S(1)}, bf16[320,384]{1,0:T(8,128)(2,1)S(1)}, u32[]{:S(2)}, u32[]{:S(2)}) %collective-permute-start.23) | collective-permute-done | bytes 245792 | tf_op jit(solution)/shard_map/ppermute | solution.py:767
  116.7 7.4 %mlp_pre.1 = (bf16[2,656,1024]{2,1,0:T(8,128)(2,1)}, bf16[656,1024]{1,0:T(8,128)(2,1)}, f32[2,256,656]{2,1,0:T(8,128)}, f32[2,256,656]{2,1,0:T(8,128)}) custom-call(bf16[16,1024]{1,0:T(8,128)(2,1)} %get-tuple-element.207.refs_0_.refs_1_, bf16[2,16,656]{2,1,0:T(8,128)(2,1)} %get-tuple-element.208.refs_1_.refs_2_, ...), custom_call_target="tpu_custom_call" | custom-call | flops 1 | bytes 1 | tf_op jit(solution)/shard_map/mlp_pre/pallas_call | solution.py:136
  125.0 7.2 %mlp.2 = (bf16[256,1024]{1,0:T(8,128)(2,1)}, bf16[256,1024]{1,0:T(8,128)(2,1)}, bf16[2,256,656]{2,1,0:T(8,128)(2,1)}, bf16[2,2,256,656]{3,2,1,0:T(8,128)(2,1)}) custom-call(bf16[2,656,1024]{2,1,0:T(8,128)(2,1)} %get-tuple-element.217.refs_0_, f32[2,256,656]{2,1,0:T(8,128)} %get-tuple-element.218.refs_1_, ...), custom_call_target="tpu_custom_call" | custom-call | flops 1 | bytes 1 | tf_op jit(solution)/shard_map/mlp/pallas_call | solution.py:136
  135.0 7.2 %mlp.3 = (bf16[256,1024]{1,0:T(8,128)(2,1)}, bf16[256,1024]{1,0:T(8,128)(2,1)}, bf16[2,256,656]{2,1,0:T(8,128)(2,1)}, bf16[2,2,256,656]{3,2,1,0:T(8,128)(2,1)}) custom-call(bf16[2,656,1024]{2,1,0:T(8,128)(2,1)} %get-tuple-element.217.refs_0_, f32[2,256,656]{2,1,0:T(8,128)} %get-tuple-element.224.refs_1_, bf16[256,1024]{1,0:T(8,128)(2,1)} %copy-done.4, ...), custom_call_target="tpu_custom_call" | custom-call | flops 1 | bytes 1 | tf_op jit(solution)/shard_map/mlp/pallas_call | solution.py:136
  146.0 9.2 %mlp_terms.1.refs_0_ = bf16[35,16,128]{2,1,0:T(8,128)(2,1)} custom-call(s32[1]{0:T(128)S(6)} %copy.31.refs_0_.refs_1_, bf16[16,1024]{1,0:T(8,128)(2,1)} %get-tuple-element.207.refs_0_.refs_1_, bf16[2,16,656]{2,1,0:T(8,128)(2,1)} %get-tuple-element.208.refs_1_.refs_2_, bf16[16,656]{1,0:T(8,128)(2,1)} %get-tuple-element.209.refs_2_.refs_3_, ...), custom_call_target="tpu_custom_call" | custom-call | flops 1 | bytes 1 | tf_op jit(solution)/shard_map/mlp_terms/pallas_call | solution.py:136
  157.0 3.5 %collective-permute-done.30.refs_8_ = bf16[256,1024]{1,0:T(8,128)(2,1)S(1)} collective-permute-done((bf16[256,1024]{1,0:T(8,128)(2,1)S(1)}, bf16[256,1024]{1,0:T(8,128)(2,1)S(1)}, u32[]{:S(2)}, u32[]{:S(2)}) %collective-permute-start.30) | collective-permute-done | bytes 524320 | tf_op jit(solution)/shard_map/ppermute | solution.py:720
  161.3 5.8 %out_back.1 = (f32[256,1024]{1,0:T(8,128)}, bf16[256,256]{1,0:T(8,128)(2,1)}, bf16[256,256]{1,0:T(8,128)(2,1)}, bf16[256,256]{1,0:T(8,128)(2,1)}, bf16[256,256]{...) custom-call(f32[256,1024]{1,0:T(8,128)} %get-tuple-element.205.refs_0_, ...), custom_call_target="tpu_custom_call" | custom-call | flops 1 | bytes 1 | tf_op jit(solution)/shard_map/out_back/pallas_call | solution.py:136
  171.4 4.4 %mlp_out.1 = (bf16[256,1024]{1,0:T(8,128)(2,1)}, bf16[256,1024]{1,0:T(8,128)(2,1)}, bf16[256,1024]{1,0:T(8,128)(2,1)}, bf16[256,1024]{1,0:T(8,128)(2,1)}) custom-call(bf16[656,1024]{1,0:T(8,128)(2,1)} %get-tuple-element.235.refs_0_, bf16[2,256,656]{2,1,0:T(8,128)(2,1)} %get-tuple-element.236.refs_1_.refs_5_, ...), custom_call_target="tpu_custom_call" | custom-call | flops 1 | bytes 1 | tf_op jit(solution)/shard_map/mlp_out/pallas_call | solution.py:136
  178.4 16.3 %attend_back.1 = (bf16[3,1024,256]{2,1,0:T(8,128)(2,1)}, bf16[11,16,128]{2,1,0:T(8,128)(2,1)}, bf16[4,16,128]{2,1,0:T(8,128)(2,1)}) custom-call(s32[1,1024]{1,0:T(1,128)} %refs_5_.3, s32[1]{0:T(128)S(6)} %copy.31.refs_0_.refs_1_, bf16[1024,256]{1,0:T(8,128)(2,1)} %get-tuple-element.178.refs_1_.refs_2_, bf16[1024,256]{1,0:T(8,128)(2,1)} %get-tuple-element.179.refs_2_.refs_3_, ...), custom_call_target="tpu_custom_call" | custom-call | flops 1 | bytes 1 | tf_op jit(solution)/shard_map/attend_back/pallas_call | solution.py:136
  194.9 6.0 %collective-permute-done.37.refs_4_ = bf16[256,1024]{1,0:T(8,128)(2,1)S(1)} collective-permute-done((bf16[256,1024]{1,0:T(8,128)(2,1)}, bf16[256,1024]{1,0:T(8,128)(2,1)S(1)}, u32[]{:S(2)}, u32[]{:S(2)}) %collective-permute-start.37) | collective-permute-done | bytes 524320 | tf_op jit(solution)/shard_map/ppermute | solution.py:720
  203.1 4.6 %qkv_back.1 = (bf16[256,1024]{1,0:T(8,128)(2,1)}, bf16[256,1024]{1,0:T(8,128)(2,1)}, bf16[256,1024]{1,0:T(8,128)(2,1)}, bf16[256,1024]{1,0:T(8,128)(2,1)}) custom-call(bf16[3,1024,256]{2,1,0:T(8,128)(2,1)} %get-tuple-element.259.refs_0_, bf16[3,1024,256]{2,1,0:T(8,128)(2,1)} %get-tuple-element.260.refs_1_), custom_call_target="tpu_custom_call" | custom-call | flops 1 | bytes 1 | tf_op jit(solution)/shard_map/qkv_back/pallas_call | solution.py:136
  217.2 2.9 %layer.1 = bf16[256,1024]{1,0:T(8,128)(2,1)} custom-call(f32[256,1024]{1,0:T(8,128)} %get-tuple-element.205.refs_0_, bf16[256,1024]{1,0:T(8,128)(2,1)} %get-tuple-element.264.refs_1_, bf16[256,1024]{1,0:T(8,128)(2,1)} %copy-done.14, bf16[256,1024]{1,0:T(8,128)(2,1)} %copy-done.15, bf16[256,1024]{1,0:T(8,128)(2,1)} %copy-done.16), custom_call_target="tpu_custom_call" | custom-call | flops 1 | bytes 1 | tf_op jit(solution)/shard_map/layer/pallas_call | solution.py:136
  220.1 3.6 %collective-permute-done.43.refs_2_ = bf16[26,16,128]{2,1,0:T(8,128)(2,1)S(1)} collective-permute-done((bf16[26,16,128]{2,1,0:T(8,128)(2,1)}, bf16[26,16,128]{2,1,0:T(8,128)(2,1)S(1)}, u32[]{:S(2)}, u32[]{:S(2)}) %collective-permute-start.43) | collective-permute-done | bytes 106528 | tf_op jit(solution)/shard_map/ppermute | solution.py:768
  223.7 2.3 collective-permute-done.44.refs_5_
  228.8 3.5 %last.1 = bf16[256,1024]{1,0:T(8,128)(2,1)} custom-call(bf16[256,1024]{1,0:T(8,128)(2,1)} %bitcast.12, f32[256,1024]{1,0:T(8,128)} %get-tuple-element.272.refs_1_, f32[2,1024]{1,0:T(2,128)} %get-tuple-element.184.refs_1_.refs_2_, bf16[256,1024]{1,0:T(8,128)(2,1)} %get-tuple-element.273.refs_3_, bf16[256,1024]{1,0:T(8,128)(2,1)} %copy-done.20, ...), custom_call_target="tpu_custom_call" | custom-call | flops 1 | bytes 1 | tf_op jit(solution)/shard_map/last/pallas_call | solution.py:136
  234.6 3.3 %collective-permute-done.48.refs_5_ = bf16[26,16,128]{2,1,0:T(8,128)(2,1)S(1)} collective-permute-done((bf16[26,16,128]{2,1,0:T(8,128)(2,1)S(1)}, bf16[26,16,128]{2,1,0:T(8,128)(2,1)S(1)}, u32[]{:S(2)}, u32[]{:S(2)}) %collective-permute-start.48) | collective-permute-done | bytes 106528 | tf_op jit(solution)/shard_map/ppermute | solution.py:767
  241.3 6.4 %spread.2 = (f32[8,16,5248]{2,1,0:T(8,128)}, f32[8,16,2624]{2,1,0:T(8,128)}, f32[8,16,1024]{2,1,0:T(8,128)}, f32[8,16,1024]{2,1,0:T(8,128)}) custom-call(bf16[8,54,16,128]{3,2,1,0:T(8,128)(2,1)} %bitcast.17, bf16[8,54,16,128]{3,2,1,0:T(8,128)(2,1)} %copy-done.7), custom_call_target="tpu_custom_call" | custom-call | flops 1 | bytes 1 | tf_op jit(solution)/shard_map/spread/pallas_call | solution.py:136
  250.8 2.6 collective-permute-done.53.refs_1_
  254.3 4.6 %spread.3 = (f32[8,16,3072]{2,1,0:T(8,128)}, f32[8,16,1024]{2,1,0:T(8,128)}, f32[8,16,1024]{2,1,0:T(8,128)}, f32[8,16,1024]{2,1,0:T(8,128)}) custom-call(bf16[8,26,16,128]{3,2,1,0:T(8,128)(2,1)} %stack.1.refs_0_, bf16[8,26,16,128]{3,2,1,0:T(8,128)(2,1)} %copy-done.10), custom_call_target="tpu_custom_call" | custom-call | flops 1 | bytes 1 | tf_op jit(solution)/shard_map/spread/pallas_call | solution.py:136
  (234 shorter events, 80.7 us)
Async XLA Ops:
  7.2 57.4 %all-gather.7.cloned.1.call-start = ((), (), s32[]{:S(2)}) async-start(), calls=%async_computation | async-start | bytes 2785280 | tf_op jit(solution)/shard_map/all_gather | solution.py:920
  7.2 19.2 %collective-permute-start = (bf16[656,256]{1,0:T(8,128)(2,1)}, bf16[656,256]{1,0:T(8,128)(2,1)S(1)}, u32[]{:S(2)}, u32[]{:S(2)}) collective-permute-start(bf16[656,256]{1,0:T(8,128)(2,1)} %bitcast.20), channel_id=1, source_target_pairs={{0,0},{1,4},{2,8},{3,12},{4,1},{5,5},{6,9},{7,13},{8,2},{9,6},{10,... | collective-permute-start | bytes 1007624 | tf_op jit(solution)/shard_map/ppermute | solution.py:886
  10.9 15.5 %collective-permute-start.2 = (bf16[256,128]{1,0:T(8,128)(2,1)}, bf16[256,128]{1,0:T(8,128)(2,1)S(1)}, u32[]{:S(2)}, u32[]{:S(2)}) collective-permute-start(bf16[256,128]{1,0:T(8,128)(2,1)} %get-tuple-element.161), channel_id=1, source_target_pairs={{0,1},{1,5},{2,9},{3,13},{4,17},{5,21},{6,25},{7,29},{8,0},{9,4},{... | collective-permute-start | bytes 196616 | tf_op jit(solution)/shard_map/ppermute | solution.py:880
  14.3 12.1 %collective-permute-start.1 = (bf16[256,256]{1,0:T(8,128)(2,1)}, bf16[256,256]{1,0:T(8,128)(2,1)S(1)}, u32[]{:S(2)}, u32[]{:S(2)}) collective-permute-start(bf16[256,256]{1,0:T(8,128)(2,1)} %get-tuple-element.160), channel_id=1, source_target_pairs={{0,0},{1,4},{2,8},{3,12},{4,2},{5,6},{6,10},{7,14},{8,3},{9,7},{10... | collective-permute-start | bytes 393224 | tf_op jit(solution)/shard_map/ppermute | solution.py:880
  26.4 83.7 %all-gather.9.cloned.1.call-start = ((), (), s32[]{:S(2)}) async-start(), calls=%async_computation.1 | async-start | bytes 2621440 | tf_op jit(solution)/shard_map/all_gather | solution.py:921
  26.6 9.4 %collective-permute-start.5 = (bf16[256,512]{1,0:T(8,128)(2,1)S(1)}, bf16[256,512]{1,0:T(8,128)(2,1)S(1)}, u32[]{:S(2)}, u32[]{:S(2)}) collective-permute-start(bf16[256,512]{1,0:T(8,128)(2,1)S(1)} %constant_dynamic-update-slice_fusion.refs_6_), channel_id=1, source_target_pairs={{8,0},{16,8},{24,16},{28,24},{20,28},{12,20},{4,12},{0,4},{9,1},{1... | collective-permute-start | bytes 786440 | tf_op jit(solution)/shard_map/ppermute | solution.py:768
  28.7 9.0 %collective-permute-start.3 = (bf16[256,512]{1,0:T(8,128)(2,1)S(1)}, bf16[256,512]{1,0:T(8,128)(2,1)S(1)}, u32[]{:S(2)}, u32[]{:S(2)}) collective-permute-start(bf16[256,512]{1,0:T(8,128)(2,1)S(1)} %constant_dynamic-update-slice_fusion.refs_6_), channel_id=1, source_target_pairs={{0,8},{8,16},{16,24},{24,28},{28,20},{20,12},{12,4},{4,0},{1,9},{9... | collective-permute-start | bytes 786440 | tf_op jit(solution)/shard_map/ppermute | solution.py:767
  45.5 187.1 %all-gather.11.cloned.1.call-start = ((), (), s32[]{:S(2)}) async-start(), calls=%async_computation.2 | async-start | bytes 1990656 | tf_op jit(solution)/shard_map/all_gather | solution.py:1037
  62.5 11.2 %collective-permute-start.12 = (bf16[656,384]{1,0:T(8,128)(2,1)S(1)}, bf16[656,384]{1,0:T(8,128)(2,1)S(1)}, u32[]{:S(2)}, u32[]{:S(2)}) collective-permute-start(bf16[656,384]{1,0:T(8,128)(2,1)S(1)} %pad_maximum_fusion.refs_5_), channel_id=1, source_target_pairs={{8,0},{16,8},{24,16},{28,24},{20,28},{12,20},{4,12},{0,4},{9,1},{1... | collective-permute-start | bytes 1511432 | tf_op jit(solution)/shard_map/ppermute | solution.py:768
  62.5 11.2 %collective-permute-start.11 = (bf16[656,384]{1,0:T(8,128)(2,1)S(1)}, bf16[656,384]{1,0:T(8,128)(2,1)S(1)}, u32[]{:S(2)}, u32[]{:S(2)}) collective-permute-start(bf16[656,384]{1,0:T(8,128)(2,1)S(1)} %pad_maximum_fusion.refs_5_), channel_id=1, source_target_pairs={{0,8},{8,16},{16,24},{24,28},{28,20},{20,12},{12,4},{4,0},{1,9},{9... | collective-permute-start | bytes 1511432 | tf_op jit(solution)/shard_map/ppermute | solution.py:767
  73.5 12.7 %collective-permute-start.16 = (bf16[256,1024]{1,0:T(8,128)(2,1)}, bf16[256,1024]{1,0:T(8,128)(2,1)S(1)}, u32[]{:S(2)}, u32[]{:S(2)}) collective-permute-start(bf16[256,1024]{1,0:T(8,128)(2,1)} %get-tuple-element.202.refs_8_.refs_13_), channel_id=1, source_target_pairs={{0,2},{1,3},{2,0},{3,1},{4,6},{5,7},{6,4},{7,5},{8,10},{9,11},{10,... | collective-permute-start | bytes 1572872 | tf_op jit(solution)/shard_map/ppermute | solution.py:720
  73.6 12.6 %collective-permute-start.15 = (bf16[256,1024]{1,0:T(8,128)(2,1)}, bf16[256,1024]{1,0:T(8,128)(2,1)S(1)}, u32[]{:S(2)}, u32[]{:S(2)}) collective-permute-start(bf16[256,1024]{1,0:T(8,128)(2,1)} %get-tuple-element.202.refs_8_.refs_13_), channel_id=1, source_target_pairs={{0,1},{1,0},{2,3},{3,2},{4,5},{5,4},{6,7},{7,6},{8,9},{9,8},{10,11... | collective-permute-start | bytes 1572872 | tf_op jit(solution)/shard_map/ppermute | solution.py:720
  73.7 14.0 %collective-permute-start.13 = (bf16[656,384]{1,0:T(8,128)(2,1)S(1)}, bf16[656,384]{1,0:T(8,128)(2,1)}, u32[]{:S(2)}, u32[]{:S(2)}) collective-permute-start(bf16[656,384]{1,0:T(8,128)(2,1)S(1)} %collective-permute-done.11.refs_6_), channel_id=1, source_target_pairs={{0,8},{8,16},{16,24},{24,28},{28,20},{20,12},{12,4},{4,0},{1,9},{9... | collective-permute-start | bytes 1511432 | tf_op jit(solution)/shard_map/ppermute | solution.py:767
  75.8 13.8 %collective-permute-start.14 = (bf16[656,384]{1,0:T(8,128)(2,1)S(1)}, bf16[656,384]{1,0:T(8,128)(2,1)}, u32[]{:S(2)}, u32[]{:S(2)}) collective-permute-start(bf16[656,384]{1,0:T(8,128)(2,1)S(1)} %collective-permute-done.12.refs_7_), channel_id=1, source_target_pairs={{8,0},{16,8},{24,16},{28,24},{20,28},{12,20},{4,12},{0,4},{9,1},{1... | collective-permute-start | bytes 1511432 | tf_op jit(solution)/shard_map/ppermute | solution.py:768
  86.2 14.3 %collective-permute-start.20 = (bf16[256,1024]{1,0:T(8,128)(2,1)S(1)}, bf16[256,1024]{1,0:T(8,128)(2,1)S(1)}, u32[]{:S(2)}, u32[]{:S(2)}) collective-permute-start(bf16[256,1024]{1,0:T(8,128)(2,1)S(1)} %collective-permute-done.16.refs_10_.refs_15_), channel_id=1, source_target_pairs={{0,1},{1,0},{2,3},{3,2},{4,5},{5,4},{6,7},{7,6},{8,9},{9,8},{10,11... | collective-permute-start | bytes 1572872 | tf_op jit(solution)/shard_map/ppermute | solution.py:720
  89.6 16.0 %collective-permute-start.21 = (bf16[656,384]{1,0:T(8,128)(2,1)}, bf16[656,384]{1,0:T(8,128)(2,1)S(1)}, u32[]{:S(2)}, u32[]{:S(2)}) collective-permute-start(bf16[656,384]{1,0:T(8,128)(2,1)} %collective-permute-done.13.refs_8_), channel_id=1, source_target_pairs={{0,8},{8,16},{16,24},{24,28},{28,20},{20,12},{12,4},{4,0},{1,9},{9... | collective-permute-start | bytes 1511432 | tf_op jit(solution)/shard_map/ppermute | solution.py:767
  91.6 14.0 %collective-permute-start.22 = (bf16[656,384]{1,0:T(8,128)(2,1)}, bf16[656,384]{1,0:T(8,128)(2,1)S(1)}, u32[]{:S(2)}, u32[]{:S(2)}) collective-permute-start(bf16[656,384]{1,0:T(8,128)(2,1)} %collective-permute-done.14.refs_9_), channel_id=1, source_target_pairs={{8,0},{16,8},{24,16},{28,24},{20,28},{12,20},{4,12},{0,4},{9,1},{1... | collective-permute-start | bytes 1511432 | tf_op jit(solution)/shard_map/ppermute | solution.py:768
  105.6 18.6 %collective-permute-start.25 = (bf16[256,1024]{1,0:T(8,128)(2,1)}, bf16[256,1024]{1,0:T(8,128)(2,1)S(1)}, u32[]{:S(2)}, u32[]{:S(2)}) collective-permute-start(bf16[256,1024]{1,0:T(8,128)(2,1)} %get-tuple-element.219.refs_2_.refs_10_), channel_id=1, source_target_pairs={{0,1},{1,0},{2,3},{3,2},{4,5},{5,4},{6,7},{7,6},{8,9},{9,8},{10,11... | collective-permute-start | bytes 1572872 | tf_op jit(solution)/shard_map/ppermute | solution.py:720
  106.0 26.2 %collective-permute-start.26 = (bf16[256,1024]{1,0:T(8,128)(2,1)}, bf16[256,1024]{1,0:T(8,128)(2,1)S(1)}, u32[]{:S(2)}, u32[]{:S(2)}) collective-permute-start(bf16[256,1024]{1,0:T(8,128)(2,1)} %get-tuple-element.219.refs_2_.refs_10_), channel_id=1, source_target_pairs={{0,2},{1,3},{2,0},{3,1},{4,6},{5,7},{6,4},{7,5},{8,10},{9,11},{10,... | collective-permute-start | bytes 1572872 | tf_op jit(solution)/shard_map/ppermute | solution.py:720
  142.4 14.6 %collective-permute-start.27 = (bf16[256,1024]{1,0:T(8,128)(2,1)S(1)}, bf16[256,1024]{1,0:T(8,128)(2,1)S(1)}, u32[]{:S(2)}, u32[]{:S(2)}) collective-permute-start(bf16[256,1024]{1,0:T(8,128)(2,1)S(1)} %copy-done.53), channel_id=1, source_target_pairs={{0,1},{1,0},{2,3},{3,2},{4,5},{5,4},{6,7},{7,6},{8,9},{9,8},{10,11... | collective-permute-start | bytes 1572872 | tf_op jit(solution)/shard_map/ppermute | solution.py:720
  145.6 14.8 %collective-permute-start.30 = (bf16[256,1024]{1,0:T(8,128)(2,1)S(1)}, bf16[256,1024]{1,0:T(8,128)(2,1)S(1)}, u32[]{:S(2)}, u32[]{:S(2)}) collective-permute-start(bf16[256,1024]{1,0:T(8,128)(2,1)S(1)} %add_convert_fusion.1), channel_id=1, source_target_pairs={{0,2},{1,3},{2,0},{3,1},{4,6},{5,7},{6,4},{7,5},{8,10},{9,11},{10,... | collective-permute-start | bytes 1572872 | tf_op jit(solution)/shard_map/ppermute | solution.py:720
  155.2 13.8 %collective-permute-start.34 = (bf16[35,16,128]{2,1,0:T(8,128)(2,1)}, bf16[35,16,128]{2,1,0:T(8,128)(2,1)S(1)}, u32[]{:S(2)}, u32[]{:S(2)}) collective-permute-start(bf16[35,16,128]{2,1,0:T(8,128)(2,1)} %mlp_terms.1.refs_0_), channel_id=1, source_target_pairs={{0,2},{1,3},{2,0},{3,1},{4,6},{5,7},{6,4},{7,5},{8,10},{9,11},{10,... | collective-permute-start | bytes 430088 | tf_op jit(solution)/shard_map/ppermute | solution.py:720
  167.0 8.8 %collective-permute-start.31 = (bf16[256,256]{1,0:T(8,128)(2,1)}, bf16[256,256]{1,0:T(8,128)(2,1)S(1)}, u32[]{:S(2)}, u32[]{:S(2)}) collective-permute-start(bf16[256,256]{1,0:T(8,128)(2,1)} %get-tuple-element.232), channel_id=1, source_target_pairs={{0,1},{1,0},{2,3},{3,2},{4,5},{5,4},{6,7},{7,6},{8,9},{9,8},{10,11... | collective-permute-start | bytes 393224 | tf_op jit(solution)/shard_map/ppermute | solution.py:720
  167.1 8.7 %collective-permute-start.32 = (bf16[256,256]{1,0:T(8,128)(2,1)}, bf16[256,256]{1,0:T(8,128)(2,1)S(1)}, u32[]{:S(2)}, u32[]{:S(2)}) collective-permute-start(bf16[256,256]{1,0:T(8,128)(2,1)} %get-tuple-element.233), channel_id=1, source_target_pairs={{0,2},{1,3},{2,0},{3,1},{4,6},{5,7},{6,4},{7,5},{8,10},{9,11},{10,... | collective-permute-start | bytes 393224 | tf_op jit(solution)/shard_map/ppermute | solution.py:720
  167.2 8.6 %collective-permute-start.33 = (bf16[256,256]{1,0:T(8,128)(2,1)}, bf16[256,256]{1,0:T(8,128)(2,1)S(1)}, u32[]{:S(2)}, u32[]{:S(2)}) collective-permute-start(bf16[256,256]{1,0:T(8,128)(2,1)} %get-tuple-element.234), channel_id=1, source_target_pairs={{0,3},{1,2},{2,1},{3,0},{4,7},{5,6},{6,5},{7,4},{8,11},{9,10},{10,... | collective-permute-start | bytes 393224 | tf_op jit(solution)/shard_map/ppermute | solution.py:720
  175.9 19.0 %collective-permute-start.35 = (bf16[256,1024]{1,0:T(8,128)(2,1)}, bf16[256,1024]{1,0:T(8,128)(2,1)S(1)}, u32[]{:S(2)}, u32[]{:S(2)}) collective-permute-start(bf16[256,1024]{1,0:T(8,128)(2,1)} %get-tuple-element.250), channel_id=1, source_target_pairs={{0,1},{1,0},{2,3},{3,2},{4,5},{5,4},{6,7},{7,6},{8,9},{9,8},{10,11... | collective-permute-start | bytes 1572872 | tf_op jit(solution)/shard_map/ppermute | solution.py:720
  176.3 18.6 %collective-permute-start.36 = (bf16[256,1024]{1,0:T(8,128)(2,1)}, bf16[256,1024]{1,0:T(8,128)(2,1)S(1)}, u32[]{:S(2)}, u32[]{:S(2)}) collective-permute-start(bf16[256,1024]{1,0:T(8,128)(2,1)} %get-tuple-element.251), channel_id=1, source_target_pairs={{0,2},{1,3},{2,0},{3,1},{4,6},{5,7},{6,4},{7,5},{8,10},{9,11},{10,... | collective-permute-start | bytes 1572872 | tf_op jit(solution)/shard_map/ppermute | solution.py:720
  176.4 24.6 %collective-permute-start.37 = (bf16[256,1024]{1,0:T(8,128)(2,1)}, bf16[256,1024]{1,0:T(8,128)(2,1)S(1)}, u32[]{:S(2)}, u32[]{:S(2)}) collective-permute-start(bf16[256,1024]{1,0:T(8,128)(2,1)} %get-tuple-element.252), channel_id=1, source_target_pairs={{0,3},{1,2},{2,1},{3,0},{4,7},{5,6},{6,5},{7,4},{8,11},{9,10},{10,... | collective-permute-start | bytes 1572872 | tf_op jit(solution)/shard_map/ppermute | solution.py:720
  177.8 23.1 %collective-permute-start.39 = (bf16[8,16,128]{2,1,0:T(8,128)(2,1)S(1)}, bf16[8,16,128]{2,1,0:T(8,128)(2,1)S(1)}, u32[]{:S(2)}, u32[]{:S(2)}) collective-permute-start(bf16[8,16,128]{2,1,0:T(8,128)(2,1)S(1)} %copy-done.54), channel_id=1, source_target_pairs={{0,1},{1,0},{2,3},{3,2},{4,5},{5,4},{6,7},{7,6},{8,9},{9,8},{10,11... | collective-permute-start | bytes 98312 | tf_op jit(solution)/shard_map/ppermute | solution.py:720
  212.9 13.2 %collective-permute-start.44 = (bf16[256,1024]{1,0:T(8,128)(2,1)S(1)}, bf16[256,1024]{1,0:T(8,128)(2,1)S(1)}, u32[]{:S(2)}, u32[]{:S(2)}) collective-permute-start(bf16[256,1024]{1,0:T(8,128)(2,1)S(1)} %add_convert_fusion), channel_id=1, source_target_pairs={{0,2},{1,3},{2,0},{3,1},{4,6},{5,7},{6,4},{7,5},{8,10},{9,11},{10,... | collective-permute-start | bytes 1572872 | tf_op jit(solution)/shard_map/ppermute | solution.py:720
  213.3 14.8 %collective-permute-start.47 = (bf16[256,1024]{1,0:T(8,128)(2,1)S(1)}, bf16[256,1024]{1,0:T(8,128)(2,1)S(1)}, u32[]{:S(2)}, u32[]{:S(2)}) collective-permute-start(bf16[256,1024]{1,0:T(8,128)(2,1)S(1)} %copy-done.52), channel_id=1, source_target_pairs={{0,1},{1,0},{2,3},{3,2},{4,5},{5,4},{6,7},{7,6},{8,9},{9,8},{10,11... | collective-permute-start | bytes 1572872 | tf_op jit(solution)/shard_map/ppermute | solution.py:720
  238.0 9.8 %collective-permute-start.50 = (bf16[13,16,128]{2,1,0:T(8,128)(2,1)S(1)}, bf16[13,16,128]{2,1,0:T(8,128)(2,1)S(1)}, u32[]{:S(2)}, u32[]{:S(2)}) collective-permute-start(bf16[13,16,128]{2,1,0:T(8,128)(2,1)S(1)} %slice.26), channel_id=1, source_target_pairs={{0,8},{8,16},{16,24},{24,28},{28,20},{20,12},{12,4},{4,0},{1,9},{9... | collective-permute-start | bytes 159752 | tf_op jit(solution)/shard_map/ppermute | solution.py:767
  (80 other events, 674.8 us)
Sparse Core Ops, SparseCore 0:
  26.5 25.6 all-gather.6
  53.8 24.4 all-gather.8
  176.0 48.2 all-gather.10

commit v5 on v4

--- a/solution.py
+++ b/solution.py
@@ -871,6 +871,7 @@
             [inputs, attn_gain, mlp_gain, qkv_weight],
             name="prepare",
         )
+        in_weight, *parts = meet(in_weight, *parts)
         for n, owners in enumerate((double, single)):
             pairs = [
                 (s * tok + t, (owners[s][1] * tok + t) * tok + owners[s][0])

time: 266 us -> 265 us (level)
  waiting for transfers between devices: 73.4 us -> 65.2 us
  starting transfers between devices: 47.6 us -> 55.2 us
    ppermute x12, starting transfers between devices: 9.03 us -> 18.1 us  [step(): self.left = lax.ppermute(self.left, 'seq', self.behind)]
    ppermute x12, waiting for transfers between devices: 21.3 us -> 16 us  [step(): self.left = lax.ppermute(self.left, 'seq', self.behind)]
    ppermute x2, waiting for transfers between devices: 4.67 us -> 0.01 us  [body(): parts[n] = lax.ppermute(parts[n], ('seq', 'tok'), pairs)]
    ppermute x2, starting transfers between devices: 4.98 us -> 2.06 us  [body(): parts[n] = lax.ppermute(parts[n], ('seq', 'tok'), pairs)]
  transfers between devices with their start and end apart: 57 -> 57, of which waited for: 25 -> 21; matrix products, arithmetic and copies ran while one was open for 2% -> 2% of each run, Pallas kernels for 37% -> 37%
where the time goes in v5:
time: 265 us
  Pallas kernels  114 us (43%)
  waiting for transfers between devices  65.2 us (25%)
  starting transfers between devices  55.2 us (21%)
  between operations  15.3 us (6%)
  local copies, waits for them, and re-layouts  9.9 us (4%)
  other arithmetic  5.59 us (2%)
    pallas_call x21, Pallas kernels, call(): pl.pallas_call(body, out_shape=list(out_shape), in_specs=[pl.BlockSpec(me...  114 us
    ppermute x27, waiting for transfers between devices, swap(): return lax.ppermute(block, 'tok', pairs)  28.2 us
    ppermute x12, waiting for transfers between devices, step(): self.right = lax.ppermute(self.right, 'seq', self.ahead)  20.9 us
    ppermute x12, starting transfers between devices, step(): self.left = lax.ppermute(self.left, 'seq', self.behind)  18.1 us
    ppermute x27, starting transfers between devices, swap(): return lax.ppermute(block, 'tok', pairs)  17 us
    ppermute x12, starting transfers between devices, step(): self.right = lax.ppermute(self.right, 'seq', self.ahead)  16.2 us
    ppermute x12, waiting for transfers between devices, step(): self.left = lax.ppermute(self.left, 'seq', self.behind)  16 us
    unnamed x112, local copies, waits for them, and re-layouts  9.72 us
  transfers between devices with their start and end apart: 57, of which 21 were waited for; matrix products, arithmetic and copies ran while one was open for 2% of the time, Pallas kernels for 37%

profile of v5, /device:TPU:0, one launch (start us, length us, event | category | flops | bytes accessed | tf_op | source)
XLA Modules:
  0.0 264.6 jit_solution(16323548061736928017)
XLA Ops:
  13.0 3.1 %fusion = (f32[1024,128]{1,0:T(8,128)}, f32[1024,128]{1,0:T(8,128)}) fusion(f32[128]{0:T(128)S(1)} %compare_select_fusion, f32[128]{0:T(128)S(1)} %mul.46, f32[1024]{0:T(1024)S(1)} %iota_convert_fusion), kind=kLoop, calls=%fused_computation.4 | loop fusion | flops 262144 | bytes 1053696 | tf_op jit(solution)/shard_map/mul | solution.py:858
  19.0 6.9 %collective-permute-start.5 = (bf16[256,512]{1,0:T(8,128)(2,1)S(1)}, bf16[256,512]{1,0:T(8,128)(2,1)S(1)}, u32[]{:S(2)}, u32[]{:S(2)}) collective-permute-start(bf16[256,512]{1,0:T(8,128)(2,1)S(1)} %constant_dynamic-update-slice_fusion.refs_6_), channel_id=1, source_target_pairs={{8,0},{16,8},{24,16},{28,24},{20,28},{12,20},{4,12},{0,4},{9,1},{1... | collective-permute-start | bytes 786440 | tf_op jit(solution)/shard_map/ppermute | solution.py:768
  25.9 4.3 %collective-permute-start.3 = (bf16[256,512]{1,0:T(8,128)(2,1)S(1)}, bf16[256,512]{1,0:T(8,128)(2,1)S(1)}, u32[]{:S(2)}, u32[]{:S(2)}) collective-permute-start(bf16[256,512]{1,0:T(8,128)(2,1)S(1)} %constant_dynamic-update-slice_fusion.refs_6_), channel_id=1, source_target_pairs={{0,8},{8,16},{16,24},{24,28},{28,20},{20,12},{12,4},{4,0},{1,9},{9... | collective-permute-start | bytes 786440 | tf_op jit(solution)/shard_map/ppermute | solution.py:767
  30.2 6.7 %collective-permute-done.5.refs_8_ = bf16[256,512]{1,0:T(8,128)(2,1)S(1)} collective-permute-done((bf16[256,512]{1,0:T(8,128)(2,1)S(1)}, bf16[256,512]{1,0:T(8,128)(2,1)S(1)}, u32[]{:S(2)}, u32[]{:S(2)}) %collective-permute-start.5) | collective-permute-done | bytes 262176 | tf_op jit(solution)/shard_map/ppermute | solution.py:768
  39.2 6.6 %collective-permute-done.6.refs_10_ = bf16[256,512]{1,0:T(8,128)(2,1)S(1)} collective-permute-done((bf16[256,512]{1,0:T(8,128)(2,1)S(1)}, bf16[256,512]{1,0:T(8,128)(2,1)S(1)}, u32[]{:S(2)}, u32[]{:S(2)}) %collective-permute-start.6) | collective-permute-done | bytes 262176 | tf_op jit(solution)/shard_map/ppermute | solution.py:768
  47.9 6.0 %collective-permute-done.7.refs_11_ = bf16[256,512]{1,0:T(8,128)(2,1)S(1)} collective-permute-done((bf16[256,512]{1,0:T(8,128)(2,1)S(1)}, bf16[256,512]{1,0:T(8,128)(2,1)S(1)}, u32[]{:S(2)}, u32[]{:S(2)}) %collective-permute-start.7) | collective-permute-done | bytes 262176 | tf_op jit(solution)/shard_map/ppermute | solution.py:767
  56.1 2.8 %collective-permute-done.8.refs_13_ = bf16[128,512]{1,0:T(8,128)(2,1)S(1)} collective-permute-done((bf16[128,512]{1,0:T(8,128)(2,1)S(1)}, bf16[128,512]{1,0:T(8,128)(2,1)S(1)}, u32[]{:S(2)}, u32[]{:S(2)}) %collective-permute-start.8) | collective-permute-done | bytes 131104 | tf_op jit(solution)/shard_map/ppermute | solution.py:767
  63.2 8.8 %qkv.1 = (bf16[1024,1024]{1,0:T(8,128)(2,1)}, f32[2,1024]{1,0:T(2,128)}, bf16[1024,256]{1,0:T(8,128)(2,1)}, bf16[1024,256]{1,0:T(8,128)(2,1)}, bf16[1024,256]{1,...) custom-call(s32[12]{0:T(128)} %constant.32.clone.refs_0_, bf16[4,272,1024]{2,1,0:T(8,128)(2,1)} %bitcast.13, ...), custom_call_target="tpu_custom_call" | custom-call | flops 1 | bytes 1 | tf_op jit(solution)/shard_map/qkv/pallas_call | solution.py:136
  72.1 3.0 %collective-permute-start.16 = (bf16[256,1024]{1,0:T(8,128)(2,1)}, bf16[256,1024]{1,0:T(8,128)(2,1)S(1)}, u32[]{:S(2)}, u32[]{:S(2)}) collective-permute-start(bf16[256,1024]{1,0:T(8,128)(2,1)} %get-tuple-element.208.refs_8_.refs_13_), channel_id=1, source_target_pairs={{0,2},{1,3},{2,0},{3,1},{4,6},{5,7},{6,4},{7,5},{8,10},{9,11},{10,... | collective-permute-start | bytes 1572872 | tf_op jit(solution)/shard_map/ppermute | solution.py:720
  77.2 10.0 %attend.1 = (bf16[256,256]{1,0:T(8,128)(2,1)}, bf16[256,256]{1,0:T(8,128)(2,1)}, bf16[256,256]{1,0:T(8,128)(2,1)}, bf16[256,256]{1,0:T(8,128)(2,1)}, f32[4,1024]{1,0:T(4,128)}, /*index=5*/f32[4,256,256]{2,1,0:T(8,128)}) custom-call(s32[1,1024]{1,0:T(1,128)} %refs_5_.3, bf16[1024,256]{1,0:T(8,128)(2,1)} %get-tuple-element.184.refs_1_.refs_2_, ...), custom_call_target="tpu_custom_call" | custom-call | flops 1 | bytes 1 | tf_op jit(solution)/shard_map/attend/pallas_call | solution.py:136
  93.1 4.6 %collective-permute-done.18.refs_6_.refs_11_ = bf16[256,256]{1,0:T(8,128)(2,1)S(1)} collective-permute-done((bf16[256,256]{1,0:T(8,128)(2,1)}, bf16[256,256]{1,0:T(8,128)(2,1)S(1)}, u32[]{:S(2)}, u32[]{:S(2)}) %collective-permute-start.18) | collective-permute-done | bytes 131104 | tf_op jit(solution)/shard_map/ppermute | solution.py:720
  100.7 4.2 %out.1 = (f32[256,1024]{1,0:T(8,128)}, bf16[256,1024]{1,0:T(8,128)(2,1)}, bf16[256,16]{1,0:T(8,128)(2,1)}) custom-call(bf16[256,1024]{1,0:T(8,128)(2,1)} %bitcast.11, f32[2,1024]{1,0:T(2,128)} %get-tuple-element.190.refs_1_.refs_2_, bf16[16,1024]{1,0:T(8,128)(2,1)} %get-tuple-element.191.refs_2_.refs_3_, ...), custom_call_target="tpu_custom_call" | custom-call | flops 1 | bytes 1 | tf_op jit(solution)/shard_map/out/pallas_call | solution.py:136
  108.4 6.8 %collective-permute-done.23.refs_12_ = bf16[320,384]{1,0:T(8,128)(2,1)S(1)} collective-permute-done((bf16[320,384]{1,0:T(8,128)(2,1)S(1)}, bf16[320,384]{1,0:T(8,128)(2,1)S(1)}, u32[]{:S(2)}, u32[]{:S(2)}) %collective-permute-start.23) | collective-permute-done | bytes 245792 | tf_op jit(solution)/shard_map/ppermute | solution.py:767
  116.0 7.4 %mlp_pre.1 = (bf16[2,656,1024]{2,1,0:T(8,128)(2,1)}, bf16[656,1024]{1,0:T(8,128)(2,1)}, f32[2,256,656]{2,1,0:T(8,128)}, f32[2,256,656]{2,1,0:T(8,128)}) custom-call(bf16[16,1024]{1,0:T(8,128)(2,1)} %get-tuple-element.213.refs_0_.refs_1_, bf16[2,16,656]{2,1,0:T(8,128)(2,1)} %get-tuple-element.214.refs_1_.refs_2_, ...), custom_call_target="tpu_custom_call" | custom-call | flops 1 | bytes 1 | tf_op jit(solution)/shard_map/mlp_pre/pallas_call | solution.py:136
  124.3 7.2 %mlp.2 = (bf16[256,1024]{1,0:T(8,128)(2,1)}, bf16[256,1024]{1,0:T(8,128)(2,1)}, bf16[2,256,656]{2,1,0:T(8,128)(2,1)}, bf16[2,2,256,656]{3,2,1,0:T(8,128)(2,1)}) custom-call(bf16[2,656,1024]{2,1,0:T(8,128)(2,1)} %get-tuple-element.223.refs_0_, f32[2,256,656]{2,1,0:T(8,128)} %get-tuple-element.224.refs_1_, ...), custom_call_target="tpu_custom_call" | custom-call | flops 1 | bytes 1 | tf_op jit(solution)/shard_map/mlp/pallas_call | solution.py:136
  134.3 7.2 %mlp.3 = (bf16[256,1024]{1,0:T(8,128)(2,1)}, bf16[256,1024]{1,0:T(8,128)(2,1)}, bf16[2,256,656]{2,1,0:T(8,128)(2,1)}, bf16[2,2,256,656]{3,2,1,0:T(8,128)(2,1)}) custom-call(bf16[2,656,1024]{2,1,0:T(8,128)(2,1)} %get-tuple-element.223.refs_0_, f32[2,256,656]{2,1,0:T(8,128)} %get-tuple-element.230.refs_1_, bf16[256,1024]{1,0:T(8,128)(2,1)} %copy-done.4, ...), custom_call_target="tpu_custom_call" | custom-call | flops 1 | bytes 1 | tf_op jit(solution)/shard_map/mlp/pallas_call | solution.py:136
  146.7 9.2 %mlp_terms.1.refs_0_ = bf16[35,16,128]{2,1,0:T(8,128)(2,1)} custom-call(s32[1]{0:T(128)S(6)} %copy.31.refs_0_.refs_1_, bf16[16,1024]{1,0:T(8,128)(2,1)} %get-tuple-element.213.refs_0_.refs_1_, bf16[2,16,656]{2,1,0:T(8,128)(2,1)} %get-tuple-element.214.refs_1_.refs_2_, bf16[16,656]{1,0:T(8,128)(2,1)} %get-tuple-element.215.refs_2_.refs_3_, ...), custom_call_target="tpu_custom_call" | custom-call | flops 1 | bytes 1 | tf_op jit(solution)/shard_map/mlp_terms/pallas_call | solution.py:136
  156.3 3.0 %collective-permute-done.30.refs_8_ = bf16[256,1024]{1,0:T(8,128)(2,1)S(1)} collective-permute-done((bf16[256,1024]{1,0:T(8,128)(2,1)S(1)}, bf16[256,1024]{1,0:T(8,128)(2,1)S(1)}, u32[]{:S(2)}, u32[]{:S(2)}) %collective-permute-start.30) | collective-permute-done | bytes 524320 | tf_op jit(solution)/shard_map/ppermute | solution.py:720
  160.0 5.8 %out_back.1 = (f32[256,1024]{1,0:T(8,128)}, bf16[256,256]{1,0:T(8,128)(2,1)}, bf16[256,256]{1,0:T(8,128)(2,1)}, bf16[256,256]{1,0:T(8,128)(2,1)}, bf16[256,256]{...) custom-call(f32[256,1024]{1,0:T(8,128)} %get-tuple-element.211.refs_0_, ...), custom_call_target="tpu_custom_call" | custom-call | flops 1 | bytes 1 | tf_op jit(solution)/shard_map/out_back/pallas_call | solution.py:136
  165.9 2.3 collective-permute-start.32
  170.6 4.4 %mlp_out.1 = (bf16[256,1024]{1,0:T(8,128)(2,1)}, bf16[256,1024]{1,0:T(8,128)(2,1)}, bf16[256,1024]{1,0:T(8,128)(2,1)}, bf16[256,1024]{1,0:T(8,128)(2,1)}) custom-call(bf16[656,1024]{1,0:T(8,128)(2,1)} %get-tuple-element.241.refs_0_, bf16[2,256,656]{2,1,0:T(8,128)(2,1)} %get-tuple-element.242.refs_1_.refs_5_, ...), custom_call_target="tpu_custom_call" | custom-call | flops 1 | bytes 1 | tf_op jit(solution)/shard_map/mlp_out/pallas_call | solution.py:136
  177.5 16.3 %attend_back.1 = (bf16[3,1024,256]{2,1,0:T(8,128)(2,1)}, bf16[11,16,128]{2,1,0:T(8,128)(2,1)}, bf16[4,16,128]{2,1,0:T(8,128)(2,1)}) custom-call(s32[1,1024]{1,0:T(1,128)} %refs_5_.3, s32[1]{0:T(128)S(6)} %copy.31.refs_0_.refs_1_, bf16[1024,256]{1,0:T(8,128)(2,1)} %get-tuple-element.184.refs_1_.refs_2_, bf16[1024,256]{1,0:T(8,128)(2,1)} %get-tuple-element.185.refs_2_.refs_3_, ...), custom_call_target="tpu_custom_call" | custom-call | flops 1 | bytes 1 | tf_op jit(solution)/shard_map/attend_back/pallas_call | solution.py:136
  194.2 6.2 %collective-permute-done.37.refs_4_ = bf16[256,1024]{1,0:T(8,128)(2,1)S(1)} collective-permute-done((bf16[256,1024]{1,0:T(8,128)(2,1)}, bf16[256,1024]{1,0:T(8,128)(2,1)S(1)}, u32[]{:S(2)}, u32[]{:S(2)}) %collective-permute-start.37) | collective-permute-done | bytes 524320 | tf_op jit(solution)/shard_map/ppermute | solution.py:720
  202.6 4.6 %qkv_back.1 = (bf16[256,1024]{1,0:T(8,128)(2,1)}, bf16[256,1024]{1,0:T(8,128)(2,1)}, bf16[256,1024]{1,0:T(8,128)(2,1)}, bf16[256,1024]{1,0:T(8,128)(2,1)}) custom-call(bf16[3,1024,256]{2,1,0:T(8,128)(2,1)} %get-tuple-element.265.refs_0_, bf16[3,1024,256]{2,1,0:T(8,128)(2,1)} %get-tuple-element.266.refs_1_), custom_call_target="tpu_custom_call" | custom-call | flops 1 | bytes 1 | tf_op jit(solution)/shard_map/qkv_back/pallas_call | solution.py:136
  217.5 2.9 %layer.1 = bf16[256,1024]{1,0:T(8,128)(2,1)} custom-call(f32[256,1024]{1,0:T(8,128)} %get-tuple-element.211.refs_0_, bf16[256,1024]{1,0:T(8,128)(2,1)} %get-tuple-element.270.refs_1_, bf16[256,1024]{1,0:T(8,128)(2,1)} %copy-done.14, bf16[256,1024]{1,0:T(8,128)(2,1)} %copy-done.15, bf16[256,1024]{1,0:T(8,128)(2,1)} %copy-done.16), custom_call_target="tpu_custom_call" | custom-call | flops 1 | bytes 1 | tf_op jit(solution)/shard_map/layer/pallas_call | solution.py:136
  221.5 3.8 %collective-permute-done.44.refs_5_ = bf16[256,1024]{1,0:T(8,128)(2,1)S(1)} collective-permute-done((bf16[256,1024]{1,0:T(8,128)(2,1)S(1)}, bf16[256,1024]{1,0:T(8,128)(2,1)S(1)}, u32[]{:S(2)}, u32[]{:S(2)}) %collective-permute-start.44) | collective-permute-done | bytes 524320 | tf_op jit(solution)/shard_map/ppermute | solution.py:720
  228.1 3.5 %last.1 = bf16[256,1024]{1,0:T(8,128)(2,1)} custom-call(bf16[256,1024]{1,0:T(8,128)(2,1)} %bitcast.12, f32[256,1024]{1,0:T(8,128)} %get-tuple-element.278.refs_1_, f32[2,1024]{1,0:T(2,128)} %get-tuple-element.190.refs_1_.refs_2_, bf16[256,1024]{1,0:T(8,128)(2,1)} %get-tuple-element.279.refs_3_, bf16[256,1024]{1,0:T(8,128)(2,1)} %copy-done.20, ...), custom_call_target="tpu_custom_call" | custom-call | flops 1 | bytes 1 | tf_op jit(solution)/shard_map/last/pallas_call | solution.py:136
  233.8 3.3 %collective-permute-done.48.refs_5_ = bf16[26,16,128]{2,1,0:T(8,128)(2,1)S(1)} collective-permute-done((bf16[26,16,128]{2,1,0:T(8,128)(2,1)S(1)}, bf16[26,16,128]{2,1,0:T(8,128)(2,1)S(1)}, u32[]{:S(2)}, u32[]{:S(2)}) %collective-permute-start.48) | collective-permute-done | bytes 106528 | tf_op jit(solution)/shard_map/ppermute | solution.py:767
  240.5 6.4 %spread.2 = (f32[8,16,5248]{2,1,0:T(8,128)}, f32[8,16,2624]{2,1,0:T(8,128)}, f32[8,16,1024]{2,1,0:T(8,128)}, f32[8,16,1024]{2,1,0:T(8,128)}) custom-call(bf16[8,54,16,128]{3,2,1,0:T(8,128)(2,1)} %bitcast.17, bf16[8,54,16,128]{3,2,1,0:T(8,128)(2,1)} %copy-done.7), custom_call_target="tpu_custom_call" | custom-call | flops 1 | bytes 1 | tf_op jit(solution)/shard_map/spread/pallas_call | solution.py:136
  247.6 2.2 stack.1.refs_0_
  249.9 2.6 collective-permute-done.53.refs_1_
  253.4 4.6 %spread.3 = (f32[8,16,3072]{2,1,0:T(8,128)}, f32[8,16,1024]{2,1,0:T(8,128)}, f32[8,16,1024]{2,1,0:T(8,128)}, f32[8,16,1024]{2,1,0:T(8,128)}) custom-call(bf16[8,26,16,128]{3,2,1,0:T(8,128)(2,1)} %stack.1.refs_0_, bf16[8,26,16,128]{3,2,1,0:T(8,128)(2,1)} %copy-done.10), custom_call_target="tpu_custom_call" | custom-call | flops 1 | bytes 1 | tf_op jit(solution)/shard_map/spread/pallas_call | solution.py:136
  (234 shorter events, 72.7 us)
Async XLA Ops:
  7.2 56.0 %all-gather.7.cloned.1.call-start = ((), (), s32[]{:S(2)}) async-start(), calls=%async_computation | async-start | bytes 2785280 | tf_op jit(solution)/shard_map/all_gather | solution.py:921
  9.2 9.5 %collective-permute-start.2 = (bf16[256,128]{1,0:T(8,128)(2,1)}, bf16[256,128]{1,0:T(8,128)(2,1)S(1)}, u32[]{:S(2)}, u32[]{:S(2)}) collective-permute-start(bf16[256,128]{1,0:T(8,128)(2,1)} %get-tuple-element.167), channel_id=1, source_target_pairs={{0,1},{1,5},{2,9},{3,13},{4,17},{5,21},{6,25},{7,29},{8,0},{9,4},{... | collective-permute-start | bytes 196616 | tf_op jit(solution)/shard_map/ppermute | solution.py:881
  9.8 9.0 %collective-permute-start.1 = (bf16[256,256]{1,0:T(8,128)(2,1)}, bf16[256,256]{1,0:T(8,128)(2,1)S(1)}, u32[]{:S(2)}, u32[]{:S(2)}) collective-permute-start(bf16[256,256]{1,0:T(8,128)(2,1)} %get-tuple-element.166), channel_id=1, source_target_pairs={{0,0},{1,4},{2,8},{3,12},{4,2},{5,6},{6,10},{7,14},{8,3},{9,7},{10... | collective-permute-start | bytes 393224 | tf_op jit(solution)/shard_map/ppermute | solution.py:881
  18.8 89.5 %all-gather.9.cloned.1.call-start = ((), (), s32[]{:S(2)}) async-start(), calls=%async_computation.1 | async-start | bytes 2621440 | tf_op jit(solution)/shard_map/all_gather | solution.py:922
  19.0 17.9 %collective-permute-start.5 = (bf16[256,512]{1,0:T(8,128)(2,1)S(1)}, bf16[256,512]{1,0:T(8,128)(2,1)S(1)}, u32[]{:S(2)}, u32[]{:S(2)}) collective-permute-start(bf16[256,512]{1,0:T(8,128)(2,1)S(1)} %constant_dynamic-update-slice_fusion.refs_6_), channel_id=1, source_target_pairs={{8,0},{16,8},{24,16},{28,24},{20,28},{12,20},{4,12},{0,4},{9,1},{1... | collective-permute-start | bytes 786440 | tf_op jit(solution)/shard_map/ppermute | solution.py:768
  25.9 11.1 %collective-permute-start.3 = (bf16[256,512]{1,0:T(8,128)(2,1)S(1)}, bf16[256,512]{1,0:T(8,128)(2,1)S(1)}, u32[]{:S(2)}, u32[]{:S(2)}) collective-permute-start(bf16[256,512]{1,0:T(8,128)(2,1)S(1)} %constant_dynamic-update-slice_fusion.refs_6_), channel_id=1, source_target_pairs={{0,8},{8,16},{16,24},{24,28},{28,20},{20,12},{12,4},{4,0},{1,9},{9... | collective-permute-start | bytes 786440 | tf_op jit(solution)/shard_map/ppermute | solution.py:767
  45.8 185.9 %all-gather.11.cloned.1.call-start = ((), (), s32[]{:S(2)}) async-start(), calls=%async_computation.2 | async-start | bytes 1990656 | tf_op jit(solution)/shard_map/all_gather | solution.py:1038
  61.1 14.0 %collective-permute-start.12 = (bf16[656,384]{1,0:T(8,128)(2,1)S(1)}, bf16[656,384]{1,0:T(8,128)(2,1)S(1)}, u32[]{:S(2)}, u32[]{:S(2)}) collective-permute-start(bf16[656,384]{1,0:T(8,128)(2,1)S(1)} %pad_maximum_fusion.refs_5_), channel_id=1, source_target_pairs={{8,0},{16,8},{24,16},{28,24},{20,28},{12,20},{4,12},{0,4},{9,1},{1... | collective-permute-start | bytes 1511432 | tf_op jit(solution)/shard_map/ppermute | solution.py:768
  61.7 13.4 %collective-permute-start.11 = (bf16[656,384]{1,0:T(8,128)(2,1)S(1)}, bf16[656,384]{1,0:T(8,128)(2,1)S(1)}, u32[]{:S(2)}, u32[]{:S(2)}) collective-permute-start(bf16[656,384]{1,0:T(8,128)(2,1)S(1)} %pad_maximum_fusion.refs_5_), channel_id=1, source_target_pairs={{0,8},{8,16},{16,24},{24,28},{28,20},{20,12},{12,4},{4,0},{1,9},{9... | collective-permute-start | bytes 1511432 | tf_op jit(solution)/shard_map/ppermute | solution.py:767
  72.1 15.1 %collective-permute-start.16 = (bf16[256,1024]{1,0:T(8,128)(2,1)}, bf16[256,1024]{1,0:T(8,128)(2,1)S(1)}, u32[]{:S(2)}, u32[]{:S(2)}) collective-permute-start(bf16[256,1024]{1,0:T(8,128)(2,1)} %get-tuple-element.208.refs_8_.refs_13_), channel_id=1, source_target_pairs={{0,2},{1,3},{2,0},{3,1},{4,6},{5,7},{6,4},{7,5},{8,10},{9,11},{10,... | collective-permute-start | bytes 1572872 | tf_op jit(solution)/shard_map/ppermute | solution.py:720
  75.1 12.1 %collective-permute-start.15 = (bf16[256,1024]{1,0:T(8,128)(2,1)}, bf16[256,1024]{1,0:T(8,128)(2,1)S(1)}, u32[]{:S(2)}, u32[]{:S(2)}) collective-permute-start(bf16[256,1024]{1,0:T(8,128)(2,1)} %get-tuple-element.208.refs_8_.refs_13_), channel_id=1, source_target_pairs={{0,1},{1,0},{2,3},{3,2},{4,5},{5,4},{6,7},{7,6},{8,9},{9,8},{10,11... | collective-permute-start | bytes 1572872 | tf_op jit(solution)/shard_map/ppermute | solution.py:720
  75.1 14.0 %collective-permute-start.13 = (bf16[656,384]{1,0:T(8,128)(2,1)S(1)}, bf16[656,384]{1,0:T(8,128)(2,1)}, u32[]{:S(2)}, u32[]{:S(2)}) collective-permute-start(bf16[656,384]{1,0:T(8,128)(2,1)S(1)} %collective-permute-done.11.refs_6_), channel_id=1, source_target_pairs={{0,8},{8,16},{16,24},{24,28},{28,20},{20,12},{12,4},{4,0},{1,9},{9... | collective-permute-start | bytes 1511432 | tf_op jit(solution)/shard_map/ppermute | solution.py:767
  75.5 13.8 %collective-permute-start.14 = (bf16[656,384]{1,0:T(8,128)(2,1)S(1)}, bf16[656,384]{1,0:T(8,128)(2,1)}, u32[]{:S(2)}, u32[]{:S(2)}) collective-permute-start(bf16[656,384]{1,0:T(8,128)(2,1)S(1)} %collective-permute-done.12.refs_7_), channel_id=1, source_target_pairs={{8,0},{16,8},{24,16},{28,24},{20,28},{12,20},{4,12},{0,4},{9,1},{1... | collective-permute-start | bytes 1511432 | tf_op jit(solution)/shard_map/ppermute | solution.py:768
  87.2 12.6 %collective-permute-start.20 = (bf16[256,1024]{1,0:T(8,128)(2,1)S(1)}, bf16[256,1024]{1,0:T(8,128)(2,1)S(1)}, u32[]{:S(2)}, u32[]{:S(2)}) collective-permute-start(bf16[256,1024]{1,0:T(8,128)(2,1)S(1)} %collective-permute-done.16.refs_10_.refs_15_), channel_id=1, source_target_pairs={{0,1},{1,0},{2,3},{3,2},{4,5},{5,4},{6,7},{7,6},{8,9},{9,8},{10,11... | collective-permute-start | bytes 1572872 | tf_op jit(solution)/shard_map/ppermute | solution.py:720
  89.2 15.6 %collective-permute-start.21 = (bf16[656,384]{1,0:T(8,128)(2,1)}, bf16[656,384]{1,0:T(8,128)(2,1)S(1)}, u32[]{:S(2)}, u32[]{:S(2)}) collective-permute-start(bf16[656,384]{1,0:T(8,128)(2,1)} %collective-permute-done.13.refs_8_), channel_id=1, source_target_pairs={{0,8},{8,16},{16,24},{24,28},{28,20},{20,12},{12,4},{4,0},{1,9},{9... | collective-permute-start | bytes 1511432 | tf_op jit(solution)/shard_map/ppermute | solution.py:767
  90.1 14.8 %collective-permute-start.22 = (bf16[656,384]{1,0:T(8,128)(2,1)}, bf16[656,384]{1,0:T(8,128)(2,1)S(1)}, u32[]{:S(2)}, u32[]{:S(2)}) collective-permute-start(bf16[656,384]{1,0:T(8,128)(2,1)} %collective-permute-done.14.refs_9_), channel_id=1, source_target_pairs={{8,0},{16,8},{24,16},{28,24},{20,28},{12,20},{4,12},{0,4},{9,1},{1... | collective-permute-start | bytes 1511432 | tf_op jit(solution)/shard_map/ppermute | solution.py:768
  104.9 18.5 %collective-permute-start.25 = (bf16[256,1024]{1,0:T(8,128)(2,1)}, bf16[256,1024]{1,0:T(8,128)(2,1)S(1)}, u32[]{:S(2)}, u32[]{:S(2)}) collective-permute-start(bf16[256,1024]{1,0:T(8,128)(2,1)} %get-tuple-element.225.refs_2_.refs_10_), channel_id=1, source_target_pairs={{0,1},{1,0},{2,3},{3,2},{4,5},{5,4},{6,7},{7,6},{8,9},{9,8},{10,11... | collective-permute-start | bytes 1572872 | tf_op jit(solution)/shard_map/ppermute | solution.py:720
  105.5 26.0 %collective-permute-start.26 = (bf16[256,1024]{1,0:T(8,128)(2,1)}, bf16[256,1024]{1,0:T(8,128)(2,1)S(1)}, u32[]{:S(2)}, u32[]{:S(2)}) collective-permute-start(bf16[256,1024]{1,0:T(8,128)(2,1)} %get-tuple-element.225.refs_2_.refs_10_), channel_id=1, source_target_pairs={{0,2},{1,3},{2,0},{3,1},{4,6},{5,7},{6,4},{7,5},{8,10},{9,11},{10,... | collective-permute-start | bytes 1572872 | tf_op jit(solution)/shard_map/ppermute | solution.py:720
  106.1 9.2 %collective-permute-start.24 = (bf16[336,384]{1,0:T(8,128)(2,1)S(1)}, bf16[336,384]{1,0:T(8,128)(2,1)S(1)}, u32[]{:S(2)}, u32[]{:S(2)}) collective-permute-start(bf16[336,384]{1,0:T(8,128)(2,1)S(1)} %slice.21), channel_id=1, source_target_pairs={{8,0},{16,8},{24,16},{28,24},{20,28},{12,20},{4,12},{0,4},{9,1},{1... | collective-permute-start | bytes 774152 | tf_op jit(solution)/shard_map/ppermute | solution.py:768
  141.7 14.6 %collective-permute-start.27 = (bf16[256,1024]{1,0:T(8,128)(2,1)S(1)}, bf16[256,1024]{1,0:T(8,128)(2,1)S(1)}, u32[]{:S(2)}, u32[]{:S(2)}) collective-permute-start(bf16[256,1024]{1,0:T(8,128)(2,1)S(1)} %copy-done.53), channel_id=1, source_target_pairs={{0,1},{1,0},{2,3},{3,2},{4,5},{5,4},{6,7},{7,6},{8,9},{9,8},{10,11... | collective-permute-start | bytes 1572872 | tf_op jit(solution)/shard_map/ppermute | solution.py:720
  144.9 14.3 %collective-permute-start.30 = (bf16[256,1024]{1,0:T(8,128)(2,1)S(1)}, bf16[256,1024]{1,0:T(8,128)(2,1)S(1)}, u32[]{:S(2)}, u32[]{:S(2)}) collective-permute-start(bf16[256,1024]{1,0:T(8,128)(2,1)S(1)} %add_convert_fusion.1), channel_id=1, source_target_pairs={{0,2},{1,3},{2,0},{3,1},{4,6},{5,7},{6,4},{7,5},{8,10},{9,11},{10,... | collective-permute-start | bytes 1572872 | tf_op jit(solution)/shard_map/ppermute | solution.py:720
  155.9 12.4 %collective-permute-start.34 = (bf16[35,16,128]{2,1,0:T(8,128)(2,1)}, bf16[35,16,128]{2,1,0:T(8,128)(2,1)S(1)}, u32[]{:S(2)}, u32[]{:S(2)}) collective-permute-start(bf16[35,16,128]{2,1,0:T(8,128)(2,1)} %mlp_terms.1.refs_0_), channel_id=1, source_target_pairs={{0,2},{1,3},{2,0},{3,1},{4,6},{5,7},{6,4},{7,5},{8,10},{9,11},{10,... | collective-permute-start | bytes 430088 | tf_op jit(solution)/shard_map/ppermute | solution.py:720
  165.8 9.2 %collective-permute-start.31 = (bf16[256,256]{1,0:T(8,128)(2,1)}, bf16[256,256]{1,0:T(8,128)(2,1)S(1)}, u32[]{:S(2)}, u32[]{:S(2)}) collective-permute-start(bf16[256,256]{1,0:T(8,128)(2,1)} %get-tuple-element.238), channel_id=1, source_target_pairs={{0,1},{1,0},{2,3},{3,2},{4,5},{5,4},{6,7},{7,6},{8,9},{9,8},{10,11... | collective-permute-start | bytes 393224 | tf_op jit(solution)/shard_map/ppermute | solution.py:720
  165.9 9.2 %collective-permute-start.32 = (bf16[256,256]{1,0:T(8,128)(2,1)}, bf16[256,256]{1,0:T(8,128)(2,1)S(1)}, u32[]{:S(2)}, u32[]{:S(2)}) collective-permute-start(bf16[256,256]{1,0:T(8,128)(2,1)} %get-tuple-element.239), channel_id=1, source_target_pairs={{0,2},{1,3},{2,0},{3,1},{4,6},{5,7},{6,4},{7,5},{8,10},{9,11},{10,... | collective-permute-start | bytes 393224 | tf_op jit(solution)/shard_map/ppermute | solution.py:720
  175.1 19.1 %collective-permute-start.35 = (bf16[256,1024]{1,0:T(8,128)(2,1)}, bf16[256,1024]{1,0:T(8,128)(2,1)S(1)}, u32[]{:S(2)}, u32[]{:S(2)}) collective-permute-start(bf16[256,1024]{1,0:T(8,128)(2,1)} %get-tuple-element.256), channel_id=1, source_target_pairs={{0,1},{1,0},{2,3},{3,2},{4,5},{5,4},{6,7},{7,6},{8,9},{9,8},{10,11... | collective-permute-start | bytes 1572872 | tf_op jit(solution)/shard_map/ppermute | solution.py:720
  175.3 18.9 %collective-permute-start.36 = (bf16[256,1024]{1,0:T(8,128)(2,1)}, bf16[256,1024]{1,0:T(8,128)(2,1)S(1)}, u32[]{:S(2)}, u32[]{:S(2)}) collective-permute-start(bf16[256,1024]{1,0:T(8,128)(2,1)} %get-tuple-element.257), channel_id=1, source_target_pairs={{0,2},{1,3},{2,0},{3,1},{4,6},{5,7},{6,4},{7,5},{8,10},{9,11},{10,... | collective-permute-start | bytes 1572872 | tf_op jit(solution)/shard_map/ppermute | solution.py:720
  177.3 23.2 %collective-permute-start.37 = (bf16[256,1024]{1,0:T(8,128)(2,1)}, bf16[256,1024]{1,0:T(8,128)(2,1)S(1)}, u32[]{:S(2)}, u32[]{:S(2)}) collective-permute-start(bf16[256,1024]{1,0:T(8,128)(2,1)} %get-tuple-element.258), channel_id=1, source_target_pairs={{0,3},{1,2},{2,1},{3,0},{4,7},{5,6},{6,5},{7,4},{8,11},{9,10},{10,... | collective-permute-start | bytes 1572872 | tf_op jit(solution)/shard_map/ppermute | solution.py:720
  177.3 23.2 %collective-permute-start.39 = (bf16[8,16,128]{2,1,0:T(8,128)(2,1)S(1)}, bf16[8,16,128]{2,1,0:T(8,128)(2,1)S(1)}, u32[]{:S(2)}, u32[]{:S(2)}) collective-permute-start(bf16[8,16,128]{2,1,0:T(8,128)(2,1)S(1)} %copy-done.54), channel_id=1, source_target_pairs={{0,1},{1,0},{2,3},{3,2},{4,5},{5,4},{6,7},{7,6},{8,9},{9,8},{10,11... | collective-permute-start | bytes 98312 | tf_op jit(solution)/shard_map/ppermute | solution.py:720
  212.1 13.2 %collective-permute-start.44 = (bf16[256,1024]{1,0:T(8,128)(2,1)S(1)}, bf16[256,1024]{1,0:T(8,128)(2,1)S(1)}, u32[]{:S(2)}, u32[]{:S(2)}) collective-permute-start(bf16[256,1024]{1,0:T(8,128)(2,1)S(1)} %add_convert_fusion), channel_id=1, source_target_pairs={{0,2},{1,3},{2,0},{3,1},{4,6},{5,7},{6,4},{7,5},{8,10},{9,11},{10,... | collective-permute-start | bytes 1572872 | tf_op jit(solution)/shard_map/ppermute | solution.py:720
  213.8 13.5 %collective-permute-start.47 = (bf16[256,1024]{1,0:T(8,128)(2,1)S(1)}, bf16[256,1024]{1,0:T(8,128)(2,1)S(1)}, u32[]{:S(2)}, u32[]{:S(2)}) collective-permute-start(bf16[256,1024]{1,0:T(8,128)(2,1)S(1)} %copy-done.52), channel_id=1, source_target_pairs={{0,1},{1,0},{2,3},{3,2},{4,5},{5,4},{6,7},{7,6},{8,9},{9,8},{10,11... | collective-permute-start | bytes 1572872 | tf_op jit(solution)/shard_map/ppermute | solution.py:720
  237.1 9.8 %collective-permute-start.50 = (bf16[13,16,128]{2,1,0:T(8,128)(2,1)S(1)}, bf16[13,16,128]{2,1,0:T(8,128)(2,1)S(1)}, u32[]{:S(2)}, u32[]{:S(2)}) collective-permute-start(bf16[13,16,128]{2,1,0:T(8,128)(2,1)S(1)} %slice.26), channel_id=1, source_target_pairs={{0,8},{8,16},{16,24},{24,28},{28,20},{20,12},{12,4},{4,0},{1,9},{9... | collective-permute-start | bytes 159752 | tf_op jit(solution)/shard_map/ppermute | solution.py:767
  237.5 9.5 %collective-permute-start.51 = (bf16[13,16,128]{2,1,0:T(8,128)(2,1)S(1)}, bf16[13,16,128]{2,1,0:T(8,128)(2,1)S(1)}, u32[]{:S(2)}, u32[]{:S(2)}) collective-permute-start(bf16[13,16,128]{2,1,0:T(8,128)(2,1)S(1)} %slice.27), channel_id=1, source_target_pairs={{8,0},{16,8},{24,16},{28,24},{20,28},{12,20},{4,12},{0,4},{9,1},{1... | collective-permute-start | bytes 159752 | tf_op jit(solution)/shard_map/ppermute | solution.py:768
  (80 other events, 653.9 us)
Sparse Core Ops, SparseCore 0:
  19.0 33.0 all-gather.6
  53.6 23.3 all-gather.8
  175.3 45.7 all-gather.10
